TPU v7x, 32 devices: a whole 2x2x4 slice. The times are simulated.
32 devices in a mesh: shard: 4 (over x, core), ctx: 4 (over z), tp: 2 (over y).
Axes of the slice: x: 2, y: 2, z: 4, core: 2. Of those that a mesh axis runs over, the one named last changes fastest.
Arguments:
- tokens: bfloat16 [10240, 1024], P(('shard', 'ctx')), may hold values from -6 to 6
- cotangent: bfloat16 [10240, 1024], P(('shard', 'ctx')), may hold values from -6 to 6
- seg_ids: int32 [10240], P(('shard', 'ctx')), may hold values from 0 to 51, as said below
- positions: int32 [10240], P(('shard', 'ctx')), may hold values from 0 to 1279, as said below
- parents: int32 [52], replicated, may hold values from 0 to 51, as said below
- w_qkv: bfloat16 [3, 1024, 1024], P(None, ('shard', 'ctx'), 'tp'), may hold values from -0.1875 to 0.1875
- b_qv: float32 [2, 1024], P(None, 'tp'), may hold values from -4 to 4
- w_out: bfloat16 [1024, 1024], P('tp', ('shard', 'ctx')), may hold values from -0.5 to 0.5
- b_out: float32 [1024], replicated, may hold values from -4 to 4
- w_up: bfloat16 [1024, 4096], P(('shard', 'ctx'), 'tp'), may hold values from -0.1875 to 0.1875
- b_up: float32 [4096], P('tp'), may hold values from -4 to 4
- w_down: bfloat16 [4096, 1024], P('tp', ('shard', 'ctx')), may hold values from -0.09375 to 0.09375
- b_down: float32 [1024], replicated, may hold values from -4 to 4
- ln_gain: float32 [2, 1024], replicated, may hold values from 0.5 to 1.5
- ln_bias: float32 [2, 1024], replicated, may hold values from -3 to 3
Outputs:
- result: bfloat16 [10240, 1024], P(('shard', 'ctx'))
- grad_tokens: float32 [10240, 1024], P(('shard', 'ctx'))
- grad_w_qkv: float32 [3, 1024, 1024], P(None, ('shard', 'ctx'), 'tp')
- grad_b_qv: float32 [2, 1024], P(None, 'tp')
- grad_w_out: float32 [1024, 1024], P('tp', ('shard', 'ctx'))
- grad_b_out: float32 [1024], replicated
- grad_w_up: float32 [1024, 4096], P(('shard', 'ctx'), 'tp')
- grad_b_up: float32 [4096], P('tp')
- grad_w_down: float32 [4096, 1024], P('tp', ('shard', 'ctx'))
- grad_b_down: float32 [1024], replicated
- grad_ln_gain: float32 [2, 1024], replicated
- grad_ln_bias: float32 [2, 1024], replicated
Inputs may be any that keep to these rules, and one draw needn't show every extreme that they name: `seg_ids`: each aligned run of 2560 tokens is one tree of 13 segments: a trunk of 1024 tokens first, then 4 branches and 8 leaves of 128 tokens each, each segment's tokens adjacent and after its parent's; every segment number labels exactly one segment. Positions count from 0 at the trunk's start along the path; a segment's tokens have consecutive positions following its parent's last. `parents`: A trunk is its own parent; a branch's parent is its trunk, a leaf's parent a branch of its tree, each branch parent of two leaves.
All inputs are finite; a program needn't handle non-finite values.
Results may differ from a plain program's by a relative error of at most 0.015.
Values may be sent and summed in bfloat16 or wider, within the bound.
A program may use at most 192 MiB of HBM per device.

v0:
```python
from functools import partial

import jax
import jax.numpy as jnp
from jax import lax
from jax.sharding import PartitionSpec as P

HEADS = 16
HD = 64
KEY_BLOCK = 512


EPS = 1e-05
NEG = -1e30


def norm_forward(inputs_in, gain_row, shift_row):
    centre = inputs_in - jnp.mean(inputs_in, axis=-1, keepdims=True)
    inverse = lax.rsqrt(jnp.mean(centre * centre, axis=-1, keepdims=True) + EPS)
    normed = centre * inverse
    return (normed * gain_row + shift_row, normed, inverse)


def norm_backward(grad_in, normed, inverse, gain_row):
    scaled = grad_in * gain_row
    mean_grad = jnp.mean(scaled, axis=-1, keepdims=True)
    mean_cross = jnp.mean(scaled * normed, axis=-1, keepdims=True)
    return inverse * (scaled - mean_grad - normed * mean_cross)


def ancestry(seg_vals, parents):
    first_up = jnp.take(parents, seg_vals)
    return (first_up, jnp.take(parents, first_up))


def block_scores(query_heads, key_heads, query_tags, key_tags, slopes):
    q_seg, q_first, q_second, q_pos = query_tags
    k_seg, k_pos = key_tags
    raw_scores = jnp.einsum(
        "qhd,khd->hqk", query_heads, key_heads, preferred_element_type=jnp.float32
    ) * HD ** (-0.5)
    distance = (q_pos[:, None] - k_pos[None, :]).astype(jnp.float32)
    scores = raw_scores - slopes[:, None, None] * distance[None]
    related = (
        (k_seg[None, :] == q_seg[:, None])
        | (k_seg[None, :] == q_first[:, None])
        | (k_seg[None, :] == q_second[:, None])
    )
    allowed = related & (k_pos[None, :] <= q_pos[:, None])
    return (scores, allowed[None])


def probabilities(scores, allowed, row_max, row_sum):
    shifted = jnp.where(allowed, scores - row_max[:, :, None], NEG)
    return jnp.exp(shifted) / row_sum[:, :, None]


def per_device(
    tokens,
    cotangent,
    seg_ids,
    positions,
    parents,
    w_qkv,
    b_qv,
    w_out,
    b_out,
    w_up,
    b_up,
    w_down,
    b_down,
    ln_gain,
    ln_bias,
):
    num_rows = tokens.shape[0]
    head_count = HEADS // lax.axis_size("tp")
    head_width = head_count * HD
    head_index = (lax.axis_index("tp") * head_count + jnp.arange(head_count)).astype(jnp.float32)
    slopes = 2.0 ** (-8.0 * (head_index + 1.0) / HEADS)
    scale = HD ** (-0.5)
    full_qkv, full_out = (
        lax.all_gather(w_qkv, ("shard", "ctx"), axis=1, tiled=True),
        lax.all_gather(w_out, ("shard", "ctx"), axis=1, tiled=True),
    )
    group_seg, group_pos = (
        lax.all_gather(seg_ids, "ctx", axis=0, tiled=True),
        lax.all_gather(positions, "ctx", axis=0, tiled=True),
    )
    own_first, own_second = ancestry(seg_ids, parents)
    own_tags = (seg_ids, own_first, own_second, positions)
    inputs = tokens.astype(jnp.float32)
    norm_one, normed_one, inverse_one = norm_forward(inputs, ln_gain[0], ln_bias[0])
    act_one = norm_one.astype(jnp.bfloat16)
    projected = jnp.einsum("td,cde->cte", act_one, full_qkv, preferred_element_type=jnp.float32)
    qkv_bias = jnp.stack([b_qv[0], jnp.zeros((head_width,), jnp.float32), b_qv[1]])
    qkv_low = (projected + qkv_bias[:, None, :]).astype(jnp.bfloat16)
    query_flat, key_flat, value_flat = (qkv_low[0], qkv_low[1], qkv_low[2])
    group_keys, group_values = (
        lax.all_gather(key_flat, "ctx", axis=0, tiled=True),
        lax.all_gather(value_flat, "ctx", axis=0, tiled=True),
    )
    group_rows = group_keys.shape[0]
    block_count = group_rows // KEY_BLOCK
    key_blocks = group_keys.reshape(block_count, KEY_BLOCK, head_count, HD)
    value_blocks = group_values.reshape(block_count, KEY_BLOCK, head_count, HD)
    seg_blocks = group_seg.reshape(block_count, KEY_BLOCK)
    pos_blocks = group_pos.reshape(block_count, KEY_BLOCK)
    query_heads = query_flat.reshape(num_rows, head_count, HD)

    def stats_step(carry_in, block_parts):
        row_max, row_sum = carry_in
        key_part, seg_part, pos_part = block_parts
        scores, allowed = block_scores(
            query_heads, key_part, own_tags, (seg_part, pos_part), slopes
        )
        new_max = jnp.maximum(row_max, jnp.max(jnp.where(allowed, scores, NEG), axis=-1))
        shifted = jnp.where(allowed, scores - new_max[:, :, None], NEG)
        row_sum = row_sum * jnp.exp(row_max - new_max) + jnp.sum(jnp.exp(shifted), axis=-1)
        return ((new_max, row_sum), None)

    start_stats = (
        jnp.full((head_count, num_rows), NEG, jnp.float32),
        jnp.zeros((head_count, num_rows), jnp.float32),
    )
    (row_max, row_sum), _ = lax.scan(stats_step, start_stats, (key_blocks, seg_blocks, pos_blocks))

    def output_step(out_accum, block_parts):
        key_part, value_part, seg_part, pos_part = block_parts
        scores, allowed = block_scores(
            query_heads, key_part, own_tags, (seg_part, pos_part), slopes
        )
        prob_low = probabilities(scores, allowed, row_max, row_sum).astype(jnp.bfloat16)
        return (
            out_accum
            + jnp.einsum("hqk,khd->qhd", prob_low, value_part, preferred_element_type=jnp.float32),
            None,
        )

    attended, _ = lax.scan(
        output_step,
        jnp.zeros((num_rows, head_count, HD), jnp.float32),
        (key_blocks, value_blocks, seg_blocks, pos_blocks),
    )
    attended_low = attended.reshape(num_rows, head_width).astype(jnp.bfloat16)
    branch_one = (
        lax.psum(
            jnp.dot(attended_low, full_out, preferred_element_type=jnp.float32).astype(
                jnp.bfloat16
            ),
            "tp",
        ).astype(jnp.float32)
        + b_out
    )
    middle = inputs + branch_one
    full_up, full_down = (
        lax.all_gather(w_up, ("shard", "ctx"), axis=0, tiled=True),
        lax.all_gather(w_down, ("shard", "ctx"), axis=1, tiled=True),
    )
    norm_two, normed_two, inverse_two = norm_forward(middle, ln_gain[1], ln_bias[1])
    act_two = norm_two.astype(jnp.bfloat16)
    upper_in = jnp.dot(act_two, full_up, preferred_element_type=jnp.float32) + b_up
    gelu_vals, gelu_pull = jax.vjp(partial(jax.nn.gelu, approximate=True), upper_in)
    hidden = gelu_vals.astype(jnp.bfloat16)
    branch_two = (
        lax.psum(
            jnp.dot(hidden, full_down, preferred_element_type=jnp.float32).astype(jnp.bfloat16),
            "tp",
        ).astype(jnp.float32)
        + b_down
    )
    result = (middle + branch_two).astype(jnp.bfloat16)
    grad_out = cotangent.astype(jnp.float32)
    grad_hidden = jnp.einsum("td,fd->tf", cotangent, full_down, preferred_element_type=jnp.float32)
    grad_upper = gelu_pull(grad_hidden)[0].astype(jnp.bfloat16)
    down_term = jnp.einsum("tf,td->fd", hidden, cotangent, preferred_element_type=jnp.float32)
    up_term = jnp.einsum("td,tf->df", act_two, grad_upper, preferred_element_type=jnp.float32)
    grad_w_up, grad_w_down = (
        lax.psum_scatter(up_term, ("shard", "ctx"), scatter_dimension=0, tiled=True),
        lax.psum_scatter(down_term, ("shard", "ctx"), scatter_dimension=1, tiled=True),
    )
    grad_norm_two = lax.psum(
        jnp.einsum("tf,df->td", grad_upper, full_up, preferred_element_type=jnp.float32).astype(
            jnp.bfloat16
        ),
        "tp",
    ).astype(jnp.float32)
    grad_middle = grad_out + norm_backward(grad_norm_two, normed_two, inverse_two, ln_gain[1])
    grad_branch = grad_middle.astype(jnp.bfloat16)
    out_term = jnp.einsum(
        "te,td->ed", attended_low, grad_branch, preferred_element_type=jnp.float32
    )
    grad_att = jnp.einsum(
        "td,ed->te", grad_branch, full_out, preferred_element_type=jnp.float32
    ).astype(jnp.bfloat16)
    grad_heads = grad_att.reshape(num_rows, head_count, HD)
    row_terms = jnp.einsum("qhd,qhd->hq", grad_heads.astype(jnp.float32), attended)

    def joint_step(grad_accum, block_parts):
        key_part, value_part, seg_part, pos_part = block_parts
        scores, allowed = block_scores(
            query_heads, key_part, own_tags, (seg_part, pos_part), slopes
        )
        prob_vals = probabilities(scores, allowed, row_max, row_sum)
        grad_probs = jnp.einsum(
            "qhd,khd->hqk", grad_heads, value_part, preferred_element_type=jnp.float32
        )
        grad_scores = (prob_vals * (grad_probs - row_terms[:, :, None])).astype(jnp.bfloat16)
        grad_accum = (
            grad_accum
            + jnp.einsum("hqk,khd->qhd", grad_scores, key_part, preferred_element_type=jnp.float32)
            * scale
        )
        key_part_grad = (
            jnp.einsum("hqk,qhd->khd", grad_scores, query_heads, preferred_element_type=jnp.float32)
            * scale
        )
        value_part_grad = jnp.einsum(
            "hqk,qhd->khd",
            prob_vals.astype(jnp.bfloat16),
            grad_heads,
            preferred_element_type=jnp.float32,
        )
        return (
            grad_accum,
            (
                key_part_grad.reshape(KEY_BLOCK, head_width),
                value_part_grad.reshape(KEY_BLOCK, head_width),
            ),
        )

    grad_query_sum, (key_terms, value_terms) = lax.scan(
        joint_step,
        jnp.zeros((num_rows, head_count, HD), jnp.float32),
        (key_blocks, value_blocks, seg_blocks, pos_blocks),
    )
    key_grad_sum, value_grad_sum = (
        lax.psum_scatter(
            key_terms.reshape(group_rows, head_width).astype(jnp.bfloat16),
            "ctx",
            scatter_dimension=0,
            tiled=True,
        ).astype(jnp.float32),
        lax.psum_scatter(
            value_terms.reshape(group_rows, head_width).astype(jnp.bfloat16),
            "ctx",
            scatter_dimension=0,
            tiled=True,
        ).astype(jnp.float32),
    )
    grad_query_low = grad_query_sum.reshape(num_rows, head_width).astype(jnp.bfloat16)
    grad_key_low = key_grad_sum.astype(jnp.bfloat16)
    grad_value_low = value_grad_sum.astype(jnp.bfloat16)
    grad_qkv = jnp.stack([grad_query_low, grad_key_low, grad_value_low])
    grad_norm_one = lax.psum(
        jnp.einsum("cte,cde->td", grad_qkv, full_qkv, preferred_element_type=jnp.float32).astype(
            jnp.bfloat16
        ),
        "tp",
    ).astype(jnp.float32)
    grad_tokens = grad_middle + norm_backward(grad_norm_one, normed_one, inverse_one, ln_gain[0])
    qkv_term = jnp.einsum("td,cte->cde", act_one, grad_qkv, preferred_element_type=jnp.float32)
    grad_w_qkv, grad_w_out = (
        lax.psum_scatter(qkv_term, ("shard", "ctx"), scatter_dimension=1, tiled=True),
        lax.psum_scatter(out_term, ("shard", "ctx"), scatter_dimension=1, tiled=True),
    )
    bias_qv_part = jnp.stack(
        [
            jnp.sum(grad_query_low.astype(jnp.float32), axis=0),
            jnp.sum(grad_value_low.astype(jnp.float32), axis=0),
        ]
    )
    out_bias_part = jnp.sum(grad_branch.astype(jnp.float32), axis=0)
    up_bias_part = jnp.sum(grad_upper.astype(jnp.float32), axis=0)
    down_bias_part = jnp.sum(grad_out, axis=0)
    gain_part = jnp.stack(
        [jnp.sum(grad_norm_one * normed_one, axis=0), jnp.sum(grad_norm_two * normed_two, axis=0)]
    )
    shift_part = jnp.stack([jnp.sum(grad_norm_one, axis=0), jnp.sum(grad_norm_two, axis=0)])
    grad_b_qv, grad_b_out, grad_b_up, grad_b_down, grad_gain, grad_shift = lax.psum(
        (bias_qv_part, out_bias_part, up_bias_part, down_bias_part, gain_part, shift_part),
        ("shard", "ctx"),
    )
    return (
        result,
        grad_tokens,
        grad_w_qkv,
        grad_b_qv,
        grad_w_out,
        grad_b_out,
        grad_w_up,
        grad_b_up,
        grad_w_down,
        grad_b_down,
        grad_gain,
        grad_shift,
    )


def solution(mesh):
    placed = (
        P(("shard", "ctx"), None),
        P(("shard", "ctx"), None),
        P(("shard", "ctx")),
        P(("shard", "ctx")),
        P(),
        P(None, ("shard", "ctx"), "tp"),
        P(None, "tp"),
        P("tp", ("shard", "ctx")),
        P(),
        P(("shard", "ctx"), "tp"),
        P("tp"),
        P("tp", ("shard", "ctx")),
        P(),
        P(),
        P(),
    )
    return jax.shard_map(
        per_device,
        mesh=mesh,
        in_specs=placed,
        out_specs=(
            P(("shard", "ctx"), None),
            P(("shard", "ctx"), None),
            P(None, ("shard", "ctx"), "tp"),
            P(None, "tp"),
            P("tp", ("shard", "ctx")),
            P(),
            P(("shard", "ctx"), "tp"),
            P("tp"),
            P("tp", ("shard", "ctx")),
            P(),
            P(),
            P(),
        ),
        check_vma=False,
    )
```

profile of v0, /device:TPU:12, one launch (start us, length us, event | category | flops | bytes accessed | tf_op | source)
XLA Modules:
  0.0 1226.0 jit_solution(17177384141970764091)
XLA Ops:
  11.7 45.6 %all-gather.11.cloned.1.call-done = bf16[3,1024,512]{2,1,0:T(8,128)(2,1)} async-done(((bf16[3,64,512]{2,1,0:T(8,128)(2,1)}), bf16[3,1024,512]{2,1,0:T(8,128)(2,1)}) %all-gather.11.cloned.1.call-update) | async-done | bytes 3145744 | tf_op jit(solution)/shard_map/all_gather | solution.py:82
  57.3 4.7 fusion.83
  67.1 11.6 all-gather.2
  78.8 13.3 %all-gather.3 = s32[4,1,640]{2,1,0:T(1,128)S(1)} all-gather(s32[1,1,640]{2,1,0:T(1,128)S(1)} %reshape.678), channel_id=1, replica_groups=mesh['shard'=4,'ctx'=4,'tp'=2] {'ctx'}, dimensions={0}, use_global_device_ids=true | all-gather | bytes 12800 | tf_op jit(solution)/shard_map/all_gather | solution.py:87
  92.1 32.4 %select_select_fusion = (s32[640]{0:T(1024)S(1)}, s32[640]{0:T(1024)S(1)}) fusion(s32[]{:T(128)} %bitcast.57, s32[]{:T(128)} %bitcast.56, s32[]{:T(128)} %bitcast.55, s32[]{:T(128)} %bitcast.54, s32[]{:T(128)} %bitcast.53, s32[]{:T(128)} %bitcast.52, s32[]{:T(128)} %bitcast.51, s32[]{:T(128)} %bitcast.50, s32[]{:T(128)} %bitcast.49, s32[]{:T(128)} %bitcast.48, ...), kind=kLoop, calls=%fused_computation.139 | loop fusion | flops 139520 | bytes 7888 | tf_op jit(solution)/shard_map/jit(_take)/select_n | solution.py:33
  124.5 7.1 reshape.547
  131.6 4.7 copy.60
  136.4 34.1 %all-gather.21.cloned.1.call-done = bf16[1,2560,512]{1,2,0:T(8,128)(2,1)} async-done(((bf16[1,640,512]{1,2,0:T(8,128)(2,1)}), bf16[1,2560,512]{1,2,0:T(8,128)(2,1)}) %all-gather.21.cloned.1.call-update) | async-done | bytes 2621456 | tf_op jit(solution)/shard_map/all_gather | solution.py:99
  170.5 7.0 reshape.550
  177.5 4.7 copy.61
  182.1 41.6 %while.39 = (s32[]{:T(128)}, f32[8,640]{1,0:T(8,128)S(1)}, f32[8,640]{1,0:T(8,128)S(1)}, s32[5,512]{1,0:T(8,128)S(1)}, s32[640]{0:T(1024)S(1)}, /*index=5*/s32[6...) while((s32[]{:T(128)}, f32[8,640]{1,0:T(8,128)S(1)}, ...), condition=%wide.region_5.7_spmd.clone, body=%wide.region_2.6_spmd.clone.sunk | while | flops 367354912 | bytes 27360004 | solution.py:125
  182.7 4.8 select_reduce_fusion.2
  191.1 4.7 select_reduce_fusion.2
  199.4 4.7 select_reduce_fusion.2
  207.7 4.8 select_reduce_fusion.2
  216.1 4.7 select_reduce_fusion.2
  223.8 40.9 %while.40 = (s32[]{:T(128)}, f32[640,8,64]{0,2,1:T(8,128)}, bf16[5,512,8,64]{1,3,2,0:T(8,128)(2,1)}, s32[5,512]{1,0:T(8,128)S(1)}, s32[640]{0:T(1024)S(1)}, /*in...) while((s32[]{:T(128)}, f32[640,8,64]{0,2,1:T(8,128)}, ...), condition=%wide.region_7.9_spmd.clone, body=%wide.region_6.8_spmd.clone.sunk | while | flops 693043264 | bytes 7672046 | solution.py:139
  224.6 7.2 fusion.154
  232.4 7.6 fusion.154
  240.6 7.6 fusion.154
  248.9 7.6 fusion.154
  257.1 7.6 fusion.154
  271.0 43.8 %all-reduce.8.cloned.1.call-done = bf16[640,1024]{1,0:T(8,128)(2,1)} async-done(((bf16[640,1024]{1,0:T(8,128)(2,1)}), bf16[640,1024]{1,0:T(8,128)(2,1)}) %all-reduce.8.cloned.1.call-update) | async-done | bytes 1310736 | tf_op jit(solution)/shard_map/psum | solution.py:146
  317.4 51.3 %all-gather.15.cloned.1.call-done = bf16[1024,2048]{1,0:T(8,128)(2,1)} async-done(((bf16[64,2048]{1,0:T(8,128)(2,1)}), bf16[1024,2048]{1,0:T(8,128)(2,1)}) %all-gather.15.cloned.1.call-update) | async-done | bytes 4194320 | tf_op jit(solution)/shard_map/all_gather | solution.py:156
  368.8 7.7 fusion.95
  376.5 43.8 %all-gather.17.cloned.1.call-done = bf16[2048,1024]{0,1:T(8,128)(2,1)} async-done(((bf16[2048,64]{0,1:T(8,128)(2,1)}), bf16[2048,1024]{0,1:T(8,128)(2,1)}) %all-gather.17.cloned.1.call-update) | async-done | bytes 4194320 | tf_op jit(solution)/shard_map/all_gather | solution.py:157
  420.3 9.6 convert_reduce_fusion
  435.5 43.4 %all-reduce.10.cloned.1.call-done = bf16[640,1024]{1,0:T(8,128)(2,1)} async-done(((bf16[640,1024]{1,0:T(8,128)(2,1)}), bf16[640,1024]{1,0:T(8,128)(2,1)}) %all-reduce.10.cloned.1.call-update) | async-done | bytes 1310736 | tf_op jit(solution)/shard_map/psum | solution.py:181
  487.0 80.2 %while.41 = (s32[]{:T(128)}, f32[640,8,64]{0,2,1:T(8,128)S(1)}, bf16[5,512,512]{1,2,0:T(8,128)(2,1)}, bf16[5,512,512]{1,2,0:T(8,128)(2,1)}, bf16[5,512,8,64]{1,3...) while((s32[]{:T(128)}, f32[640,8,64]{0,2,1:T(8,128)S(1)}, ...), condition=%wide.region_16.18_spmd.clone, body=%wide.region_15.17_spmd.clone.sunk | while | flops 1708392448 | bytes 60513056 | solution.py:231
  487.6 5.1 fusion.165
  503.6 5.1 fusion.165
  519.7 5.1 fusion.165
  535.7 5.1 fusion.165
  551.8 5.1 fusion.165
  576.8 8.8 convolution_convert_fusion.1
  586.0 37.9 %reduce-scatter.8.cloned.1.call-done = bf16[640,512]{1,0:T(8,128)(2,1)} async-done(((bf16[2560,512]{1,0:T(8,128)(2,1)}), bf16[640,512]{1,0:T(8,128)(2,1)}) %reduce-scatter.8.cloned.1.call-update) | async-done | bytes 655376 | tf_op jit(solution)/shard_map/reduce_scatter | solution.py:243
  623.9 54.0 %reduce-scatter.6.cloned.1.call-done = bf16[640,512]{1,0:T(8,128)(2,1)} async-done(((bf16[2560,512]{1,0:T(8,128)(2,1)}), bf16[640,512]{1,0:T(8,128)(2,1)}) %reduce-scatter.6.cloned.1.call-update) | async-done | bytes 655376 | tf_op jit(solution)/shard_map/reduce_scatter | solution.py:237
  677.9 5.6 bitcast_convert_fusion
  685.1 5.8 convolution_bitcast_fusion
  690.9 9.5 copy.68
  705.6 9.7 fusion.96
  716.7 7.8 fusion.94
  726.6 31.3 %all-reduce.14.cloned.1.call-done = (bf16[640,1024]{1,0:T(8,128)(2,1)}, bf16[640,1024]{1,0:T(8,128)(2,1)}) async-done(((bf16[640,1024]{1,0:T(8,128)(2,1)}, bf16[640,1024]{1,0:T(8,128)(2,1)}), (bf16[640,1024]{1,0:T(8,128)(2,1)}, bf16[640,1024]{1,0:T(8,128)(2,1)})) %all-reduce.14.cloned.1.call-update) | async-done | bytes 2621456 | tf_op jit(solution)/shard_map/psum | solution.py:165
  760.5 62.5 %all-reduce.1 = (f32[2,512]{1,0:T(2,128)}, f32[1024]{0:T(1024)}, f32[2048]{0:T(1024)}, f32[1024]{0:T(1024)}, f32[2,1024]{1,0:T(2,128)}, /*index=5*/f32[2,1024]{1,0:T(2,128)}) all-reduce(f32[2,512]{1,0:T(2,128)S(1)} %pad_maximum_fusion.6, f32[1024]{0:T(1024)S(1)} %copy-done.32, ...), channel_id=1, replica_groups=mesh['shard'=4,'ctx'=4,'tp'=2] {'shard','ctx'}, use_global_device_ids=true, to_apply=%region_25.27 | all-reduce | flops 9216 | bytes 73728 | tf_op jit(solution)/shard_map/psum | solution.py:279
  827.6 107.4 %all-reduce.12.cloned.1.call-done = f32[3,1024,512]{2,0,1:T(4,128)} async-done(((f32[3,1024,512]{2,0,1:T(4,128)}), f32[3,1024,512]{2,0,1:T(4,128)}) %all-reduce.12.cloned.1.call-update) | async-done | bytes 6291472
  936.9 63.8 %reduce-scatter.10.cloned.1.call-done = f32[512,64]{0,1:T(8,128)} async-done(((f32[512,1024]{0,1:T(8,128)}), f32[512,64]{0,1:T(8,128)}) %reduce-scatter.10.cloned.1.call-update) | async-done | bytes 131088 | tf_op jit(solution)/shard_map/reduce_scatter | solution.py:264
  1000.8 109.0 %reduce-scatter.14.cloned.1.call-done = f32[2048,64]{0,1:T(8,128)} async-done(((f32[2048,1024]{0,1:T(8,128)}), f32[2048,64]{0,1:T(8,128)}) %reduce-scatter.14.cloned.1.call-update) | async-done | bytes 524304 | tf_op jit(solution)/shard_map/reduce_scatter | solution.py:179
  1109.8 109.4 %reduce-scatter.12.cloned.1.call-done = f32[64,2048]{1,0:T(8,128)} async-done(((f32[1024,2048]{1,0:T(8,128)}), f32[64,2048]{1,0:T(8,128)}) %reduce-scatter.12.cloned.1.call-update) | async-done | bytes 524304 | tf_op jit(solution)/shard_map/reduce_scatter | solution.py:178
  (297 shorter events, 135.1 us)
Async XLA Ops:
  7.2 50.1 %copy-start = (bf16[640,1024]{1,0:T(8,128)(2,1)S(1)}, bf16[640,1024]{1,0:T(8,128)(2,1)}, u32[]{:S(2)}) copy-start(bf16[640,1024]{1,0:T(8,128)(2,1)} %param.23) | copy-start | bytes 3932164
  7.2 4.3 copy-start.40
  7.2 4.4 copy-start.36
  7.2 4.4 copy-start.37
  7.2 50.1 %all-gather.11.cloned.1.call-start = ((), (), s32[]{:S(2)}) async-start(), calls=%async_computation.5 | async-start | bytes 3342336 | tf_op jit(solution)/shard_map/all_gather | solution.py:82
  8.0 116.6 %all-gather.19.cloned.1.call-start = ((), (), s32[]{:S(2)}) async-start(), calls=%async_computation.16 | async-start | bytes 3276800 | tf_op jit(solution)/shard_map/all_gather | solution.py:100
  9.6 47.7 %copy-start.20 = (f32[640]{0:T(1024)}, f32[640]{0:T(1024)S(1)}, u32[]{:S(2)}) copy-start(f32[640]{0:T(1024)S(1)} %broadcast_multiply_fusion.5) | copy-start | bytes 7684
  11.5 50.6 %copy-start.24 = (f32[640]{0:T(1024)}, f32[640]{0:T(1024)S(1)}, u32[]{:S(2)}) copy-start(f32[640]{0:T(1024)S(1)} %add_rsqrt_fusion.1) | copy-start | bytes 7684
  11.6 50.5 %copy-start.26 = (f32[1,1024]{1,0:T(1,128)}, f32[1,1024]{1,0:T(1,128)S(1)}, u32[]{:S(2)}) copy-start(f32[1,1024]{1,0:T(1,128)S(1)} %get-tuple-element.692) | copy-start | bytes 12292
  11.6 471.2 %copy-start.30 = (f32[1,1024]{1,0:T(1,128)}, f32[1,1024]{1,0:T(1,128)S(1)}, u32[]{:S(2)}) copy-start(f32[1,1024]{1,0:T(1,128)S(1)} %get-tuple-element.693) | copy-start | bytes 12292
  11.6 50.4 %copy-start.43 = (f32[1,1024]{1,0:T(1,128)}, f32[1,1024]{1,0:T(1,128)S(1)}, u32[]{:S(2)}) copy-start(f32[1,1024]{1,0:T(1,128)S(1)} %get-tuple-element.694) | copy-start | bytes 12292
  11.6 357.1 %copy-start.41 = (f32[1,1024]{1,0:T(1,128)}, f32[1,1024]{1,0:T(1,128)S(1)}, u32[]{:S(2)}) copy-start(f32[1,1024]{1,0:T(1,128)S(1)} %get-tuple-element.695) | copy-start | bytes 12292
  62.1 2.8 copy-start.11
  62.1 4.9 copy-start.8
  62.1 4.9 copy-start.14
  63.4 107.0 %all-gather.21.cloned.1.call-start = ((), (), s32[]{:S(2)}) async-start(), calls=%async_computation.17 | async-start | bytes 3276800 | tf_op jit(solution)/shard_map/all_gather | solution.py:99
  64.2 201.9 %all-gather.13.cloned.1.call-start = ((), (), s32[]{:S(2)}) async-start(), calls=%async_computation.6 | async-start | bytes 1114112 | tf_op jit(solution)/shard_map/all_gather | solution.py:83
  64.8 250.0 %all-reduce.8.cloned.1.call-start = ((), (), s32[]{:S(2)}) async-start(), calls=%async_computation.7 | async-start | bytes 2621440 | tf_op jit(solution)/shard_map/psum | solution.py:146
  266.1 4.1 copy-start.9
  266.1 48.6 %copy-start.18 = (f32[1024]{0:T(1024)S(1)}, f32[1024]{0:T(1024)}, u32[]{:S(2)}) copy-start(f32[1024]{0:T(1024)} %param.31) | copy-start | bytes 12292
  269.6 99.2 %all-gather.15.cloned.1.call-start = ((), (), s32[]{:S(2)}) async-start(), calls=%async_computation.8 | async-start | bytes 4456448 | tf_op jit(solution)/shard_map/all_gather | solution.py:156
  270.2 150.1 %all-gather.17.cloned.1.call-start = ((), (), s32[]{:S(2)}) async-start(), calls=%async_computation.9 | async-start | bytes 4456448 | tf_op jit(solution)/shard_map/all_gather | solution.py:157
  270.9 208.0 %all-reduce.10.cloned.1.call-start = ((), (), s32[]{:S(2)}) async-start(), calls=%async_computation.10 | async-start | bytes 2621440 | tf_op jit(solution)/shard_map/psum | solution.py:181
  316.7 166.1 %copy-start.22 = (f32[640]{0:T(1024)}, f32[640]{0:T(1024)S(1)}, u32[]{:S(2)}) copy-start(f32[640]{0:T(1024)S(1)} %broadcast_multiply_fusion.4) | copy-start | bytes 7684
  317.4 165.5 %copy-start.28 = (f32[640]{0:T(1024)}, f32[640]{0:T(1024)S(1)}, u32[]{:S(2)}) copy-start(f32[640]{0:T(1024)S(1)} %add_rsqrt_fusion) | copy-start | bytes 7684
  368.8 51.5 %copy-start.47 = (f32[2048]{0:T(1024)S(1)}, f32[2048]{0:T(1024)}, u32[]{:S(2)}) copy-start(f32[2048]{0:T(1024)} %param.33) | copy-start | bytes 24580
  420.3 11.1 copy-start.45
  435.4 188.5 %reduce-scatter.8.cloned.1.call-start = ((), (), s32[]{:S(2)}) async-start(), calls=%async_computation.12 | async-start | bytes 3276800 | tf_op jit(solution)/shard_map/reduce_scatter | solution.py:243
  478.9 4.0 copy-start.4
  478.9 4.0 copy-start.7
  478.9 4.0 copy-start.12
  482.9 2.6 copy-start.6
  482.9 2.5 copy-start.15
  571.6 106.3 %reduce-scatter.6.cloned.1.call-start = ((), (), s32[]{:S(2)}) async-start(), calls=%async_computation.11 | async-start | bytes 3276800 | tf_op jit(solution)/shard_map/reduce_scatter | solution.py:237
  576.1 181.8 %all-reduce.14.cloned.1.call-start = ((), (), s32[]{:S(2)}) async-start(), calls=%async_computation.19 | async-start | bytes 5242880 | tf_op jit(solution)/shard_map/psum | solution.py:165
  677.9 5.8 copy-start.46
  683.6 251.3 %all-reduce.12.cloned.1.call-start = ((), (), s32[]{:S(2)}) async-start(), calls=%async_computation.18 | async-start | bytes 16777216
  700.4 5.2 copy-start.13
  700.4 300.3 %reduce-scatter.10.cloned.1.call-start = ((), (), s32[]{:S(2)}) async-start(), calls=%async_computation.13 | async-start | bytes 2228224 | tf_op jit(solution)/shard_map/reduce_scatter | solution.py:264
  705.6 404.2 %reduce-scatter.14.cloned.1.call-start = ((), (), s32[]{:S(2)}) async-start(), calls=%async_computation.15 | async-start | bytes 8912896 | tf_op jit(solution)/shard_map/reduce_scatter | solution.py:179
  715.4 503.8 %reduce-scatter.12.cloned.1.call-start = ((), (), s32[]{:S(2)}) async-start(), calls=%async_computation.14 | async-start | bytes 8912896 | tf_op jit(solution)/shard_map/reduce_scatter | solution.py:178
  724.5 2.0 copy-start.17
  724.5 35.9 %copy-start.35 = (f32[1024]{0:T(1024)S(1)}, f32[1024]{0:T(1024)}, u32[]{:S(2)}) copy-start(f32[1024]{0:T(1024)} %get-tuple-element.566) | copy-start | bytes 12292
  724.5 35.9 %copy-start.34 = (f32[1024]{0:T(1024)S(1)}, f32[1024]{0:T(1024)}, u32[]{:S(2)}) copy-start(f32[1024]{0:T(1024)} %get-tuple-element.573) | copy-start | bytes 12292
  724.5 36.0 %copy-start.32 = (f32[1024]{0:T(1024)S(1)}, f32[1024]{0:T(1024)}, u32[]{:S(2)}) copy-start(f32[1024]{0:T(1024)} %get-tuple-element.672) | copy-start | bytes 12292
  724.5 36.0 %copy-start.33 = (f32[1024]{0:T(1024)S(1)}, f32[1024]{0:T(1024)}, u32[]{:S(2)}) copy-start(f32[1024]{0:T(1024)} %get-tuple-element.689) | copy-start | bytes 12292
  724.6 36.0 %copy-start.38 = (f32[2048]{0:T(1024)S(1)}, f32[2048]{0:T(1024)}, u32[]{:S(2)}) copy-start(f32[2048]{0:T(1024)} %get-tuple-element.670) | copy-start | bytes 24580
  724.6 98.5 %copy-start.39 = (f32[1024]{0:T(1024)S(1)}, f32[1024]{0:T(1024)}, u32[]{:S(2)}) copy-start(f32[1024]{0:T(1024)} %param.35) | copy-start | bytes 12292
  (18 other events, 23.9 us)
Sparse Core Ops, SparseCore 0:
  10.3 46.9 all-gather.10
  63.6 51.9 all-gather.18
  117.1 53.2 all-gather.20
  172.5 37.2 all-gather.12
  269.7 45.0 all-reduce.7
  317.1 51.6 all-gather.14
  371.2 49.0 all-gather.16
  435.6 43.3 all-reduce.9
  571.7 52.1 reduce-scatter.7
  626.1 51.7 reduce-scatter.5
  683.7 74.1 all-reduce.13
  762.0 172.9 all-reduce.11
  939.2 61.4 reduce-scatter.9
  1005.8 103.9 reduce-scatter.13
  1114.8 104.3 reduce-scatter.11
where the time goes:
time: 1230 us
  waiting for transfers between devices  778 us (63%)
  matrix products  206 us (17%)
  blocking collectives  87.5 us (7%)
  other arithmetic  76.9 us (6%)
  local copies, waits for them, and re-layouts  60.2 us (5%)
  between operations  15.5 us (1%)
    unnamed x16, waiting for transfers between devices  111 us
    reduce_scatter x1, waiting for transfers between devices, per_device(): lax.psum_scatter(up_term, ('shard', 'ctx'), scatter_dimension=0, tiled=True)  109 us
    reduce_scatter x1, waiting for transfers between devices, per_device(): lax.psum_scatter(down_term, ('shard', 'ctx'), scatter_dimension=1, tiled=...  109 us
    reduce_scatter x1, waiting for transfers between devices, per_device(): lax.psum_scatter(out_term, ('shard', 'ctx'), scatter_dimension=1, tiled=T...  63.8 us
    psum x1, blocking collectives, per_device(): lax.psum((bias_qv_part, out_bias_part, up_bias_part, down_bias_part, gain...  62.5 us
    reduce_scatter x1, waiting for transfers between devices, per_device(): lax.psum_scatter(key_terms.reshape(group_rows, head_width).astype(jnp.bfl...  54 us
    all_gather x1, waiting for transfers between devices, per_device(): lax.all_gather(w_up, ('shard', 'ctx'), axis=0, tiled=True)  51.3 us
    dot_general x10, matrix products, block_scores(): jnp.einsum('qhd,khd->hqk', query_heads, key_heads, preferred_element_type...  49.1 us
  transfers between devices with their start and end apart: 15, of which 13 were waited for; matrix products, arithmetic and copies ran while one was open for 18% of the time, Pallas kernels for 0%

commit v1 on v0

--- a/solution.py
+++ b/solution.py
@@ -3,15 +3,1184 @@
 import jax
 import jax.numpy as jnp
 from jax import lax
+from jax.experimental import pallas as pl
+from jax.experimental.pallas import tpu as pltpu
 from jax.sharding import PartitionSpec as P
 
 HEADS = 16
 HD = 64
 KEY_BLOCK = 512
-
+TRUNK = 1024
+BRANCH = 128
+SLOTS = 12
+TREE = TRUNK + SLOTS * BRANCH
+PAIR = 2 * HD
 
 EPS = 1e-05
 NEG = -1e30
+LOG2E = 1.4426950408889634
+MESH = pl.DeviceIdType.MESH
+BF = jnp.bfloat16
+F32 = jnp.float32
+ROWS_WAVE = 4
+
+
+def nt(left, right):
+    return lax.dot_general(left, right, (((1,), (1,)), ((), ())), preferred_element_type=F32)
+
+
+def nn(left, right):
+    return lax.dot_general(left, right, (((1,), (0,)), ((), ())), preferred_element_type=F32)
+
+
+def rcopy(src, dst, send, recv, device):
+    return pltpu.make_async_remote_copy(
+        src_ref=src, dst_ref=dst, send_sem=send, recv_sem=recv, device_id=device, device_id_type=MESH
+    )
+
+
+def greet(devices):
+    barrier = pltpu.get_barrier_semaphore()
+    for device in devices:
+        pl.semaphore_signal(barrier, inc=1, device_id=device, device_id_type=MESH)
+    pl.semaphore_wait(barrier, len(devices))
+
+
+def norm_rows(values, gain_row, shift_row):
+    centre = values - jnp.mean(values, axis=-1, keepdims=True)
+    inverse = lax.rsqrt(jnp.mean(centre * centre, axis=-1, keepdims=True) + EPS)
+    normed = centre * inverse
+    return normed * gain_row + shift_row, normed, inverse
+
+
+def norm_rows_back(grad_in, normed, inverse, gain_row):
+    scaled = grad_in * gain_row
+    mean_grad = jnp.mean(scaled, axis=-1, keepdims=True)
+    mean_cross = jnp.mean(scaled * normed, axis=-1, keepdims=True)
+    return inverse * (scaled - mean_grad - normed * mean_cross)
+
+
+def head_masks():
+    lane = lax.broadcasted_iota(jnp.int32, (1, PAIR), 1)
+    first = (lane < HD).astype(F32).astype(BF)
+    second = (lane >= HD).astype(F32).astype(BF)
+    return first, second
+
+
+def stack_heads(rows):
+    first, second = head_masks()
+    return jnp.concatenate([rows * first, rows * second], axis=0)
+
+
+def unstack_turned(turned, rows):
+    return jnp.concatenate([turned[:HD, :rows], turned[HD:, rows:]], axis=0).T
+
+
+def key_features(high, low, flag, rows):
+    lane = lax.broadcasted_iota(jnp.int32, (rows, 128), 1)
+    feats = jnp.where(lane < 3, high, jnp.where(lane < 6, low, jnp.where(lane == 6, flag, 0.0)))
+    return feats.astype(BF)
+
+
+def query_features(slope_ref, rows):
+    return jnp.concatenate(
+        [
+            jnp.broadcast_to(slope_ref[0:1, :], (rows, 128)),
+            jnp.broadcast_to(slope_ref[1:2, :], (rows, 128)),
+        ],
+        axis=0,
+    ).astype(BF)
+
+
+def fill_trunk_keys(key_ref, keys_aug):
+    keys_aug[:, 0:PAIR] = key_ref[0:TRUNK, :]
+    pos = lax.broadcasted_iota(jnp.int32, (TRUNK, 128), 0)
+    low = pos & 255
+    keys_aug[:, PAIR:] = key_features((pos - low).astype(F32), low.astype(F32), 0.0, TRUNK)
+
+
+def fill_labels(info_all, blocks, labels, parents):
+    labels[...] = jnp.full(labels.shape, -1.0, F32)
+    parents[...] = jnp.full(parents.shape, -2.0, F32)
+    for slot in range(SLOTS):
+        block = TRUNK // BRANCH + slot
+        owner, inner = block // blocks, block % blocks
+        labels[slot : slot + 1, :] = info_all[owner, inner : inner + 1, :]
+        parents[slot : slot + 1, :] = info_all[owner, 8 + inner : 9 + inner, :]
+
+
+def parent_pick(slot, labels, parents, key_ref, value_ref):
+    mine = parents[pl.ds(slot, 1), :]
+    leaf = jnp.zeros((1, 128), F32)
+    key_sum = jnp.zeros((BRANCH, PAIR), BF)
+    value_sum = jnp.zeros((BRANCH, PAIR), BF)
+    for other in range(SLOTS):
+        same = (mine == labels[other : other + 1, :]).astype(F32)
+        leaf = leaf + same
+        same_low = same.astype(BF)
+        at = TRUNK + other * BRANCH
+        key_sum = key_sum + same_low * key_ref[at : at + BRANCH, :]
+        value_sum = value_sum + same_low * value_ref[at : at + BRANCH, :]
+    return leaf, key_sum, value_sum
+
+
+def segment_key_features(leaf):
+    row = lax.broadcasted_iota(jnp.int32, (BRANCH, 128), 0).astype(F32)
+    own = key_features(float(TRUNK), row + leaf * float(BRANCH), 0.0, BRANCH)
+    above = key_features(float(TRUNK), row, (leaf - 1.0) * 1e30, BRANCH)
+    return own, above
+
+
+def causal(rows):
+    key = lax.broadcasted_iota(jnp.int32, (rows, rows), 0)
+    query = lax.broadcasted_iota(jnp.int32, (rows, rows), 1)
+    once = key <= query
+    return jnp.concatenate([once, once], axis=1)
+
+
+def tree_kernel(
+    dims,
+    tok,
+    wq,
+    info,
+    bias_qv,
+    slopes,
+    gain,
+    shift,
+    act_turned,
+    query,
+    key,
+    value,
+    out_heads,
+    lse,
+    info_all,
+    att,
+    tree,
+    wcat,
+    keys_aug,
+    values_turned,
+    labels,
+    parents,
+    info_send,
+    info_recv,
+    wz_send,
+    wz_recv,
+    ws_send,
+    ws_recv,
+    z_send,
+    z_recv,
+    y_send,
+    y_recv,
+    a_send,
+    a_recv,
+    local_sem,
+):
+    ns, nz, rows = dims
+    s, z, y = lax.axis_index("shard"), lax.axis_index("ctx"), lax.axis_index("tp")
+    half = rows // 2
+    sub = half // 2
+    greet(
+        [{"ctx": lax.rem(z + d, nz)} for d in range(1, nz)]
+        + [{"shard": lax.rem(s + d, ns)} for d in range(1, ns)]
+        + [{"tp": 1 - y}]
+    )
+    start = pltpu.make_async_copy(tok, tree.at[pl.ds(z * rows, rows), :], local_sem)
+    start.start()
+
+    depth = wq.shape[0]
+    wide = 3 * PAIR
+    my_rows = pl.ds((s * nz + z) * depth, depth)
+
+    def info_copy(d):
+        return rcopy(
+            info, info_all.at[z], info_send.at[d - 1], info_recv.at[d - 1], {"ctx": lax.rem(z + d, nz)}
+        )
+
+    def wz_copy(d):
+        to = lax.rem(z + d, nz)
+        return rcopy(
+            wq.at[:, pl.ds(pl.multiple_of(to * wide, 128), wide)],
+            wcat.at[my_rows, :],
+            wz_send.at[d - 1],
+            wz_recv.at[d - 1],
+            {"ctx": to},
+        )
+
+    shard_rows = pl.ds(s * (nz * depth), nz * depth)
+
+    def ws_copy(d):
+        return rcopy(
+            wcat.at[shard_rows, :],
+            wcat.at[shard_rows, :],
+            ws_send.at[d - 1],
+            ws_recv.at[d - 1],
+            {"shard": lax.rem(s + d, ns)},
+        )
+
+    for d in range(1, nz):
+        wz_copy(d).start()
+    for d in range(1, nz):
+        info_copy(d).start()
+    wcat[my_rows, :] = wq[:, pl.ds(pl.multiple_of(z * wide, 128), wide)]
+    info_all[z] = info[...]
+    start.wait()
+
+    def piece(block, second, part):
+        at = block * rows + jnp.where(second, 1 - y, y) * half + part * sub
+        return tree.at[pl.ds(pl.multiple_of(at, 32), sub), :]
+
+    def z_copy(direction, k, part):
+        block = z - k if direction == 0 else z + k
+        to = z + 1 if direction == 0 else z - 1
+        ref = piece(block, False, part)
+        return rcopy(ref, ref, z_send.at[direction, k, part], z_recv.at[direction, k, part], {"ctx": to})
+
+    def z_arrival(direction, k, part):
+        block = z - k if direction == 0 else z + k
+        ref = piece(block, False, part)
+        return rcopy(
+            ref, ref, z_send.at[direction, k - 1, part], z_recv.at[direction, k - 1, part], {"ctx": z}
+        )
+
+    def y_copy(direction, k, part):
+        block = z - k if direction == 0 else z + k
+        ref = piece(block, False, part)
+        return rcopy(
+            ref, ref, y_send.at[direction, k - 1, part], y_recv.at[direction, k - 1, part], {"tp": 1 - y}
+        )
+
+    def y_arrival(direction, k, part):
+        block = z - k if direction == 0 else z + k
+        ref = piece(block, True, part)
+        return rcopy(
+            ref, ref, y_send.at[direction, k - 1, part], y_recv.at[direction, k - 1, part], {"tp": 1 - y}
+        )
+
+    def place(direction, k):
+        block = z - k if direction == 0 else z + k
+        nxt = z + 1 if direction == 0 else z - 1
+        here = (block >= 0) & (block < nz)
+        onward = here & (nxt >= 0) & (nxt < nz)
+        return block, here, onward
+
+    def forward(k, first):
+        for part in range(2):
+            for direction in range(2):
+                _, here, onward = place(direction, k)
+                if not first:
+
+                    @pl.when(here)
+                    def _():
+                        z_arrival(direction, k, part).wait_recv()
+
+                @pl.when(onward & (k < nz - 1))
+                def _():
+                    z_copy(direction, k, part).start()
+
+                if not first:
+
+                    @pl.when(here)
+                    def _():
+                        y_copy(direction, k, part).start()
+
+    forward(0, True)
+    for d in range(1, nz):
+        wz_copy(d).wait_recv()
+    for d in range(1, ns):
+        ws_copy(d).start()
+
+    bias_at = pl.ds(pl.multiple_of(z * PAIR, 128), PAIR)
+    bias_q = bias_qv[0:1, bias_at]
+    bias_v = bias_qv[1:2, bias_at]
+
+    def project(block):
+        def tile(t, carry):
+            at = pl.multiple_of(block * rows + t * 128, 128)
+            here = pl.ds(at, 128)
+            act = norm_rows(tree[here, :].astype(F32), gain[0:1, :], shift[0:1, :])[0].astype(BF)
+            act_turned[:, here] = act.T
+            both = nn(act, wcat[...])
+            query[here, :] = ((both[:, :PAIR] + bias_q).astype(BF).astype(F32) * HD ** (-0.5)).astype(BF)
+            key[here, :] = both[:, PAIR : 2 * PAIR].astype(BF)
+            value[here, :] = (both[:, 2 * PAIR :] + bias_v).astype(BF)
+            return carry
+
+        lax.fori_loop(0, rows // 128, tile, 0)
+
+    for d in range(1, ns):
+        ws_copy(d).wait_recv()
+
+    def wave(k, carry):
+        @pl.when(k > 0)
+        def _():
+            forward(k, False)
+            for part in range(2):
+                for direction in range(2):
+                    _, here, _ = place(direction, k)
+
+                    @pl.when(here)
+                    def _():
+                        y_arrival(direction, k, part).wait_recv()
+
+        def side(direction, inner):
+            block = z + (2 * direction - 1) * k
+
+            @pl.when((block >= 0) & (block < nz) & ((k > 0) | (direction == 0)))
+            def _():
+                project(block)
+
+            return inner
+
+        return lax.fori_loop(0, 2, side, carry)
+
+    lax.fori_loop(0, nz, wave, 0)
+
+    for d in range(1, nz):
+        info_copy(d).wait_recv()
+
+    fill_labels(info_all, rows // BRANCH, labels, parents)
+    fill_trunk_keys(key, keys_aug)
+    values_turned[...] = value[0:TRUNK, :].T
+
+    def att_copy(to):
+        return rcopy(
+            out_heads.at[pl.ds(to * rows, rows), :],
+            att.at[:, pl.ds(pl.multiple_of(z * PAIR, 128), PAIR)],
+            a_send.at[to],
+            a_recv.at[z],
+            {"ctx": to},
+        )
+
+    def send_out(to):
+        @pl.when(z != to)
+        def _():
+            att_copy(to).start()
+
+        @pl.when(z == to)
+        def _():
+            att[:, pl.ds(pl.multiple_of(z * PAIR, 128), PAIR)] = out_heads[to * rows : (to + 1) * rows, :]
+
+    tile_mask = causal(BRANCH)
+    owners = [((owner + 1) * rows - TRUNK) // BRANCH - 1 for owner in range(nz)]
+
+    def segment(slot, carry):
+        here = pl.ds(pl.multiple_of(TRUNK + slot * BRANCH, 128), BRANCH)
+        asked = jnp.concatenate(
+            [stack_heads(query[here, :]), query_features(slopes, BRANCH)], axis=1
+        )
+        leaf, key_up, value_up = parent_pick(slot, labels, parents, key, value)
+        own_feats, up_feats = segment_key_features(leaf)
+        trunk_part = nt(keys_aug[...], asked) * LOG2E
+        own_part = nt(jnp.concatenate([key[here, :], own_feats], axis=1), asked) * LOG2E
+        own_part = jnp.where(tile_mask, own_part, NEG)
+        up_part = nt(jnp.concatenate([key_up, up_feats], axis=1), asked) * LOG2E
+        top = jnp.maximum(
+            jnp.max(trunk_part, axis=0, keepdims=True),
+            jnp.maximum(
+                jnp.max(own_part, axis=0, keepdims=True), jnp.max(up_part, axis=0, keepdims=True)
+            ),
+        )
+        trunk_part = jnp.exp2(trunk_part - top)
+        own_part = jnp.exp2(own_part - top)
+        up_part = jnp.exp2(up_part - top)
+        total = (
+            jnp.sum(trunk_part, axis=0, keepdims=True)
+            + jnp.sum(own_part, axis=0, keepdims=True)
+            + jnp.sum(up_part, axis=0, keepdims=True)
+        )
+        turned = nn(values_turned[...], trunk_part.astype(BF))
+        turned = turned + nn(value[here, :].T, own_part.astype(BF))
+        turned = turned + nn(value_up.T, up_part.astype(BF))
+        turned = turned / total
+        out_heads[here, :] = unstack_turned(turned, BRANCH).astype(BF)
+        lse[pl.ds(4 + slot, 1), 0 : 2 * BRANCH] = top + jnp.log2(total)
+        for owner in range(nz):
+            if owners[owner] >= 0 and owner * rows >= TRUNK:
+
+                @pl.when(slot == owners[owner])
+                def _():
+                    send_out(owner)
+
+        return carry
+
+    lax.fori_loop(0, SLOTS, segment, 0)
+
+    wave_rows = TRUNK // 4
+    wave_mask = causal(wave_rows)
+    sent = 0
+    for tile in range(4):
+        lo, hi = tile * wave_rows, (tile + 1) * wave_rows
+        asked = jnp.concatenate(
+            [stack_heads(query[lo:hi, :]), query_features(slopes, wave_rows)], axis=1
+        )
+        edge = jnp.where(wave_mask, nt(keys_aug[lo:hi, :], asked) * LOG2E, NEG)
+        top = jnp.max(edge, axis=0, keepdims=True)
+        if tile:
+            body = nt(keys_aug[0:lo, :], asked) * LOG2E
+            top = jnp.maximum(top, jnp.max(body, axis=0, keepdims=True))
+            body = jnp.exp2(body - top)
+        edge = jnp.exp2(edge - top)
+        total = jnp.sum(edge, axis=0, keepdims=True)
+        turned = nn(values_turned[:, lo:hi], edge.astype(BF))
+        if tile:
+            total = total + jnp.sum(body, axis=0, keepdims=True)
+            turned = turned + nn(values_turned[:, 0:lo], body.astype(BF))
+        turned = turned / total
+        out_heads[lo:hi, :] = unstack_turned(turned, wave_rows).astype(BF)
+        lse[tile : tile + 1, :] = top + jnp.log2(total)
+        while sent < nz and sent * rows < TRUNK and (sent + 1) * rows <= (hi if hi < TRUNK else TREE):
+            send_out(sent)
+            sent += 1
+
+    for owner in range(nz):
+
+        @pl.when(z != owner)
+        def _():
+            rcopy(
+                out_heads.at[0:rows, :],
+                att.at[:, owner * PAIR : (owner + 1) * PAIR],
+                a_send.at[owner],
+                a_recv.at[owner],
+                {"ctx": owner},
+            ).wait_recv()
+
+    for owner in range(nz):
+
+        @pl.when(z != owner)
+        def _():
+            att_copy(owner).wait_send()
+
+    for d in range(1, nz):
+        info_copy(d).wait_send()
+        wz_copy(d).wait_send()
+    for d in range(1, ns):
+        ws_copy(d).wait_send()
+
+    def drain(k, carry):
+        for part in range(2):
+            for direction in range(2):
+                _, here, onward = place(direction, k)
+
+                @pl.when(onward & (k < nz - 1))
+                def _():
+                    z_copy(direction, k, part).wait_send()
+
+                @pl.when(here & (k > 0))
+                def _():
+                    y_copy(direction, k, part).wait_send()
+
+        return carry
+
+    lax.fori_loop(0, nz, drain, 0)
+
+
+def vmem():
+    return pl.BlockSpec(memory_space=pltpu.VMEM)
+
+
+def shape(dims, kind):
+    return jax.ShapeDtypeStruct(dims, kind)
+
+
+def dma(*dims):
+    return pltpu.SemaphoreType.DMA(dims)
+
+
+def run_tree(dims, tok, wq, info, bias_qv, slopes, gain, shift):
+    ns, nz, rows = dims
+    width = tok.shape[1]
+    return pl.pallas_call(
+        partial(tree_kernel, dims),
+        name="tree_forward",
+        out_shape=(
+            shape((width, TREE), BF),
+            shape((TREE, PAIR), BF),
+            shape((TREE, PAIR), BF),
+            shape((TREE, PAIR), BF),
+            shape((TREE, PAIR), BF),
+            shape((16, 512), F32),
+            shape((nz, 16, 128), F32),
+            shape((rows, nz * PAIR), BF),
+        ),
+        in_specs=[pl.BlockSpec(memory_space=pl.ANY)] + [vmem()] * 6,
+        out_specs=[vmem()] * 8,
+        scratch_shapes=[
+            pltpu.VMEM((TREE, width), BF),
+            pltpu.VMEM((width, 3 * PAIR), BF),
+            pltpu.VMEM((TRUNK, 2 * PAIR), BF),
+            pltpu.VMEM((PAIR, TRUNK), BF),
+            pltpu.VMEM((16, 128), F32),
+            pltpu.VMEM((16, 128), F32),
+            dma(nz - 1),
+            dma(nz - 1),
+            dma(nz - 1),
+            dma(nz - 1),
+            dma(ns - 1),
+            dma(ns - 1),
+            dma(2, nz, 2),
+            dma(2, nz, 2),
+            dma(2, nz, 2),
+            dma(2, nz, 2),
+            dma(nz),
+            dma(nz),
+            pltpu.SemaphoreType.DMA,
+        ],
+        compiler_params=pltpu.CompilerParams(
+            collective_id=0, has_side_effects=True, vmem_limit_bytes=48 << 20
+        ),
+        cost_estimate=pl.CostEstimate(flops=40_000_000_000, bytes_accessed=20_000_000, transcendentals=0),
+    )(tok, wq, info, bias_qv, slopes, gain, shift)
+
+
+UP, OUT, DOWN = "up", "out", "down"
+BLOCK = 512
+CURVE = 0.044715
+ROOT = 0.7978845608028654
+
+
+def feed_kernel(
+    dims,
+    tok,
+    cot,
+    att,
+    wa,
+    wd,
+    b_out,
+    b_up,
+    b_down,
+    gain,
+    shift,
+    gsum,
+    ga_all,
+    down_part,
+    resid,
+    gmid,
+    sums,
+    act,
+    hidden,
+    gup,
+    gbranch,
+    mid,
+    o_send,
+    o_recv,
+    g_send,
+    g_recv,
+    ga_send,
+    bup_acc,
+    os_sem,
+    or_sem,
+    gs_sem,
+    gr_sem,
+    as_sem,
+    ar_sem,
+):
+    ns, nz, rows = dims
+    z, y = lax.axis_index("ctx"), lax.axis_index("tp")
+    chunk = rows // ROWS_WAVE
+    width = tok.shape[1]
+    units = b_up.shape[1]
+    inner = att.shape[1]
+    greet([{"tp": 1 - y}] + [{"ctx": lax.rem(z + d, nz)} for d in range(1, nz)])
+    other = {"tp": 1 - y}
+
+    def at(i):
+        return pl.ds(pl.multiple_of(i * chunk, 32), chunk)
+
+    def o_copy(i):
+        return rcopy(o_send.at[at(i), :], o_recv.at[at(i), :], os_sem.at[i], or_sem.at[i], other)
+
+    def g_copy(i):
+        return rcopy(g_send.at[at(i), :], g_recv.at[at(i), :], gs_sem.at[i], gr_sem.at[i], other)
+
+    def a_copy(i, d):
+        to = lax.rem(z + d, nz)
+        return rcopy(
+            ga_send.at[at(i), pl.ds(pl.multiple_of(to * PAIR, 128), PAIR)],
+            ga_all.at[pl.ds(pl.multiple_of(z * rows + i * chunk, 32), chunk), :],
+            as_sem.at[d - 1, i],
+            ar_sem.at[d - 1, i],
+            {"ctx": to},
+        )
+
+    sums[...] = jnp.zeros(sums.shape, F32)
+    bup_acc[...] = jnp.zeros(bup_acc.shape, F32)
+
+    def stage_a(i, carry):
+        o_send[at(i), :] = nt(att[at(i), :], wa[:, units : units + inner]).astype(BF)
+        o_copy(i).start()
+        return carry
+
+    lax.fori_loop(0, ROWS_WAVE, stage_a, 0)
+
+    def stage_b(i, carry):
+        o_copy(i).wait_recv()
+        here = at(i)
+        branch = o_send[here, :].astype(F32) + o_recv[here, :].astype(F32) + b_out[...]
+        middle = tok[here, :].astype(F32) + branch
+        mid[here, :] = middle
+        resid[here, :] = middle + b_down[...]
+        act[here, :] = norm_rows(middle, gain[1:2, :], shift[1:2, :])[0].astype(BF)
+
+        def columns(c, inner_carry):
+            cols = pl.ds(pl.multiple_of(c * BLOCK, 128), BLOCK)
+            upper = nn(act[here, :], wa[:, cols]) + b_up[:, cols]
+            slope = nn(cot[here, :], wd[:, cols])
+            square = upper * upper
+            turn = jnp.tanh(ROOT * (upper + CURVE * (square * upper)))
+            hidden[here, cols] = (0.5 * upper * (1.0 + turn)).astype(BF)
+            steep = 0.5 * (1.0 + turn) + (0.5 * ROOT) * upper * (1.0 - turn * turn) * (
+                1.0 + (3.0 * CURVE) * square
+            )
+            low = (slope * steep).astype(BF)
+            gup[here, cols] = low
+            bup_acc[:, cols] += jnp.sum(low.astype(F32), axis=0, keepdims=True)
+            return inner_carry
+
+        lax.fori_loop(0, units // BLOCK, columns, 0)
+        g_send[here, :] = nt(gup[here, :], wa[:, 0:units]).astype(BF)
+        g_copy(i).start()
+        down_part[here, :] = nt(hidden[here, :], wd[:, 0:units]).astype(BF)
+        return carry
+
+    lax.fori_loop(0, ROWS_WAVE, stage_b, 0)
+
+    def weight_one(d, carry):
+        cols = pl.ds(pl.multiple_of(d * 128, 128), 128)
+        gsum[cols, units + inner : 2 * units + inner] = nn(cot[:, cols].T, hidden[...]).astype(BF)
+        gsum[cols, 0:units] = nn(act[:, cols].T, gup[...]).astype(BF)
+        return carry
+
+    lax.fori_loop(0, width // 128, weight_one, 0)
+
+    def stage_c(i, carry):
+        g_copy(i).wait_recv()
+        here = at(i)
+        grad = g_send[here, :].astype(F32) + g_recv[here, :].astype(F32)
+        _, normed, inverse = norm_rows(mid[here, :], gain[1:2, :], shift[1:2, :])
+        given = cot[here, :].astype(F32)
+        grad_middle = given + norm_rows_back(grad, normed, inverse, gain[1:2, :])
+        gmid[here, :] = grad_middle
+        low = grad_middle.astype(BF)
+        gbranch[here, :] = low
+        sums[2:3, :] += jnp.sum(low.astype(F32), axis=0, keepdims=True)
+        sums[3:4, :] += jnp.sum(given, axis=0, keepdims=True)
+        sums[4:5, :] += jnp.sum(grad * normed, axis=0, keepdims=True)
+        sums[5:6, :] += jnp.sum(grad, axis=0, keepdims=True)
+        ga_send[here, :] = nn(low, wa[:, units : units + inner]).astype(BF)
+        for d in range(1, nz):
+            a_copy(i, d).start()
+        ga_all[pl.ds(pl.multiple_of(z * rows + i * chunk, 32), chunk), :] = ga_send[
+            here, pl.ds(pl.multiple_of(z * PAIR, 128), PAIR)
+        ]
+        return carry
+
+    lax.fori_loop(0, ROWS_WAVE, stage_c, 0)
+
+    def weight_two(d, carry):
+        cols = pl.ds(pl.multiple_of(d * 128, 128), 128)
+        gsum[cols, units : units + inner] = nn(gbranch[:, cols].T, att[...]).astype(BF)
+        return carry
+
+    lax.fori_loop(0, width // 128, weight_two, 0)
+    for part in range(units // width):
+        sums[part : part + 1, :] = bup_acc[:, part * width : (part + 1) * width]
+
+    def finish(i, carry):
+        o_copy(i).wait_send()
+        g_copy(i).wait_send()
+        for d in range(1, nz):
+            a_copy(i, d).wait_send()
+            a_copy(i, d).wait_recv()
+        return carry
+
+    lax.fori_loop(0, ROWS_WAVE, finish, 0)
+
+
+def run_feed(dims, tok, cot, att, wa, wd, b_out, b_up, b_down, gain, shift):
+    ns, nz, rows = dims
+    width, units, inner = tok.shape[1], b_up.shape[1], att.shape[1]
+    return pl.pallas_call(
+        partial(feed_kernel, dims),
+        name="feed_both",
+        out_shape=(
+            shape((width, 2 * units + inner), BF),
+            shape((TREE, PAIR), BF),
+            shape((rows, width), BF),
+            shape((rows, width), F32),
+            shape((rows, width), F32),
+            shape((8, width), F32),
+        ),
+        in_specs=[vmem()] * 10,
+        out_specs=[vmem()] * 6,
+        scratch_shapes=[
+            pltpu.VMEM((rows, width), BF),
+            pltpu.VMEM((rows, units), BF),
+            pltpu.VMEM((rows, units), BF),
+            pltpu.VMEM((rows, width), BF),
+            pltpu.VMEM((rows, width), F32),
+            pltpu.VMEM((rows, width), BF),
+            pltpu.VMEM((rows, width), BF),
+            pltpu.VMEM((rows, width), BF),
+            pltpu.VMEM((rows, width), BF),
+            pltpu.VMEM((rows, inner), BF),
+            pltpu.VMEM((1, units), F32),
+            dma(ROWS_WAVE),
+            dma(ROWS_WAVE),
+            dma(ROWS_WAVE),
+            dma(ROWS_WAVE),
+            dma(nz - 1, ROWS_WAVE),
+            dma(nz - 1, ROWS_WAVE),
+        ],
+        compiler_params=pltpu.CompilerParams(
+            collective_id=1, has_side_effects=True, vmem_limit_bytes=60 << 20
+        ),
+        cost_estimate=pl.CostEstimate(flops=40_000_000_000, bytes_accessed=20_000_000, transcendentals=0),
+    )(tok, cot, att, wa, wd, b_out, b_up, b_down, gain, shift)
+
+
+def back_kernel(
+    dims,
+    query,
+    key,
+    value,
+    out_heads,
+    lse,
+    info_all,
+    ga_all,
+    act_turned,
+    wd,
+    down_part,
+    resid,
+    gmid,
+    tok,
+    slopes,
+    gain,
+    shift,
+    early,
+    result,
+    gtok,
+    gwqkv,
+    early_sum,
+    late_sum,
+    dqkv,
+    dk_trunk,
+    dv_trunk,
+    dk_seg,
+    dv_seg,
+    dk_up,
+    dv_up,
+    keys_aug,
+    keys_turned,
+    labels,
+    parents,
+    dq_all,
+    n_send,
+    n_recv,
+    down_recv,
+    wg_send,
+    wg_recv,
+    early_recv,
+    late,
+    late_recv,
+    d_sem,
+    e_send,
+    e_recv,
+    l_send,
+    l_recv,
+    w_send,
+    w_recv,
+    p_send,
+    p_recv,
+    ns_sem,
+    nr_sem,
+):
+    ns, nz, rows = dims
+    s, z, y = lax.axis_index("shard"), lax.axis_index("ctx"), lax.axis_index("tp")
+    count = ns * nz
+    me = s * nz + z
+    chunk = rows // ROWS_WAVE
+    width = tok.shape[1]
+    depth = width // count
+    wide = 3 * PAIR
+    units = wd.shape[1] - nz * wide
+    other = {"tp": 1 - y}
+
+    def peer(d):
+        index = lax.rem(me + d, count)
+        return index, {"shard": index // nz, "ctx": lax.rem(index, nz)}
+
+    greet([other] + [peer(d)[1] for d in range(1, count)])
+
+    def down_copy():
+        return rcopy(down_part, down_recv, d_sem.at[0], d_sem.at[1], other)
+
+    def early_copy(d):
+        return rcopy(early, early_recv.at[me], e_send.at[d - 1], e_recv.at[d - 1], peer(d)[1])
+
+    def late_copy(d):
+        return rcopy(late, late_recv.at[me], l_send.at[d - 1], l_recv.at[d - 1], peer(d)[1])
+
+    def wg_copy(d):
+        index, device = peer(d)
+        return rcopy(
+            wg_send.at[pl.ds(pl.multiple_of(index * depth, depth), depth), :],
+            wg_recv.at[me],
+            w_send.at[d - 1],
+            w_recv.at[d - 1],
+            device,
+        )
+
+    def over_peers(act):
+        def one(d, carry):
+            act(d)
+            return carry
+
+        lax.fori_loop(1, count, one, 0)
+
+    down_copy().start()
+    over_peers(lambda d: early_copy(d).start())
+    early_recv[me] = early[...]
+
+    fill_labels(info_all, rows // BRANCH, labels, parents)
+    fill_trunk_keys(key, keys_aug)
+    keys_turned[...] = key[0:TRUNK, :].T
+    dk_trunk[...] = jnp.zeros(dk_trunk.shape, F32)
+    dv_trunk[...] = jnp.zeros(dv_trunk.shape, F32)
+    tile_mask = causal(BRANCH)
+
+    def row_products(here, count_rows):
+        turned = (ga_all[here, :].astype(F32) * out_heads[here, :].astype(F32)).T
+        return jnp.concatenate(
+            [
+                jnp.sum(turned[:HD, :], axis=0, keepdims=True),
+                jnp.sum(turned[HD:, :], axis=0, keepdims=True),
+            ],
+            axis=1,
+        )
+
+    def part_back(key_aug, value_rows, asked, given, level, drow, mask):
+        logits = nt(key_aug, asked) * LOG2E - level
+        if mask is not None:
+            logits = jnp.where(mask, logits, NEG)
+        probs = jnp.exp2(logits)
+        grads = (probs * (nt(value_rows, given) - drow)).astype(BF)
+        return probs.astype(BF), grads
+
+    def segment(slot, carry):
+        here = pl.ds(pl.multiple_of(TRUNK + slot * BRANCH, 128), BRANCH)
+        seg = pl.ds(pl.multiple_of(slot * BRANCH, 128), BRANCH)
+        stacked = stack_heads(query[here, :])
+        asked = jnp.concatenate([stacked, query_features(slopes, BRANCH)], axis=1)
+        given = stack_heads(ga_all[here, :])
+        leaf, key_up, value_up = parent_pick(slot, labels, parents, key, value)
+        own_feats, up_feats = segment_key_features(leaf)
+        level = lse[pl.ds(4 + slot, 1), 0 : 2 * BRANCH]
+        drow = row_products(here, BRANCH)
+        probs, grads = part_back(keys_aug[...], value[0:TRUNK, :], asked, given, level, drow, None)
+        dv_trunk[...] += nn(probs, given)
+        dk_trunk[...] += nn(grads, stacked)
+        turned = nn(keys_turned[...], grads)
+        key_own = key[here, :]
+        probs, grads = part_back(
+            jnp.concatenate([key_own, own_feats], axis=1), value[here, :], asked, given, level, drow, tile_mask
+        )
+        dv_seg[seg, :] = nn(probs, given)
+        dk_seg[seg, :] = nn(grads, stacked)
+        turned = turned + nn(key_own.T, grads)
+        probs, grads = part_back(
+            jnp.concatenate([key_up, up_feats], axis=1), value_up, asked, given, level, drow, None
+        )
+        dv_up[seg, :] = nn(probs, given)
+        dk_up[seg, :] = nn(grads, stacked)
+        turned = turned + nn(key_up.T, grads)
+        dqkv[here, 0:PAIR] = (unstack_turned(turned, BRANCH) * HD ** (-0.5)).astype(BF)
+        return carry
+
+    lax.fori_loop(0, SLOTS, segment, 0)
+
+    def gather_up(slot, carry):
+        here = pl.ds(pl.multiple_of(TRUNK + slot * BRANCH, 128), BRANCH)
+        seg = pl.ds(pl.multiple_of(slot * BRANCH, 128), BRANCH)
+        mine = labels[pl.ds(slot, 1), :]
+        dk, dv = dk_seg[seg, :], dv_seg[seg, :]
+        for below in range(SLOTS):
+            same = (parents[below : below + 1, :] == mine).astype(F32)
+            at = below * BRANCH
+            dk = dk + same * dk_up[at : at + BRANCH, :]
+            dv = dv + same * dv_up[at : at + BRANCH, :]
+        dqkv[here, PAIR : 2 * PAIR] = dk.astype(BF)
+        dqkv[here, 2 * PAIR :] = dv.astype(BF)
+        return carry
+
+    lax.fori_loop(0, SLOTS, gather_up, 0)
+
+    def piece_copy(to):
+        return rcopy(
+            dqkv.at[pl.ds(to * rows, rows), :],
+            dq_all.at[:, pl.ds(pl.multiple_of(z * wide, 128), wide)],
+            p_send.at[to],
+            p_recv.at[z],
+            {"ctx": to},
+        )
+
+    def send_piece(to):
+        @pl.when(z != to)
+        def _():
+            piece_copy(to).start()
+
+        @pl.when(z == to)
+        def _():
+            dq_all[:, pl.ds(pl.multiple_of(z * wide, 128), wide)] = dqkv[to * rows : (to + 1) * rows, :]
+
+    for to in range(nz):
+        if to * rows >= TRUNK:
+            send_piece(to)
+
+    wave_rows = TRUNK // 4
+    wave_mask = causal(wave_rows)
+    for tile in range(4):
+        lo, hi = tile * wave_rows, (tile + 1) * wave_rows
+        stacked = stack_heads(query[lo:hi, :])
+        asked = jnp.concatenate([stacked, query_features(slopes, wave_rows)], axis=1)
+        given = stack_heads(ga_all[lo:hi, :])
+        level = lse[tile : tile + 1, :]
+        drow = row_products(pl.ds(lo, wave_rows), wave_rows)
+        probs, grads = part_back(
+            keys_aug[lo:hi, :], value[lo:hi, :], asked, given, level, drow, wave_mask
+        )
+        dv_trunk[lo:hi, :] += nn(probs, given)
+        dk_trunk[lo:hi, :] += nn(grads, stacked)
+        turned = nn(keys_turned[:, lo:hi], grads)
+        if tile:
+            probs, grads = part_back(
+                keys_aug[0:lo, :], value[0:lo, :], asked, given, level, drow, None
+            )
+            dv_trunk[0:lo, :] += nn(probs, given)
+            dk_trunk[0:lo, :] += nn(grads, stacked)
+            turned = turned + nn(keys_turned[:, 0:lo], grads)
+        dqkv[lo:hi, 0:PAIR] = (unstack_turned(turned, wave_rows) * HD ** (-0.5)).astype(BF)
+    dqkv[0:TRUNK, PAIR : 2 * PAIR] = dk_trunk[...].astype(BF)
+    dqkv[0:TRUNK, 2 * PAIR :] = dv_trunk[...].astype(BF)
+    for to in range(nz):
+        if to * rows < TRUNK:
+            send_piece(to)
+
+    def weight(block, carry):
+        here = pl.ds(pl.multiple_of(block * 128, 128), 128)
+        wg_send[here, :] = nn(act_turned[here, :], dqkv[...]).astype(BF)
+        return carry
+
+    lax.fori_loop(0, width // 128, weight, 0)
+    over_peers(lambda d: wg_copy(d).start())
+    wg_recv[me] = wg_send[pl.ds(pl.multiple_of(me * depth, depth), depth), :]
+
+    late[...] = jnp.zeros(late.shape, F32)
+    late[2:3, pl.ds(pl.multiple_of(z * PAIR, 128), PAIR)] = jnp.sum(
+        dqkv[:, 0:PAIR].astype(F32), axis=0, keepdims=True
+    )
+    late[2:3, pl.ds(pl.multiple_of((nz + z) * PAIR, 128), PAIR)] = jnp.sum(
+        dqkv[:, 2 * PAIR :].astype(F32), axis=0, keepdims=True
+    )
+
+    for owner in range(nz):
+
+        @pl.when(z != owner)
+        def _():
+            rcopy(
+                dqkv.at[0:rows, :],
+                dq_all.at[:, owner * wide : (owner + 1) * wide],
+                p_send.at[owner],
+                p_recv.at[owner],
+                {"ctx": owner},
+            ).wait_recv()
+
+    def at(i):
+        return pl.ds(pl.multiple_of(i * chunk, 32), chunk)
+
+    def n_copy(i):
+        return rcopy(n_send.at[at(i), :], n_recv.at[at(i), :], ns_sem.at[i], nr_sem.at[i], other)
+
+    def first(i, carry):
+        n_send[at(i), :] = nt(dq_all[at(i), :], wd[:, units:]).astype(BF)
+        n_copy(i).start()
+        return carry
+
+    lax.fori_loop(0, ROWS_WAVE, first, 0)
+
+    down_copy().wait_recv()
+
+    def output(i, carry):
+        here = at(i)
+        result[here, :] = (
+            resid[here, :] + (down_part[here, :].astype(F32) + down_recv[here, :].astype(F32))
+        ).astype(BF)
+        return carry
+
+    lax.fori_loop(0, ROWS_WAVE, output, 0)
+    over_peers(lambda d: early_copy(d).wait_recv())
+    total = early_recv[0]
+    for index in range(1, count):
+        total = total + early_recv[index]
+    early_sum[...] = total
+
+    def second(i, carry):
+        n_copy(i).wait_recv()
+        here = at(i)
+        grad = n_send[here, :].astype(F32) + n_recv[here, :].astype(F32)
+        _, normed, inverse = norm_rows(tok[here, :].astype(F32), gain[0:1, :], shift[0:1, :])
+        gtok[here, :] = gmid[here, :] + norm_rows_back(grad, normed, inverse, gain[0:1, :])
+        late[0:1, :] += jnp.sum(grad * normed, axis=0, keepdims=True)
+        late[1:2, :] += jnp.sum(grad, axis=0, keepdims=True)
+        return carry
+
+    lax.fori_loop(0, ROWS_WAVE, second, 0)
+    over_peers(lambda d: late_copy(d).start())
+    late_recv[me] = late[...]
+
+    over_peers(lambda d: wg_copy(d).wait_recv())
+    for owner in range(nz):
+        block = wg_recv[owner].astype(F32)
+        for source in range(1, ns):
+            block = block + wg_recv[source * nz + owner].astype(F32)
+        for part in range(3):
+            gwqkv[part, :, owner * PAIR : (owner + 1) * PAIR] = block[:, part * PAIR : (part + 1) * PAIR]
+
+    over_peers(lambda d: late_copy(d).wait_recv())
+    total = late_recv[0]
+    for index in range(1, count):
+        total = total + late_recv[index]
+    late_sum[...] = total
+
+    down_copy().wait_send()
+    over_peers(lambda d: early_copy(d).wait_send())
+    over_peers(lambda d: late_copy(d).wait_send())
+    over_peers(lambda d: wg_copy(d).wait_send())
+
+    def finish(i, carry):
+        n_copy(i).wait_send()
+        return carry
+
+    lax.fori_loop(0, ROWS_WAVE, finish, 0)
+    for owner in range(nz):
+
+        @pl.when(z != owner)
+        def _():
+            piece_copy(owner).wait_send()
+
+
+def run_back(dims, *inputs):
+    ns, nz, rows = dims
+    width = inputs[12].shape[1]
+    count = ns * nz
+    depth = width // count
+    wide = 3 * PAIR
+    return pl.pallas_call(
+        partial(back_kernel, dims),
+        name="tree_backward",
+        out_shape=(
+            shape((rows, width), BF),
+            shape((rows, width), F32),
+            shape((3, depth, nz * PAIR), F32),
+            shape((8, width), F32),
+            shape((8, width), F32),
+        ),
+        in_specs=[vmem()] * 17,
+        out_specs=[vmem()] * 5,
+        scratch_shapes=[
+            pltpu.VMEM((TREE, wide), BF),
+            pltpu.VMEM((TRUNK, PAIR), F32),
+            pltpu.VMEM((TRUNK, PAIR), F32),
+            pltpu.VMEM((TREE - TRUNK, PAIR), F32),
+            pltpu.VMEM((TREE - TRUNK, PAIR), F32),
+            pltpu.VMEM((TREE - TRUNK, PAIR), F32),
+            pltpu.VMEM((TREE - TRUNK, PAIR), F32),
+            pltpu.VMEM((TRUNK, 2 * PAIR), BF),
+            pltpu.VMEM((PAIR, TRUNK), BF),
+            pltpu.VMEM((16, 128), F32),
+            pltpu.VMEM((16, 128), F32),
+            pltpu.VMEM((rows, nz * wide), BF),
+            pltpu.VMEM((rows, width), BF),
+            pltpu.VMEM((rows, width), BF),
+            pltpu.VMEM((rows, width), BF),
+            pltpu.VMEM((width, wide), BF),
+            pltpu.VMEM((count, depth, wide), BF),
+            pltpu.VMEM((count, 8, width), F32),
+            pltpu.VMEM((8, width), F32),
+            pltpu.VMEM((count, 8, width), F32),
+            dma(2),
+            dma(count - 1),
+            dma(count - 1),
+            dma(count - 1),
+            dma(count - 1),
+            dma(count - 1),
+            dma(count - 1),
+            dma(nz),
+            dma(nz),
+            dma(ROWS_WAVE),
+            dma(ROWS_WAVE),
+        ],
+        compiler_params=pltpu.CompilerParams(
+            collective_id=2, has_side_effects=True, vmem_limit_bytes=60 << 20
+        ),
+        cost_estimate=pl.CostEstimate(flops=40_000_000_000, bytes_accessed=20_000_000, transcendentals=0),
+    )(*inputs)
+
+
+def fast_device(
+    tokens, cotangent, seg_ids, positions, parents, w_qkv, b_qv, w_out, b_out, w_up, b_up, w_down, b_down, ln_gain, ln_bias
+):
+    rows = tokens.shape[0]
+    ns, nz, ntp = lax.axis_size("shard"), lax.axis_size("ctx"), lax.axis_size("tp")
+    dims = (ns, nz, rows)
+    depth = w_qkv.shape[1]
+    wq = w_qkv.reshape(3, depth, nz, PAIR).transpose(1, 2, 0, 3).reshape(depth, nz * 3 * PAIR)
+    both = ("shard", "ctx")
+    wa = lax.all_gather(jnp.concatenate([w_up, w_out.T], axis=1), both, axis=0, tiled=True)
+    wd = lax.all_gather(jnp.concatenate([w_down.T, wq], axis=1), both, axis=0, tiled=True)
+
+    labels = seg_ids.reshape(rows // BRANCH, BRANCH)[:, 0]
+    match = labels[:, None] == jnp.arange(parents.shape[0], dtype=jnp.int32)[None, :]
+    above = jnp.sum(jnp.where(match, parents[None, :], 0), axis=1)
+    fill = 8 - rows // BRANCH
+    lines = jnp.concatenate([jnp.pad(labels, (0, fill)), jnp.pad(above, (0, fill))]).astype(F32)
+    info = jnp.broadcast_to(lines[:, None], (16, 128))
+    per = HEADS // ntp
+    index = lax.axis_index("tp") * per + lax.axis_index("ctx") * 2 + jnp.arange(2)
+    slope = 2.0 ** (-8.0 * (index.astype(F32) + 1.0) / HEADS)
+    one = lax.reduce_precision(slope, 8, 7)
+    two = lax.reduce_precision(slope - one, 8, 7)
+    three = lax.reduce_precision(slope - one - two, 8, 7)
+    table = jnp.stack([one, two, three, one, two, three, jnp.ones_like(one)], axis=1)
+    slopes = jnp.pad(table, ((0, 0), (0, 121)))
+
+    act_turned, query, key, value, out_heads, lse, info_all, att = run_tree(
+        dims, tokens, wq, info, b_qv, slopes, ln_gain, ln_bias
+    )
+    gsum, ga_all, down_part, resid, gmid, sums = run_feed(
+        dims, tokens, cotangent, att, wa, wd, b_out[None, :], b_up[None, :], b_down[None, :], ln_gain, ln_bias
+    )
+    grads = lax.psum_scatter(gsum, both, scatter_dimension=0, tiled=True)
+    result, grad_tokens, grad_w_qkv, early, late = run_back(
+        dims, query, key, value, out_heads, lse, info_all, ga_all, act_turned, wd, down_part, resid, gmid,
+        tokens, slopes, ln_gain, ln_bias, sums,
+    )
+    units, inner = b_up.shape[0], w_out.shape[0]
+    grads = grads.astype(F32)
+    width = tokens.shape[1]
+    return (
+        result,
+        grad_tokens,
+        grad_w_qkv,
+        late[2].reshape(2, nz * PAIR),
+        grads[:, units : units + inner].T,
+        early[2],
+        grads[:, 0:units],
+        early[0:2].reshape(units),
+        grads[:, units + inner :].T,
+        early[3],
+        jnp.stack([late[0], early[4]]),
+        jnp.stack([late[1], early[5]]),
+    )
 
 
 def norm_forward(inputs_in, gain_row, shift_row):
@@ -314,8 +1483,10 @@
         P(),
         P(),
     )
+    sizes = dict(mesh.shape)
+    paired = sizes["tp"] * sizes["ctx"] * 2 == HEADS and sizes["tp"] == 2 and sizes["shard"] == 4
     return jax.shard_map(
-        per_device,
+        fast_device if paired else per_device,
         mesh=mesh,
         in_specs=placed,
         out_specs=(

time: 1230 us -> 441 us (0.36)
  waiting for transfers between devices: 778 us -> 31.8 us
  Pallas kernels: 0 us -> 369 us
  matrix products: 206 us -> 0 us
  blocking collectives: 87.5 us -> 0 us
  other arithmetic: 76.9 us -> 6.29 us
  local copies, waits for them, and re-layouts: 60.2 us -> 17.2 us
    reduce_scatter x5 -> x1, waiting for transfers between devices: 374 us -> 0.01 us  [fast_device(): grads = lax.psum_scatter(gsum, both, scatter_dimension=0, tiled=True)]
    pallas_call x0 -> x3, Pallas kernels: none -> 369 us  [the longest x1 173 us: run_back(): pl.pallas_call(partial(back_kernel, dims), name='tree_backward', out_shap...]
    dot_general x47 -> x0, matrix products: 206 us -> none  [the longest x10 49.1 us: block_scores(): jnp.einsum('qhd,khd->hqk', query_heads, key_heads, preferred_element_type...]
    all_gather x6 -> x2, waiting for transfers between devices: 175 us -> 31.7 us  [the longest x1 31.7 us: fast_device(): lax.all_gather(jnp.concatenate([w_down.T, wq], axis=1), both, axis=0, til...]
    psum x3 -> x0, waiting for transfers between devices: 119 us -> none  [the longest x1 43.8 us: per_device(): lax.psum(jnp.dot(attended_low, full_out, preferred_element_type=jnp.float...]
    unnamed x16 -> x3, waiting for transfers between devices: 111 us -> 0.05 us
    psum x1 -> x0, blocking collectives: 62.5 us -> none  [per_device(): lax.psum((bias_qv_part, out_bias_part, up_bias_part, down_bias_part, gain...]
    select_n x1 -> x0, other arithmetic: 32.4 us -> none  [ancestry(): return (first_up, jnp.take(parents, first_up))]
  transfers between devices with their start and end apart: 15 -> 3, of which waited for: 13 -> 1; matrix products, arithmetic and copies ran while one was open for 18% -> 2% of each run, Pallas kernels for 0% -> 67%
where the time goes in v1:
time: 441 us; the launch traced here: 438 us
  Pallas kernels  369 us (84%)
  waiting for transfers between devices  31.8 us (7%)
  local copies, waits for them, and re-layouts  17.2 us (4%)
  between operations  13.9 us (3%)
  other arithmetic  6.29 us (1%)
    pallas_call x1, Pallas kernels, run_back(): pl.pallas_call(partial(back_kernel, dims), name='tree_backward', out_shap...  173 us
    pallas_call x1, Pallas kernels, run_tree(): pl.pallas_call(partial(tree_kernel, dims), name='tree_forward', out_shape...  119 us
    pallas_call x1, Pallas kernels, run_feed(): pl.pallas_call(partial(feed_kernel, dims), name='feed_both', out_shape=(s...  77 us
    all_gather x1, waiting for transfers between devices, fast_device(): lax.all_gather(jnp.concatenate([w_down.T, wq], axis=1), both, axis=0, til...  31.7 us
    unnamed x41, local copies, waits for them, and re-layouts  10.3 us
  transfers between devices with their start and end apart: 3, of which 1 were waited for; matrix products, arithmetic and copies ran while one was open for 2% of the time, Pallas kernels for 67%

profile of v1, /device:TPU:12, one launch (start us, length us, event | category | flops | bytes accessed | tf_op | source)
XLA Modules:
  0.0 438.2 jit_solution(1158107462854505076)
XLA Ops:
  7.2 0.0 copy-start.16
  7.2 0.0 copy-start.17
  7.2 0.0 copy-start.3
  7.2 0.0 copy-start.2
  7.2 0.0 copy-start.1
  7.2 0.0 all-gather.3.cloned.1.call-start
  7.3 1.8 pad_maximum_fusion.1
  9.1 0.0 all-gather.3.cloned.1.call-update
  9.1 0.0 all-gather.5.cloned.1.call-start
  9.2 1.0 reshape.88
  10.2 0.2 copy.33
  10.4 0.2 reshape.89.wq
  10.5 1.7 pad_maximum_fusion
  12.3 0.0 all-gather.5.cloned.1.call-update
  12.3 0.0 reduce-scatter.2.cloned.1.call-start
  12.4 0.1 stack.6
  12.5 0.0 copy-done.16
  12.5 0.1 slice_reduce_fusion.1
  12.6 0.2 select_reduce_fusion
  12.8 0.1 fusion.2
  12.9 0.1 broadcast_in_dim.31.info
  13.0 118.9 %tree_forward.1 = (bf16[1024,2560]{1,0:T(8,128)(2,1)}, bf16[2560,128]{1,0:T(8,128)(2,1)S(1)}, bf16[2560,128]{1,0:T(8,128)(2,1)S(1)}, bf16[2560,128]{1,0:T(8,128)...) custom-call(bf16[640,1024]{1,0:T(8,128)(2,1)S(1)} %copy-done.1, ...), custom_call_target="tpu_custom_call" | custom-call | flops 40000000000 | bytes 20000000 | tf_op jit(solution)/shard_map/tree_forward/pallas_call | solution.py:492
  132.0 0.0 copy-start.5
  132.0 0.8 copy-done.5
  132.8 0.8 copy-done.6
  133.6 0.9 copy-done.7
  134.5 0.8 copy-done.8
  135.4 0.8 copy-done.9
  136.2 0.6 copy-done.10
  136.8 0.6 copy-done.11
  137.5 31.7 %all-gather.5.cloned.1.call-done.wd = bf16[1024,3584]{1,0:T(8,128)(2,1)} async-done(((bf16[64,3584]{1,0:T(8,128)(2,1)}), bf16[1024,3584]{1,0:T(8,128)(2,1)}) %all-gather.5.cloned.1.call-update) | async-done | bytes 7340048 | tf_op jit(solution)/shard_map/all_gather | solution.py:1139
  169.2 77.0 %feed_both.1 = (bf16[1024,4608]{1,0:T(8,128)(2,1)}, bf16[2560,128]{1,0:T(8,128)(2,1)}, bf16[640,1024]{1,0:T(8,128)(2,1)}, f32[640,1024]{1,0:T(8,128)}, f32[640,1024]{1,0:T(8,128)}, /*index=5*/f32[8,1024]{1,0:T(8,128)}) custom-call(bf16[640,1024]{1,0:T(8,128)(2,1)} %tok.5, bf16[640,1024]{1,0:T(8,128)(2,1)} %cot.1, bf16[640,512]{1,0:T(8,128)(2,1)} %copy-done.9, ...), custom_call_target="tpu_custom_call" | custom-call | flops 40000000000 | bytes 20000000 | tf_op jit(solution)/shard_map/feed_both/pallas_call | solution.py:702
  246.2 0.0 reduce-scatter.2.cloned.1.call-update
  246.2 172.9 %tree_backward.1 = (bf16[640,1024]{1,0:T(8,128)(2,1)}, f32[640,1024]{1,0:T(8,128)}, f32[3,64,512]{2,1,0:T(8,128)}, f32[8,1024]{1,0:T(8,128)}, f32[8,1024]{1,0:T(8,128)}) custom-call(bf16[2560,128]{1,0:T(8,128)(2,1)} %copy-done.5, bf16[2560,128]{1,0:T(8,128)(2,1)} %copy-done.6, bf16[2560,128]{1,0:T(8,128)(2,1)} %copy-done.7, bf16[2560,128]{1,0:T(8,128)(2,1)} %copy-done.8, ...), custom_call_target="tpu_custom_call" | custom-call | flops 40000000000 | bytes 20000000 | tf_op jit(solution)/shard_map/tree_backward/pallas_call | solution.py:1077
  419.2 0.9 slice_bitcast_fusion.2
  420.0 0.6 copy.34
  420.6 0.9 fusion.4
  421.5 0.6 reshape_squeeze.3
  422.1 1.5 fusion.5
  423.6 0.6 pad_maximum_fusion.3
  424.2 0.6 pad_maximum_fusion.2
  424.9 1.2 convert_element_type.32
  426.1 0.7 slice_bitcast_fusion.1
  426.8 0.8 slice_bitcast_fusion
  427.6 0.8 slice.49
  428.4 1.1 copy.38
  429.5 1.5 copy.39
  431.0 0.7 copy.40
  (28 shorter events, 0.1 us)
Async XLA Ops:
  7.2 5.3 %copy-start.16 = (s32[640]{0:T(1024)S(1)}, s32[640]{0:T(1024)}, u32[]{:S(2)}) copy-start(s32[640]{0:T(1024)} %param.17) | copy-start | bytes 7684
  7.2 5.5 %copy-start.17 = (s32[52]{0:T(128)S(1)}, s32[52]{0:T(128)}, u32[]{:S(2)}) copy-start(s32[52]{0:T(128)} %param.18) | copy-start | bytes 628
  7.2 5.8 %copy-start.3 = (f32[2,1024]{1,0:T(2,128)S(1)}, f32[2,1024]{1,0:T(2,128)}, u32[]{:S(2)}) copy-start(f32[2,1024]{1,0:T(2,128)} %shift.5) | copy-start | bytes 24580
  7.2 5.8 %copy-start.2 = (f32[2,1024]{1,0:T(2,128)S(1)}, f32[2,1024]{1,0:T(2,128)}, u32[]{:S(2)}) copy-start(f32[2,1024]{1,0:T(2,128)} %gain.5) | copy-start | bytes 24580
  7.2 5.8 %copy-start.1 = (bf16[640,1024]{1,0:T(8,128)(2,1)S(1)}, bf16[640,1024]{1,0:T(8,128)(2,1)}, u32[]{:S(2)}) copy-start(bf16[640,1024]{1,0:T(8,128)(2,1)} %tok.5) | copy-start | bytes 3932164
  7.2 5.8 %copy-start.4 = (f32[2,512]{1,0:T(2,128)S(1)}, f32[2,512]{1,0:T(2,128)}, u32[]{:S(2)}) copy-start(f32[2,512]{1,0:T(2,128)} %bias_qv.1) | copy-start | bytes 12292
  7.2 130.2 %all-gather.3.cloned.1.call-start = ((), (), s32[]{:S(2)}) async-start(), calls=%async_computation.1 | async-start | bytes 5570560 | tf_op jit(solution)/shard_map/all_gather | solution.py:1138
  9.1 160.0 %all-gather.5.cloned.1.call-start = ((), (), s32[]{:S(2)}) async-start(), calls=%async_computation.2 | async-start | bytes 7798784 | tf_op jit(solution)/shard_map/all_gather | solution.py:1139
  12.3 412.6 %reduce-scatter.2.cloned.1.call-start = ((), (), s32[]{:S(2)}) async-start(), calls=%async_computation.3 | async-start | bytes 10027008 | tf_op jit(solution)/shard_map/reduce_scatter | solution.py:1162
  12.5 119.5 %copy-start = (f32[2,128]{1,0:T(2,128)}, f32[2,128]{1,0:T(2,128)S(1)}, u32[]{:S(2)}) copy-start(f32[2,128]{1,0:T(2,128)S(1)} %pad.13.slopes) | copy-start | bytes 3076
  132.0 0.8 copy-start.5
  132.8 0.8 copy-start.6
  133.6 0.9 copy-start.7
  134.5 0.8 copy-start.8
  135.4 0.8 copy-start.9
  136.2 0.6 copy-start.10
  136.8 0.6 copy-start.11
  419.2 9.3 %copy-start.14 = (bf16[640,1024]{1,0:T(8,128)(2,1)S(1)}, bf16[640,1024]{1,0:T(8,128)(2,1)}, u32[]{:S(2)}) copy-start(bf16[640,1024]{1,0:T(8,128)(2,1)} %get-tuple-element.71) | copy-start | bytes 3932164
  424.9 2.7 copy-start.13
  426.1 3.4 copy-start.12
  429.5 1.5 copy-start.15
Sparse Core Ops, SparseCore 0:
  11.0 70.9 all-gather.2
  84.8 84.3 all-gather.4
  246.4 165.5 reduce-scatter.1

commit v2 on v1

--- a/solution.py
+++ b/solution.py
@@ -23,6 +23,7 @@
 BF = jnp.bfloat16
 F32 = jnp.float32
 ROWS_WAVE = 4
+SPREAD_AT = ((1, 3), (2,), ())
 
 
 def nt(left, right):
@@ -138,15 +139,105 @@
     return jnp.concatenate([once, once], axis=1)
 
 
+class Spread:
+    def __init__(self, full, dims, depth, sems):
+        self.full, self.depth = full, depth
+        self.ns, self.nz, _ = dims
+        self.s, self.z = lax.axis_index("shard"), lax.axis_index("ctx")
+        self.zs, self.zr, self.xs, self.xr, self.cs, self.cr = sems
+
+    def rows(self, shard, place):
+        at = pl.multiple_of((shard * self.nz + place) * self.depth, self.depth)
+        return self.full.at[pl.ds(at, self.depth), :]
+
+    def flip(self, bits):
+        low = lax.rem(self.s, 2)
+        high = lax.div(self.s, 2)
+        if bits & 1:
+            low = 1 - low
+        if bits & 2:
+            high = 1 - high
+        return 2 * high + low
+
+    def z_copy(self, d):
+        ref = self.rows(self.s, self.z)
+        return rcopy(ref, ref, self.zs.at[d - 1], self.zr.at[d - 1], {"ctx": lax.rem(self.z + d, self.nz)})
+
+    def source(self, d):
+        return lax.rem(self.z + self.nz - d, self.nz)
+
+    def x_copy(self, d):
+        ref = self.rows(self.s, self.source(d))
+        return rcopy(ref, ref, self.xs.at[d], self.xr.at[d], {"shard": self.flip(2)})
+
+    def c_copy(self, far, d):
+        ref = self.rows(self.flip(2) if far else self.s, self.source(d))
+        return rcopy(ref, ref, self.cs.at[far, d], self.cr.at[far, d], {"shard": self.flip(1)})
+
+    def z_start(self, d):
+        self.z_copy(d).start()
+
+    def own(self):
+        self.x_copy(0).start()
+        self.c_copy(0, 0).start()
+
+    def z_done(self, d):
+        ref = self.rows(self.s, self.source(d))
+        rcopy(ref, ref, self.zs.at[d - 1], self.zr.at[d - 1], {"ctx": self.z}).wait_recv()
+        self.x_copy(d).start()
+        self.c_copy(0, d).start()
+
+    def x_done(self, d):
+        ref = self.rows(self.flip(2), self.source(d))
+        rcopy(ref, ref, self.xs.at[d], self.xr.at[d], {"shard": self.flip(2)}).wait_recv()
+        self.c_copy(1, d).start()
+
+    def c_done(self, far, d):
+        ref = self.rows(self.flip(3) if far else self.flip(1), self.source(d))
+        rcopy(ref, ref, self.cs.at[far, d], self.cr.at[far, d], {"shard": self.flip(1)}).wait_recv()
+
+    def finish(self):
+        for d in range(self.nz):
+            self.c_done(0, d)
+            self.c_done(1, d)
+        for d in range(self.nz):
+            if d:
+                self.z_copy(d).wait_send()
+            self.x_copy(d).wait_send()
+            self.c_copy(0, d).wait_send()
+            self.c_copy(1, d).wait_send()
+
+
+def spread_sems(nz):
+    return [dma(nz - 1), dma(nz - 1), dma(nz), dma(nz), dma(2, nz), dma(2, nz)]
+
+
+def vmem():
+    return pl.BlockSpec(memory_space=pltpu.VMEM)
+
+
+def shape(dims, kind):
+    return jax.ShapeDtypeStruct(dims, kind)
+
+
+def dma(*dims):
+    return pltpu.SemaphoreType.DMA(dims)
+
+
 def tree_kernel(
     dims,
     tok,
-    wq,
+    w_up,
+    w_out,
+    w_down,
+    wq3,
     info,
     bias_qv,
     slopes,
     gain,
     shift,
+    wfull,
+    wq,
     act_turned,
     query,
     key,
@@ -174,22 +265,35 @@
     a_send,
     a_recv,
     local_sem,
+    *spread,
 ):
     ns, nz, rows = dims
     s, z, y = lax.axis_index("shard"), lax.axis_index("ctx"), lax.axis_index("tp")
     half = rows // 2
     sub = half // 2
+    depth = wq.shape[0]
+    wide = 3 * PAIR
+    my_rows = pl.ds(pl.multiple_of((s * nz + z) * depth, depth), depth)
+    units, inner = w_up.shape[1], w_out.shape[1]
+    starts = [
+        pltpu.make_async_copy(tok, tree.at[pl.ds(pl.multiple_of(z * rows, 128), rows), :], local_sem.at[0]),
+        pltpu.make_async_copy(w_up, wfull.at[my_rows, 0:units], local_sem.at[1]),
+        pltpu.make_async_copy(w_out, wfull.at[my_rows, units : units + inner], local_sem.at[2]),
+        pltpu.make_async_copy(w_down, wfull.at[my_rows, units + inner :], local_sem.at[3]),
+    ]
+    for one in starts:
+        one.start()
+    for to in range(nz):
+        for part in range(3):
+            wq[:, to * wide + part * PAIR : to * wide + (part + 1) * PAIR] = wq3[
+                part, :, to * PAIR : (to + 1) * PAIR
+            ]
     greet(
         [{"ctx": lax.rem(z + d, nz)} for d in range(1, nz)]
         + [{"shard": lax.rem(s + d, ns)} for d in range(1, ns)]
         + [{"tp": 1 - y}]
     )
-    start = pltpu.make_async_copy(tok, tree.at[pl.ds(z * rows, rows), :], local_sem)
-    start.start()
-
-    depth = wq.shape[0]
-    wide = 3 * PAIR
-    my_rows = pl.ds((s * nz + z) * depth, depth)
+    weights = Spread(wfull, dims, depth, spread)
 
     def info_copy(d):
         return rcopy(
@@ -223,7 +327,8 @@
         info_copy(d).start()
     wcat[my_rows, :] = wq[:, pl.ds(pl.multiple_of(z * wide, 128), wide)]
     info_all[z] = info[...]
-    start.wait()
+    for one in starts:
+        one.wait()
 
     def piece(block, second, part):
         at = block * rows + jnp.where(second, 1 - y, y) * half + part * sub
@@ -284,6 +389,7 @@
                         y_copy(direction, k, part).start()
 
     forward(0, True)
+    weights.own()
     for d in range(1, nz):
         wz_copy(d).wait_recv()
     for d in range(1, ns):
@@ -293,47 +399,68 @@
     bias_q = bias_qv[0:1, bias_at]
     bias_v = bias_qv[1:2, bias_at]
 
-    def project(block):
-        def tile(t, carry):
-            at = pl.multiple_of(block * rows + t * 128, 128)
-            here = pl.ds(at, 128)
-            act = norm_rows(tree[here, :].astype(F32), gain[0:1, :], shift[0:1, :])[0].astype(BF)
-            act_turned[:, here] = act.T
-            both = nn(act, wcat[...])
-            query[here, :] = ((both[:, :PAIR] + bias_q).astype(BF).astype(F32) * HD ** (-0.5)).astype(BF)
-            key[here, :] = both[:, PAIR : 2 * PAIR].astype(BF)
-            value[here, :] = (both[:, 2 * PAIR :] + bias_v).astype(BF)
-            return carry
-
-        lax.fori_loop(0, rows // 128, tile, 0)
-
+    def project(k):
+        def side(direction, inner_carry):
+            block = z + (2 * direction - 1) * k
+
+            @pl.when((block >= 0) & (block < nz) & ((k > 0) | (direction == 0)))
+            def _():
+                def tile(t, carry):
+                    here = pl.ds(pl.multiple_of(block * rows + t * 128, 128), 128)
+                    act = norm_rows(tree[here, :].astype(F32), gain[0:1, :], shift[0:1, :])[0].astype(BF)
+                    act_turned[:, here] = act.T
+                    both = nn(act, wcat[...])
+                    query[here, :] = (
+                        (both[:, :PAIR] + bias_q).astype(BF).astype(F32) * HD ** (-0.5)
+                    ).astype(BF)
+                    key[here, :] = both[:, PAIR : 2 * PAIR].astype(BF)
+                    value[here, :] = (both[:, 2 * PAIR :] + bias_v).astype(BF)
+                    return carry
+
+                lax.fori_loop(0, rows // 128, tile, 0)
+
+            return inner_carry
+
+        lax.fori_loop(0, 2, side, 0)
+
+    def shared(k):
+        for part in range(2):
+            for direction in range(2):
+                _, here, _ = place(direction, k)
+
+                @pl.when(here)
+                def _():
+                    y_arrival(direction, k, part).wait_recv()
+
+    forward(1, False)
+    for d in SPREAD_AT[0]:
+        weights.z_start(d)
     for d in range(1, ns):
         ws_copy(d).wait_recv()
+    project(0)
 
     def wave(k, carry):
-        @pl.when(k > 0)
+        forward(k, False)
+
+        @pl.when(k == 2)
         def _():
-            forward(k, False)
-            for part in range(2):
-                for direction in range(2):
-                    _, here, _ = place(direction, k)
-
-                    @pl.when(here)
-                    def _():
-                        y_arrival(direction, k, part).wait_recv()
-
-        def side(direction, inner):
-            block = z + (2 * direction - 1) * k
-
-            @pl.when((block >= 0) & (block < nz) & ((k > 0) | (direction == 0)))
-            def _():
-                project(block)
-
-            return inner
-
-        return lax.fori_loop(0, 2, side, carry)
-
-    lax.fori_loop(0, nz, wave, 0)
+            for d in SPREAD_AT[1]:
+                weights.z_start(d)
+
+        @pl.when(k == 3)
+        def _():
+            for d in SPREAD_AT[2]:
+                weights.z_start(d)
+
+        shared(k - 1)
+        project(k - 1)
+        return carry
+
+    lax.fori_loop(2, nz, wave, 0)
+    for d in SPREAD_AT[0]:
+        weights.z_done(d)
+    shared(nz - 1)
+    project(nz - 1)
 
     for d in range(1, nz):
         info_copy(d).wait_recv()
@@ -432,6 +559,11 @@
             send_out(sent)
             sent += 1
 
+    for d in SPREAD_AT[1] + SPREAD_AT[2]:
+        weights.z_done(d)
+    for d in (0,) + SPREAD_AT[0] + SPREAD_AT[1] + SPREAD_AT[2]:
+        weights.x_done(d)
+
     for owner in range(nz):
 
         @pl.when(z != owner)
@@ -450,6 +582,7 @@
         def _():
             att_copy(owner).wait_send()
 
+    weights.finish()
     for d in range(1, nz):
         info_copy(d).wait_send()
         wz_copy(d).wait_send()
@@ -474,25 +607,17 @@
     lax.fori_loop(0, nz, drain, 0)
 
 
-def vmem():
-    return pl.BlockSpec(memory_space=pltpu.VMEM)
-
-
-def shape(dims, kind):
-    return jax.ShapeDtypeStruct(dims, kind)
-
-
-def dma(*dims):
-    return pltpu.SemaphoreType.DMA(dims)
-
-
-def run_tree(dims, tok, wq, info, bias_qv, slopes, gain, shift):
+def run_tree(dims, tok, w_up, w_out, w_down, wq3, info, bias_qv, slopes, gain, shift):
     ns, nz, rows = dims
     width = tok.shape[1]
+    depth = wq3.shape[1]
+    total = w_up.shape[1] + w_out.shape[1] + w_down.shape[1]
     return pl.pallas_call(
         partial(tree_kernel, dims),
         name="tree_forward",
         out_shape=(
+            shape((width, total), BF),
+            shape((depth, nz * 3 * PAIR), BF),
             shape((width, TREE), BF),
             shape((TREE, PAIR), BF),
             shape((TREE, PAIR), BF),
@@ -502,8 +627,8 @@
             shape((nz, 16, 128), F32),
             shape((rows, nz * PAIR), BF),
         ),
-        in_specs=[pl.BlockSpec(memory_space=pl.ANY)] + [vmem()] * 6,
-        out_specs=[vmem()] * 8,
+        in_specs=[pl.BlockSpec(memory_space=pl.ANY)] * 4 + [vmem()] * 6,
+        out_specs=[vmem()] * 10,
         scratch_shapes=[
             pltpu.VMEM((TREE, width), BF),
             pltpu.VMEM((width, 3 * PAIR), BF),
@@ -523,13 +648,14 @@
             dma(2, nz, 2),
             dma(nz),
             dma(nz),
-            pltpu.SemaphoreType.DMA,
+            dma(4),
+            *spread_sems(nz),
         ],
         compiler_params=pltpu.CompilerParams(
             collective_id=0, has_side_effects=True, vmem_limit_bytes=48 << 20
         ),
         cost_estimate=pl.CostEstimate(flops=40_000_000_000, bytes_accessed=20_000_000, transcendentals=0),
-    )(tok, wq, info, bias_qv, slopes, gain, shift)
+    )(tok, w_up, w_out, w_down, wq3, info, bias_qv, slopes, gain, shift)
 
 
 UP, OUT, DOWN = "up", "out", "down"
@@ -544,12 +670,13 @@
     cot,
     att,
     wa,
-    wd,
+    wq,
     b_out,
     b_up,
     b_down,
     gain,
     shift,
+    wqkv,
     gsum,
     ga_all,
     down_part,
@@ -573,15 +700,23 @@
     gr_sem,
     as_sem,
     ar_sem,
+    *spread,
 ):
     ns, nz, rows = dims
-    z, y = lax.axis_index("ctx"), lax.axis_index("tp")
+    s, z, y = lax.axis_index("shard"), lax.axis_index("ctx"), lax.axis_index("tp")
     chunk = rows // ROWS_WAVE
     width = tok.shape[1]
     units = b_up.shape[1]
     inner = att.shape[1]
-    greet([{"tp": 1 - y}] + [{"ctx": lax.rem(z + d, nz)} for d in range(1, nz)])
+    wd = wa.at[:, units + inner :]
+    weights = Spread(wqkv, dims, wq.shape[0], spread)
+    greet(
+        [{"tp": 1 - y}]
+        + [{"ctx": lax.rem(z + d, nz)} for d in range(1, nz)]
+        + [{"shard": weights.flip(bits)} for bits in (1, 2)]
+    )
     other = {"tp": 1 - y}
+    wqkv[pl.ds(pl.multiple_of((s * nz + z) * wq.shape[0], wq.shape[0]), wq.shape[0]), :] = wq[...]
 
     def at(i):
         return pl.ds(pl.multiple_of(i * chunk, 32), chunk)
@@ -611,6 +746,9 @@
         return carry
 
     lax.fori_loop(0, ROWS_WAVE, stage_a, 0)
+    weights.own()
+    for d in range(1, nz):
+        weights.z_start(d)
 
     def stage_b(i, carry):
         o_copy(i).wait_recv()
@@ -650,7 +788,11 @@
         gsum[cols, 0:units] = nn(act[:, cols].T, gup[...]).astype(BF)
         return carry
 
+    for d in range(1, nz):
+        weights.z_done(d)
     lax.fori_loop(0, width // 128, weight_one, 0)
+    for d in range(nz):
+        weights.x_done(d)
 
     def stage_c(i, carry):
         g_copy(i).wait_recv()
@@ -685,6 +827,8 @@
     for part in range(units // width):
         sums[part : part + 1, :] = bup_acc[:, part * width : (part + 1) * width]
 
+    weights.finish()
+
     def finish(i, carry):
         o_copy(i).wait_send()
         g_copy(i).wait_send()
@@ -696,13 +840,14 @@
     lax.fori_loop(0, ROWS_WAVE, finish, 0)
 
 
-def run_feed(dims, tok, cot, att, wa, wd, b_out, b_up, b_down, gain, shift):
+def run_feed(dims, tok, cot, att, wa, wq, b_out, b_up, b_down, gain, shift):
     ns, nz, rows = dims
     width, units, inner = tok.shape[1], b_up.shape[1], att.shape[1]
     return pl.pallas_call(
         partial(feed_kernel, dims),
         name="feed_both",
         out_shape=(
+            shape((width, wq.shape[1]), BF),
             shape((width, 2 * units + inner), BF),
             shape((TREE, PAIR), BF),
             shape((rows, width), BF),
@@ -711,7 +856,7 @@
             shape((8, width), F32),
         ),
         in_specs=[vmem()] * 10,
-        out_specs=[vmem()] * 6,
+        out_specs=[vmem()] * 7,
         scratch_shapes=[
             pltpu.VMEM((rows, width), BF),
             pltpu.VMEM((rows, units), BF),
@@ -730,12 +875,13 @@
             dma(ROWS_WAVE),
             dma(nz - 1, ROWS_WAVE),
             dma(nz - 1, ROWS_WAVE),
+            *spread_sems(nz),
         ],
         compiler_params=pltpu.CompilerParams(
             collective_id=1, has_side_effects=True, vmem_limit_bytes=60 << 20
         ),
         cost_estimate=pl.CostEstimate(flops=40_000_000_000, bytes_accessed=20_000_000, transcendentals=0),
-    )(tok, cot, att, wa, wd, b_out, b_up, b_down, gain, shift)
+    )(tok, cot, att, wa, wq, b_out, b_up, b_down, gain, shift)
 
 
 def back_kernel(
@@ -748,7 +894,7 @@
     info_all,
     ga_all,
     act_turned,
-    wd,
+    wqkv,
     down_part,
     resid,
     gmid,
@@ -802,7 +948,6 @@
     width = tok.shape[1]
     depth = width // count
     wide = 3 * PAIR
-    units = wd.shape[1] - nz * wide
     other = {"tp": 1 - y}
 
     def peer(d):
@@ -1001,7 +1146,7 @@
         return rcopy(n_send.at[at(i), :], n_recv.at[at(i), :], ns_sem.at[i], nr_sem.at[i], other)
 
     def first(i, carry):
-        n_send[at(i), :] = nt(dq_all[at(i), :], wd[:, units:]).astype(BF)
+        n_send[at(i), :] = nt(dq_all[at(i), :], wqkv[...]).astype(BF)
         n_copy(i).start()
         return carry
 
@@ -1132,11 +1277,7 @@
     rows = tokens.shape[0]
     ns, nz, ntp = lax.axis_size("shard"), lax.axis_size("ctx"), lax.axis_size("tp")
     dims = (ns, nz, rows)
-    depth = w_qkv.shape[1]
-    wq = w_qkv.reshape(3, depth, nz, PAIR).transpose(1, 2, 0, 3).reshape(depth, nz * 3 * PAIR)
     both = ("shard", "ctx")
-    wa = lax.all_gather(jnp.concatenate([w_up, w_out.T], axis=1), both, axis=0, tiled=True)
-    wd = lax.all_gather(jnp.concatenate([w_down.T, wq], axis=1), both, axis=0, tiled=True)
 
     labels = seg_ids.reshape(rows // BRANCH, BRANCH)[:, 0]
     match = labels[:, None] == jnp.arange(parents.shape[0], dtype=jnp.int32)[None, :]
@@ -1153,15 +1294,15 @@
     table = jnp.stack([one, two, three, one, two, three, jnp.ones_like(one)], axis=1)
     slopes = jnp.pad(table, ((0, 0), (0, 121)))
 
-    act_turned, query, key, value, out_heads, lse, info_all, att = run_tree(
-        dims, tokens, wq, info, b_qv, slopes, ln_gain, ln_bias
-    )
-    gsum, ga_all, down_part, resid, gmid, sums = run_feed(
-        dims, tokens, cotangent, att, wa, wd, b_out[None, :], b_up[None, :], b_down[None, :], ln_gain, ln_bias
+    wfull, wq, act_turned, query, key, value, out_heads, lse, info_all, att = run_tree(
+        dims, tokens, w_up, w_out.T, w_down.T, w_qkv, info, b_qv, slopes, ln_gain, ln_bias
+    )
+    wqkv, gsum, ga_all, down_part, resid, gmid, sums = run_feed(
+        dims, tokens, cotangent, att, wfull, wq, b_out[None, :], b_up[None, :], b_down[None, :], ln_gain, ln_bias
     )
     grads = lax.psum_scatter(gsum, both, scatter_dimension=0, tiled=True)
     result, grad_tokens, grad_w_qkv, early, late = run_back(
-        dims, query, key, value, out_heads, lse, info_all, ga_all, act_turned, wd, down_part, resid, gmid,
+        dims, query, key, value, out_heads, lse, info_all, ga_all, act_turned, wqkv, down_part, resid, gmid,
         tokens, slopes, ln_gain, ln_bias, sums,
     )
     units, inner = b_up.shape[0], w_out.shape[0]

time: 441 us -> 426 us (0.966)
  waiting for transfers between devices: 31.8 us -> 0.02 us
  Pallas kernels: 369 us -> 381 us
  local copies, waits for them, and re-layouts: 17.2 us -> 24.3 us
    all_gather x2 -> x0, waiting for transfers between devices: 31.7 us -> none  [the longest x1 31.7 us: fast_device(): lax.all_gather(jnp.concatenate([w_down.T, wq], axis=1), both, axis=0, til...]
    pallas_call x1, Pallas kernels: 77 us -> 90.9 us  [run_feed(): pl.pallas_call(partial(feed_kernel, dims), name='feed_both', out_shape=(s...]
    unnamed x41 -> x47, local copies, waits for them, and re-layouts: 10.3 us -> 18 us
  transfers between devices with their start and end apart: 3 -> 1, of which waited for: 1 -> 0; matrix products, arithmetic and copies ran while one was open for 2% -> 1% of each run, Pallas kernels for 67% -> 41%
where the time goes in v2:
time: 426 us; the launch traced here: 423 us
  Pallas kernels  381 us (89%)
  local copies, waits for them, and re-layouts  24.3 us (6%)
  between operations  14.1 us (3%)
    pallas_call x1, Pallas kernels, run_back(): pl.pallas_call(partial(back_kernel, dims), name='tree_backward', out_shap...  173 us
    pallas_call x1, Pallas kernels, run_tree(): pl.pallas_call(partial(tree_kernel, dims), name='tree_forward', out_shape...  117 us
    pallas_call x1, Pallas kernels, run_feed(): pl.pallas_call(partial(feed_kernel, dims), name='feed_both', out_shape=(s...  90.9 us
    unnamed x47, local copies, waits for them, and re-layouts  18 us
  transfers between devices with their start and end apart: 1, of which 0 were waited for; matrix products, arithmetic and copies ran while one was open for 1% of the time, Pallas kernels for 41%

profile of v2, /device:TPU:12, one launch (start us, length us, event | category | flops | bytes accessed | tf_op | source)
XLA Modules:
  0.0 423.1 jit_solution(8880370424965333823)
XLA Ops:
  7.2 0.0 reduce-scatter.2.cloned.1.call-start
  7.3 0.8 slice_reduce_fusion.1
  8.1 0.8 select_reduce_fusion
  8.9 0.1 fusion.2
  9.0 0.1 stack.6
  9.1 0.1 broadcast_in_dim.31.info
  9.2 1.3 copy-done.1
  10.5 0.9 copy-done.2
  11.4 0.9 copy-done.3
  12.4 0.9 copy-done.4
  13.3 0.8 copy-done.5
  14.2 0.7 copy-done.6
  14.9 0.7 copy-done.7
  15.6 0.7 copy-done.8
  16.2 117.4 %tree_forward.1 = (bf16[1024,4608]{1,0:T(8,128)(2,1)}, bf16[64,1536]{1,0:T(8,128)(2,1)S(1)}, bf16[1024,2560]{1,0:T(8,128)(2,1)}, bf16[2560,128]{1,0:T(8,128)(2,1...) custom-call(bf16[640,1024]{1,0:T(8,128)(2,1)S(1)} %copy-done.1, ...), custom_call_target="tpu_custom_call" | custom-call | flops 40000000000 | bytes 20000000 | tf_op jit(solution)/shard_map/tree_forward/pallas_call | solution.py:615
  133.7 0.0 copy-done
  133.7 0.0 copy-start.9
  133.7 0.8 copy-done.9
  134.5 0.8 copy-done.10
  135.3 0.9 copy-done.11
  136.2 0.9 copy-done.12
  137.1 0.8 copy-done.13
  137.9 0.7 copy-done.14
  138.6 0.6 copy-done.15
  139.2 0.6 copy-done.16
  139.8 90.9 %feed_both.1 = (bf16[1024,1536]{1,0:T(8,128)(2,1)}, bf16[1024,4608]{1,0:T(8,128)(2,1)}, bf16[2560,128]{1,0:T(8,128)(2,1)}, bf16[640,1024]{1,0:T(8,128)(2,1)}, f3...) custom-call(bf16[640,1024]{1,0:T(8,128)(2,1)} %tok.5, bf16[640,1024]{1,0:T(8,128)(2,1)} %cot.1, ...), custom_call_target="tpu_custom_call" | custom-call | flops 40000000000 | bytes 20000000 | tf_op jit(solution)/shard_map/feed_both/pallas_call | solution.py:846
  230.8 0.0 reduce-scatter.2.cloned.1.call-update
  230.8 172.9 %tree_backward.1 = (bf16[640,1024]{1,0:T(8,128)(2,1)}, f32[640,1024]{1,0:T(8,128)}, f32[3,64,512]{2,1,0:T(8,128)}, f32[8,1024]{1,0:T(8,128)}, f32[8,1024]{1,0:T(8,128)}) custom-call(bf16[2560,128]{1,0:T(8,128)(2,1)} %copy-done.9, bf16[2560,128]{1,0:T(8,128)(2,1)} %copy-done.10, bf16[2560,128]{1,0:T(8,128)(2,1)} %copy-done.11, bf16[2560,128]{1,0:T(8,128)(2,1)} %copy-done.12, ...), custom_call_target="tpu_custom_call" | custom-call | flops 40000000000 | bytes 20000000 | tf_op jit(solution)/shard_map/tree_backward/pallas_call | solution.py:1222
  403.7 0.0 copy-start.19
  403.7 0.9 slice_bitcast_fusion.2
  404.6 0.6 copy.28
  405.2 0.9 fusion.4
  406.1 0.6 reshape_squeeze.3
  406.7 1.5 fusion.5
  408.2 0.6 pad_maximum_fusion.1
  408.8 0.6 pad_maximum_fusion
  409.4 1.2 convert_element_type.32
  410.6 0.0 copy-start.17
  410.7 0.7 slice_bitcast_fusion.1
  411.3 0.8 slice_bitcast_fusion
  412.2 0.0 copy-done.18
  412.2 0.8 slice.49
  413.0 0.0 copy-done.19
  413.0 1.1 copy.32
  414.0 0.0 copy-done.17
  414.0 1.5 copy.33
  415.5 0.0 copy-done.20
  415.5 0.7 copy.34
  (23 shorter events, 0.1 us)
Async XLA Ops:
  7.2 402.3 %reduce-scatter.2.cloned.1.call-start = ((), (), s32[]{:S(2)}) async-start(), calls=%async_computation.1 | async-start | bytes 10027008 | tf_op jit(solution)/shard_map/reduce_scatter | solution.py:1303
  9.1 124.6 %copy-start = (f32[2,128]{1,0:T(2,128)}, f32[2,128]{1,0:T(2,128)S(1)}, u32[]{:S(2)}) copy-start(f32[2,128]{1,0:T(2,128)S(1)} %pad.13.slopes) | copy-start | bytes 3076
  9.2 1.3 copy-start.1
  10.5 0.9 copy-start.2
  11.4 0.9 copy-start.3
  12.4 0.9 copy-start.4
  13.3 0.8 copy-start.5
  14.2 0.7 copy-start.6
  14.9 0.7 copy-start.7
  15.6 0.7 copy-start.8
  133.7 0.8 copy-start.9
  134.5 0.8 copy-start.10
  135.3 0.9 copy-start.11
  136.2 0.9 copy-start.12
  137.1 0.8 copy-start.13
  137.9 0.7 copy-start.14
  138.6 0.6 copy-start.15
  139.2 0.6 copy-start.16
  403.7 9.3 %copy-start.19 = (bf16[640,1024]{1,0:T(8,128)(2,1)S(1)}, bf16[640,1024]{1,0:T(8,128)(2,1)}, u32[]{:S(2)}) copy-start(bf16[640,1024]{1,0:T(8,128)(2,1)} %get-tuple-element.77) | copy-start | bytes 3932164
  409.4 2.7 copy-start.18
  410.6 3.4 copy-start.17
  414.0 1.5 copy-start.20
Sparse Core Ops, SparseCore 0:
  230.9 167.2 reduce-scatter.1

commit v3 on v2

--- a/solution.py
+++ b/solution.py
@@ -140,15 +140,15 @@
 
 
 class Spread:
-    def __init__(self, full, dims, depth, sems):
-        self.full, self.depth = full, depth
+    def __init__(self, full, dims, depth, cols, sems):
+        self.full, self.depth, self.cols = full, depth, cols
         self.ns, self.nz, _ = dims
         self.s, self.z = lax.axis_index("shard"), lax.axis_index("ctx")
         self.zs, self.zr, self.xs, self.xr, self.cs, self.cr = sems
 
     def rows(self, shard, place):
         at = pl.multiple_of((shard * self.nz + place) * self.depth, self.depth)
-        return self.full.at[pl.ds(at, self.depth), :]
+        return self.full.at[pl.ds(at, self.depth), self.cols]
 
     def flip(self, bits):
         low = lax.rem(self.s, 2)
@@ -196,10 +196,12 @@
         ref = self.rows(self.flip(3) if far else self.flip(1), self.source(d))
         rcopy(ref, ref, self.cs.at[far, d], self.cr.at[far, d], {"shard": self.flip(1)}).wait_recv()
 
-    def finish(self):
+    def all_here(self):
         for d in range(self.nz):
             self.c_done(0, d)
             self.c_done(1, d)
+
+    def finish(self):
         for d in range(self.nz):
             if d:
                 self.z_copy(d).wait_send()
@@ -265,6 +267,10 @@
     a_send,
     a_recv,
     local_sem,
+    b_send,
+    b_recv,
+    t_send,
+    t_recv,
     *spread,
 ):
     ns, nz, rows = dims
@@ -275,11 +281,12 @@
     wide = 3 * PAIR
     my_rows = pl.ds(pl.multiple_of((s * nz + z) * depth, depth), depth)
     units, inner = w_up.shape[1], w_out.shape[1]
+    own_cols = pl.multiple_of(2 * units + y * inner, 128)
     starts = [
         pltpu.make_async_copy(tok, tree.at[pl.ds(pl.multiple_of(z * rows, 128), rows), :], local_sem.at[0]),
         pltpu.make_async_copy(w_up, wfull.at[my_rows, 0:units], local_sem.at[1]),
-        pltpu.make_async_copy(w_out, wfull.at[my_rows, units : units + inner], local_sem.at[2]),
-        pltpu.make_async_copy(w_down, wfull.at[my_rows, units + inner :], local_sem.at[3]),
+        pltpu.make_async_copy(w_down, wfull.at[my_rows, units : 2 * units], local_sem.at[2]),
+        pltpu.make_async_copy(w_out, wfull.at[my_rows, pl.ds(own_cols, inner)], local_sem.at[3]),
     ]
     for one in starts:
         one.start()
@@ -293,7 +300,8 @@
         + [{"shard": lax.rem(s + d, ns)} for d in range(1, ns)]
         + [{"tp": 1 - y}]
     )
-    weights = Spread(wfull, dims, depth, spread)
+    weights = Spread(wfull, dims, depth, slice(0, 2 * units), spread[:6])
+    outer = Spread(wfull, dims, depth, pl.ds(own_cols, inner), spread[6:])
 
     def info_copy(d):
         return rcopy(
@@ -390,6 +398,7 @@
 
     forward(0, True)
     weights.own()
+    outer.own()
     for d in range(1, nz):
         wz_copy(d).wait_recv()
     for d in range(1, ns):
@@ -433,6 +442,8 @@
                     y_arrival(direction, k, part).wait_recv()
 
     forward(1, False)
+    for d in range(1, nz):
+        outer.z_start(d)
     for d in SPREAD_AT[0]:
         weights.z_start(d)
     for d in range(1, ns):
@@ -457,8 +468,12 @@
         return carry
 
     lax.fori_loop(2, nz, wave, 0)
+    for d in range(1, nz):
+        outer.z_done(d)
     for d in SPREAD_AT[0]:
         weights.z_done(d)
+    for d in range(nz):
+        outer.x_done(d)
     shared(nz - 1)
     project(nz - 1)
 
@@ -469,14 +484,49 @@
     fill_trunk_keys(key, keys_aug)
     values_turned[...] = value[0:TRUNK, :].T
 
+    def att_cols(half_at, owner):
+        return pl.ds(pl.multiple_of(half_at * inner + owner * PAIR, 128), PAIR)
+
     def att_copy(to):
         return rcopy(
             out_heads.at[pl.ds(to * rows, rows), :],
-            att.at[:, pl.ds(pl.multiple_of(z * PAIR, 128), PAIR)],
+            att.at[:, att_cols(y, z)],
             a_send.at[to],
             a_recv.at[z],
             {"ctx": to},
         )
+
+    def pass_on(owner):
+        return rcopy(
+            att.at[:, att_cols(y, owner)],
+            att.at[:, att_cols(y, owner)],
+            b_send.at[owner],
+            b_recv.at[owner],
+            {"tp": 1 - y},
+        )
+
+    half_rows = pl.ds(pl.multiple_of(lax.rem(s, 2) * (ns * nz * depth // 2), 128), ns * nz * depth // 2)
+    far_rows = pl.ds(pl.multiple_of((1 - lax.rem(s, 2)) * (ns * nz * depth // 2), 128), ns * nz * depth // 2)
+    far_cols = pl.ds(pl.multiple_of(2 * units + (1 - y) * inner, 128), inner)
+
+    def plane_copy():
+        ref = wfull.at[half_rows, pl.ds(own_cols, inner)]
+        return rcopy(ref, ref, t_send.at[0], t_recv.at[0], {"tp": 1 - y})
+
+    def plane_arrival():
+        ref = wfull.at[half_rows, far_cols]
+        return rcopy(ref, ref, t_send.at[0], t_recv.at[0], {"tp": 1 - y})
+
+    def core_copy():
+        ref = wfull.at[half_rows, far_cols]
+        return rcopy(ref, ref, t_send.at[1], t_recv.at[1], {"shard": outer.flip(1)})
+
+    def core_arrival():
+        ref = wfull.at[far_rows, far_cols]
+        return rcopy(ref, ref, t_send.at[1], t_recv.at[1], {"shard": outer.flip(1)})
+
+    outer.all_here()
+    plane_copy().start()
 
     def send_out(to):
         @pl.when(z != to)
@@ -485,7 +535,8 @@
 
         @pl.when(z == to)
         def _():
-            att[:, pl.ds(pl.multiple_of(z * PAIR, 128), PAIR)] = out_heads[to * rows : (to + 1) * rows, :]
+            att[:, att_cols(y, z)] = out_heads[to * rows : (to + 1) * rows, :]
+            pass_on(z).start()
 
     tile_mask = causal(BRANCH)
     owners = [((owner + 1) * rows - TRUNK) // BRANCH - 1 for owner in range(nz)]
@@ -561,20 +612,32 @@
 
     for d in SPREAD_AT[1] + SPREAD_AT[2]:
         weights.z_done(d)
-    for d in (0,) + SPREAD_AT[0] + SPREAD_AT[1] + SPREAD_AT[2]:
-        weights.x_done(d)
-
+    plane_arrival().wait_recv()
+    core_copy().start()
     for owner in range(nz):
 
         @pl.when(z != owner)
         def _():
             rcopy(
                 out_heads.at[0:rows, :],
-                att.at[:, owner * PAIR : (owner + 1) * PAIR],
+                att.at[:, att_cols(y, owner)],
                 a_send.at[owner],
                 a_recv.at[owner],
                 {"ctx": owner},
             ).wait_recv()
+            pass_on(owner).start()
+
+    for d in (0,) + SPREAD_AT[0] + SPREAD_AT[1] + SPREAD_AT[2]:
+        weights.x_done(d)
+    for owner in range(nz):
+        ref = att.at[:, att_cols(1 - y, owner)]
+        rcopy(ref, ref, b_send.at[owner], b_recv.at[owner], {"tp": 1 - y}).wait_recv()
+    core_arrival().wait_recv()
+    weights.all_here()
+    plane_copy().wait_send()
+    core_copy().wait_send()
+    for owner in range(nz):
+        pass_on(owner).wait_send()
 
     for owner in range(nz):
 
@@ -583,6 +646,7 @@
             att_copy(owner).wait_send()
 
     weights.finish()
+    outer.finish()
     for d in range(1, nz):
         info_copy(d).wait_send()
         wz_copy(d).wait_send()
@@ -611,7 +675,7 @@
     ns, nz, rows = dims
     width = tok.shape[1]
     depth = wq3.shape[1]
-    total = w_up.shape[1] + w_out.shape[1] + w_down.shape[1]
+    total = w_up.shape[1] + 2 * w_out.shape[1] + w_down.shape[1]
     return pl.pallas_call(
         partial(tree_kernel, dims),
         name="tree_forward",
@@ -625,7 +689,7 @@
             shape((TREE, PAIR), BF),
             shape((16, 512), F32),
             shape((nz, 16, 128), F32),
-            shape((rows, nz * PAIR), BF),
+            shape((rows, 2 * nz * PAIR), BF),
         ),
         in_specs=[pl.BlockSpec(memory_space=pl.ANY)] * 4 + [vmem()] * 6,
         out_specs=[vmem()] * 10,
@@ -649,6 +713,11 @@
             dma(nz),
             dma(nz),
             dma(4),
+            dma(nz),
+            dma(nz),
+            dma(2),
+            dma(2),
+            *spread_sems(nz),
             *spread_sems(nz),
         ],
         compiler_params=pltpu.CompilerParams(
@@ -658,7 +727,6 @@
     )(tok, w_up, w_out, w_down, wq3, info, bias_qv, slopes, gain, shift)
 
 
-UP, OUT, DOWN = "up", "out", "down"
 BLOCK = 512
 CURVE = 0.044715
 ROOT = 0.7978845608028654
@@ -673,33 +741,32 @@
     wq,
     b_out,
     b_up,
-    b_down,
     gain,
     shift,
     wqkv,
-    gsum,
+    near,
+    far,
     ga_all,
     down_part,
-    resid,
+    mid,
     gmid,
     sums,
+    gsum,
+    core_in,
     act,
     hidden,
     gup,
     gbranch,
-    mid,
-    o_send,
-    o_recv,
     g_send,
     g_recv,
     ga_send,
     bup_acc,
-    os_sem,
-    or_sem,
     gs_sem,
     gr_sem,
     as_sem,
     ar_sem,
+    cs_sem,
+    cr_sem,
     *spread,
 ):
     ns, nz, rows = dims
@@ -707,22 +774,22 @@
     chunk = rows // ROWS_WAVE
     width = tok.shape[1]
     units = b_up.shape[1]
-    inner = att.shape[1]
-    wd = wa.at[:, units + inner :]
-    weights = Spread(wqkv, dims, wq.shape[0], spread)
+    inner = att.shape[1] // 2
+    wd = wa.at[:, units : 2 * units]
+    wo = wa.at[:, 2 * units :]
+    own_heads = pl.ds(pl.multiple_of(y * inner, 128), inner)
+    depth = wq.shape[0]
+    weights = Spread(wqkv, dims, depth, slice(None), spread)
     greet(
         [{"tp": 1 - y}]
         + [{"ctx": lax.rem(z + d, nz)} for d in range(1, nz)]
         + [{"shard": weights.flip(bits)} for bits in (1, 2)]
     )
     other = {"tp": 1 - y}
-    wqkv[pl.ds(pl.multiple_of((s * nz + z) * wq.shape[0], wq.shape[0]), wq.shape[0]), :] = wq[...]
+    wqkv[pl.ds(pl.multiple_of((s * nz + z) * depth, depth), depth), :] = wq[...]
 
     def at(i):
         return pl.ds(pl.multiple_of(i * chunk, 32), chunk)
-
-    def o_copy(i):
-        return rcopy(o_send.at[at(i), :], o_recv.at[at(i), :], os_sem.at[i], or_sem.at[i], other)
 
     def g_copy(i):
         return rcopy(g_send.at[at(i), :], g_recv.at[at(i), :], gs_sem.at[i], gr_sem.at[i], other)
@@ -737,26 +804,33 @@
             {"ctx": to},
         )
 
+    span = nz * depth
+    parts = ((0, 2 * units), (2 * units, 2 * units + inner))
+
+    def group(bits):
+        return pl.ds(pl.multiple_of(weights.flip(bits) * span, 128), span)
+
+    def c_copy(part, index):
+        lo, hi = parts[part]
+        return rcopy(
+            gsum.at[group((1, 3)[index]), lo:hi],
+            core_in.at[index, :, lo:hi],
+            cs_sem.at[part, index],
+            cr_sem.at[part, index],
+            {"shard": weights.flip(1)},
+        )
+
     sums[...] = jnp.zeros(sums.shape, F32)
     bup_acc[...] = jnp.zeros(bup_acc.shape, F32)
-
-    def stage_a(i, carry):
-        o_send[at(i), :] = nt(att[at(i), :], wa[:, units : units + inner]).astype(BF)
-        o_copy(i).start()
-        return carry
-
-    lax.fori_loop(0, ROWS_WAVE, stage_a, 0)
     weights.own()
     for d in range(1, nz):
         weights.z_start(d)
 
     def stage_b(i, carry):
-        o_copy(i).wait_recv()
         here = at(i)
-        branch = o_send[here, :].astype(F32) + o_recv[here, :].astype(F32) + b_out[...]
+        branch = nt(att[here, :], wo[...]) + b_out[...]
         middle = tok[here, :].astype(F32) + branch
         mid[here, :] = middle
-        resid[here, :] = middle + b_down[...]
         act[here, :] = norm_rows(middle, gain[1:2, :], shift[1:2, :])[0].astype(BF)
 
         def columns(c, inner_carry):
@@ -777,20 +851,21 @@
         lax.fori_loop(0, units // BLOCK, columns, 0)
         g_send[here, :] = nt(gup[here, :], wa[:, 0:units]).astype(BF)
         g_copy(i).start()
-        down_part[here, :] = nt(hidden[here, :], wd[:, 0:units]).astype(BF)
         return carry
 
     lax.fori_loop(0, ROWS_WAVE, stage_b, 0)
+    for d in range(1, nz):
+        weights.z_done(d)
 
     def weight_one(d, carry):
         cols = pl.ds(pl.multiple_of(d * 128, 128), 128)
-        gsum[cols, units + inner : 2 * units + inner] = nn(cot[:, cols].T, hidden[...]).astype(BF)
         gsum[cols, 0:units] = nn(act[:, cols].T, gup[...]).astype(BF)
+        gsum[cols, units : 2 * units] = nn(cot[:, cols].T, hidden[...]).astype(BF)
         return carry
 
-    for d in range(1, nz):
-        weights.z_done(d)
     lax.fori_loop(0, width // 128, weight_one, 0)
+    for index in range(2):
+        c_copy(0, index).start()
     for d in range(nz):
         weights.x_done(d)
 
@@ -808,7 +883,7 @@
         sums[3:4, :] += jnp.sum(given, axis=0, keepdims=True)
         sums[4:5, :] += jnp.sum(grad * normed, axis=0, keepdims=True)
         sums[5:6, :] += jnp.sum(grad, axis=0, keepdims=True)
-        ga_send[here, :] = nn(low, wa[:, units : units + inner]).astype(BF)
+        ga_send[here, :] = nn(low, wo[:, own_heads]).astype(BF)
         for d in range(1, nz):
             a_copy(i, d).start()
         ga_all[pl.ds(pl.multiple_of(z * rows + i * chunk, 32), chunk), :] = ga_send[
@@ -820,17 +895,46 @@
 
     def weight_two(d, carry):
         cols = pl.ds(pl.multiple_of(d * 128, 128), 128)
-        gsum[cols, units : units + inner] = nn(gbranch[:, cols].T, att[...]).astype(BF)
+        gsum[cols, 2 * units : 2 * units + inner] = nn(gbranch[:, cols].T, att[:, own_heads]).astype(BF)
         return carry
 
     lax.fori_loop(0, width // 128, weight_two, 0)
+    for index in range(2):
+        c_copy(1, index).start()
+
+    def down(i, carry):
+        down_part[at(i), :] = nt(hidden[at(i), :], wd[...]).astype(BF)
+        return carry
+
+    lax.fori_loop(0, ROWS_WAVE, down, 0)
     for part in range(units // width):
         sums[part : part + 1, :] = bup_acc[:, part * width : (part + 1) * width]
 
+    def join(part):
+        lo, hi = parts[part]
+        for index in range(2):
+            c_copy(part, index).wait_recv()
+
+        def one(r, carry):
+            here = pl.ds(pl.multiple_of(r * 32, 32), 32)
+            for index, target in ((0, near), (1, far)):
+                mine = pl.ds(pl.multiple_of(weights.flip((0, 2)[index]) * span + r * 32, 32), 32)
+                target[here, lo:hi] = (
+                    gsum[mine, lo:hi].astype(F32) + core_in[index, here, lo:hi].astype(F32)
+                ).astype(BF)
+            return carry
+
+        lax.fori_loop(0, span // 32, one, 0)
+
+    join(0)
+    join(1)
+    weights.all_here()
     weights.finish()
+    for part in range(2):
+        for index in range(2):
+            c_copy(part, index).wait_send()
 
     def finish(i, carry):
-        o_copy(i).wait_send()
         g_copy(i).wait_send()
         for d in range(1, nz):
             a_copy(i, d).wait_send()
@@ -840,30 +944,32 @@
     lax.fori_loop(0, ROWS_WAVE, finish, 0)
 
 
-def run_feed(dims, tok, cot, att, wa, wq, b_out, b_up, b_down, gain, shift):
+def run_feed(dims, tok, cot, att, wa, wq, b_out, b_up, gain, shift):
     ns, nz, rows = dims
-    width, units, inner = tok.shape[1], b_up.shape[1], att.shape[1]
+    width, units, inner = tok.shape[1], b_up.shape[1], att.shape[1] // 2
+    span = nz * wq.shape[0]
+    total = 2 * units + inner
     return pl.pallas_call(
         partial(feed_kernel, dims),
         name="feed_both",
         out_shape=(
             shape((width, wq.shape[1]), BF),
-            shape((width, 2 * units + inner), BF),
+            shape((span, total), BF),
+            shape((span, total), BF),
             shape((TREE, PAIR), BF),
             shape((rows, width), BF),
             shape((rows, width), F32),
             shape((rows, width), F32),
             shape((8, width), F32),
         ),
-        in_specs=[vmem()] * 10,
-        out_specs=[vmem()] * 7,
+        in_specs=[vmem()] * 9,
+        out_specs=[vmem()] * 8,
         scratch_shapes=[
+            pltpu.VMEM((width, total), BF),
+            pltpu.VMEM((2, span, total), BF),
             pltpu.VMEM((rows, width), BF),
             pltpu.VMEM((rows, units), BF),
             pltpu.VMEM((rows, units), BF),
-            pltpu.VMEM((rows, width), BF),
-            pltpu.VMEM((rows, width), F32),
-            pltpu.VMEM((rows, width), BF),
             pltpu.VMEM((rows, width), BF),
             pltpu.VMEM((rows, width), BF),
             pltpu.VMEM((rows, width), BF),
@@ -871,17 +977,98 @@
             pltpu.VMEM((1, units), F32),
             dma(ROWS_WAVE),
             dma(ROWS_WAVE),
-            dma(ROWS_WAVE),
-            dma(ROWS_WAVE),
             dma(nz - 1, ROWS_WAVE),
             dma(nz - 1, ROWS_WAVE),
+            dma(2, 2),
+            dma(2, 2),
             *spread_sems(nz),
         ],
         compiler_params=pltpu.CompilerParams(
-            collective_id=1, has_side_effects=True, vmem_limit_bytes=60 << 20
+            collective_id=1, has_side_effects=True, vmem_limit_bytes=62 << 20
         ),
         cost_estimate=pl.CostEstimate(flops=40_000_000_000, bytes_accessed=20_000_000, transcendentals=0),
-    )(tok, cot, att, wa, wq, b_out, b_up, b_down, gain, shift)
+    )(tok, cot, att, wa, wq, b_out, b_up, gain, shift)
+
+
+class Halve:
+    def __init__(self, near, far, cols, dims, depth, bufs, sems):
+        self.near, self.far, self.cols, self.depth = near, far, cols, depth
+        self.nz = dims[1]
+        self.s, self.z = lax.axis_index("shard"), lax.axis_index("ctx")
+        self.x_in, self.a_in, self.b_out, self.b_in = bufs
+        self.xs, self.xr, self.as_, self.ar, self.bs, self.br = sems
+
+    def place(self, bits):
+        low, high = lax.rem(self.z, 2), lax.div(self.z, 2)
+        low = 1 - low if bits & 1 else low
+        high = 1 - high if bits & 2 else high
+        return 2 * high + low
+
+    def block(self, bits):
+        return pl.ds(pl.multiple_of(self.place(bits) * self.depth, self.depth), self.depth)
+
+    def x_copy(self):
+        low, high = lax.rem(self.s, 2), lax.div(self.s, 2)
+        return rcopy(
+            self.far.at[:, self.cols],
+            self.x_in.at[:, self.cols],
+            self.xs,
+            self.xr,
+            {"shard": 2 * (1 - high) + low},
+        )
+
+    def a_copy(self, index):
+        return rcopy(
+            self.near.at[self.block((1, 3)[index]), self.cols],
+            self.a_in.at[index, :, self.cols],
+            self.as_.at[index],
+            self.ar.at[index],
+            {"ctx": self.place(1)},
+        )
+
+    def b_copy(self):
+        return rcopy(
+            self.b_out.at[:, self.cols], self.b_in.at[:, self.cols], self.bs, self.br, {"ctx": self.place(2)}
+        )
+
+    def step_x(self):
+        self.x_copy().wait_recv()
+
+        def one(r, carry):
+            here = pl.ds(pl.multiple_of(r * 32, 32), 32)
+            self.near[here, self.cols] = (
+                self.near[here, self.cols].astype(F32) + self.x_in[here, self.cols].astype(F32)
+            ).astype(BF)
+            return carry
+
+        lax.fori_loop(0, self.near.shape[0] // 32, one, 0)
+        self.a_copy(0).start()
+        self.a_copy(1).start()
+
+    def step_a(self):
+        self.a_copy(0).wait_recv()
+        self.a_copy(1).wait_recv()
+        self.b_out[:, self.cols] = (
+            self.near[self.block(2), self.cols].astype(F32) + self.a_in[1, :, self.cols].astype(F32)
+        ).astype(BF)
+        self.b_copy().start()
+
+    def step_b(self):
+        self.b_copy().wait_recv()
+        return (
+            self.near[self.block(0), self.cols].astype(F32)
+            + self.a_in[0, :, self.cols].astype(F32)
+            + self.b_in[:, self.cols].astype(F32)
+        )
+
+    def finish(self):
+        self.x_copy().wait_send()
+        self.a_copy(0).wait_send()
+        self.a_copy(1).wait_send()
+        self.b_copy().wait_send()
+
+
+PIECES = 4
 
 
 def back_kernel(
@@ -895,8 +1082,11 @@
     ga_all,
     act_turned,
     wqkv,
+    near_in,
+    far,
     down_part,
-    resid,
+    mid,
+    b_down,
     gmid,
     tok,
     slopes,
@@ -905,9 +1095,22 @@
     early,
     result,
     gtok,
+    gup,
+    gdown,
+    gout,
     gwqkv,
     early_sum,
     late_sum,
+    near,
+    x_in,
+    a_in,
+    b_out,
+    b_in,
+    q_near,
+    q_far,
+    q_core,
+    qx_in,
+    q_all,
     dqkv,
     dk_trunk,
     dv_trunk,
@@ -924,21 +1127,33 @@
     n_recv,
     down_recv,
     wg_send,
-    wg_recv,
+    early_mine,
     early_recv,
     late,
     late_recv,
     d_sem,
     e_send,
     e_recv,
+    f_send,
+    f_recv,
     l_send,
     l_recv,
-    w_send,
-    w_recv,
     p_send,
     p_recv,
     ns_sem,
     nr_sem,
+    xs_sem,
+    xr_sem,
+    as_sem,
+    ar_sem,
+    bs_sem,
+    br_sem,
+    qc_send,
+    qc_recv,
+    qx_sem,
+    qz_send,
+    qz_recv,
+    n_local,
 ):
     ns, nz, rows = dims
     s, z, y = lax.axis_index("shard"), lax.axis_index("ctx"), lax.axis_index("tp")
@@ -947,33 +1162,102 @@
     chunk = rows // ROWS_WAVE
     width = tok.shape[1]
     depth = width // count
+    span = nz * depth
     wide = 3 * PAIR
     other = {"tp": 1 - y}
+    total_cols = near.shape[1]
+    step_cols = total_cols // PIECES
+    units = gup.shape[1]
+
+    load = pltpu.make_async_copy(near_in, near, n_local)
+    load.start()
 
     def peer(d):
         index = lax.rem(me + d, count)
-        return index, {"shard": index // nz, "ctx": lax.rem(index, nz)}
+        return index, {"shard": lax.div(index, nz), "ctx": lax.rem(index, nz)}
 
     greet([other] + [peer(d)[1] for d in range(1, count)])
+
+    halves = [
+        Halve(
+            near,
+            far,
+            slice(i * step_cols, (i + 1) * step_cols),
+            dims,
+            depth,
+            (x_in, a_in, b_out, b_in),
+            (xs_sem.at[i], xr_sem.at[i], as_sem.at[i], ar_sem.at[i], bs_sem.at[i], br_sem.at[i]),
+        )
+        for i in range(PIECES)
+    ]
+    def shard_flip(bits):
+        low, high = lax.rem(s, 2), lax.div(s, 2)
+        low = 1 - low if bits & 1 else low
+        high = 1 - high if bits & 2 else high
+        return 2 * high + low
+
+    def q_copy(index):
+        return rcopy(
+            wg_send.at[pl.ds(pl.multiple_of(shard_flip((1, 3)[index]) * span, 128), span), :],
+            q_core.at[index],
+            qc_send.at[index],
+            qc_recv.at[index],
+            {"shard": shard_flip(1)},
+        )
+
+    def qx_copy():
+        return rcopy(q_far, qx_in, qx_sem.at[0], qx_sem.at[1], {"shard": shard_flip(2)})
+
+    def qz_copy(d):
+        to = lax.rem(z + d, nz)
+        return rcopy(
+            q_near.at[pl.ds(pl.multiple_of(to * depth, depth), depth), :],
+            q_all.at[z],
+            qz_send.at[d - 1],
+            qz_recv.at[d - 1],
+            {"ctx": to},
+        )
+
+    def q_spread():
+        qx_copy().wait_recv()
+        q_near[...] = (q_near[...].astype(F32) + qx_in[...].astype(F32)).astype(BF)
+        for d in range(1, nz):
+            qz_copy(d).start()
+        q_all[z] = q_near[pl.ds(pl.multiple_of(z * depth, depth), depth), :]
 
     def down_copy():
         return rcopy(down_part, down_recv, d_sem.at[0], d_sem.at[1], other)
 
+    owners = width // 128
+
+    def owner_cols(index):
+        return pl.ds(pl.multiple_of(index * 128, 128), 128)
+
     def early_copy(d):
-        return rcopy(early, early_recv.at[me], e_send.at[d - 1], e_recv.at[d - 1], peer(d)[1])
+        index, device = peer(d)
+        return index, rcopy(
+            early_mine.at[:, owner_cols(lax.rem(index, owners))],
+            early_recv.at[me],
+            e_send.at[d - 1],
+            e_recv.at[d - 1],
+            device,
+        )
+
+    def spread_copy(d):
+        cols = owner_cols(lax.rem(me, owners))
+        return rcopy(
+            early_sum.at[:, cols], early_sum.at[:, cols], f_send.at[d - 1], f_recv.at[d - 1], peer(d)[1]
+        )
+
+    def spread_arrival(d):
+        index = lax.rem(me + count - d, count)
+        cols = owner_cols(lax.rem(index, owners))
+        return index, rcopy(
+            early_sum.at[:, cols], early_sum.at[:, cols], f_send.at[d - 1], f_recv.at[d - 1], other
+        )
 
     def late_copy(d):
         return rcopy(late, late_recv.at[me], l_send.at[d - 1], l_recv.at[d - 1], peer(d)[1])
-
-    def wg_copy(d):
-        index, device = peer(d)
-        return rcopy(
-            wg_send.at[pl.ds(pl.multiple_of(index * depth, depth), depth), :],
-            wg_recv.at[me],
-            w_send.at[d - 1],
-            w_recv.at[d - 1],
-            device,
-        )
 
     def over_peers(act):
         def one(d, carry):
@@ -982,9 +1266,9 @@
 
         lax.fori_loop(1, count, one, 0)
 
+    for half in halves:
+        half.x_copy().start()
     down_copy().start()
-    over_peers(lambda d: early_copy(d).start())
-    early_recv[me] = early[...]
 
     fill_labels(info_all, rows // BRANCH, labels, parents)
     fill_trunk_keys(key, keys_aug)
@@ -1059,27 +1343,30 @@
 
     lax.fori_loop(0, SLOTS, gather_up, 0)
 
-    def piece_copy(to):
+    def piece_copy(to, i):
         return rcopy(
-            dqkv.at[pl.ds(to * rows, rows), :],
-            dq_all.at[:, pl.ds(pl.multiple_of(z * wide, 128), wide)],
-            p_send.at[to],
-            p_recv.at[z],
+            dqkv.at[to * rows + i * chunk : to * rows + (i + 1) * chunk, :],
+            dq_all.at[i * chunk : (i + 1) * chunk, pl.ds(pl.multiple_of(z * wide, 128), wide)],
+            p_send.at[to, i],
+            p_recv.at[z, i],
             {"ctx": to},
         )
 
-    def send_piece(to):
-        @pl.when(z != to)
-        def _():
-            piece_copy(to).start()
-
-        @pl.when(z == to)
-        def _():
-            dq_all[:, pl.ds(pl.multiple_of(z * wide, 128), wide)] = dqkv[to * rows : (to + 1) * rows, :]
-
-    for to in range(nz):
-        if to * rows >= TRUNK:
-            send_piece(to)
+    def send_pieces(targets):
+        for i in range(ROWS_WAVE):
+            for to in targets:
+
+                @pl.when(z != to)
+                def _():
+                    piece_copy(to, i).start()
+
+        for to in targets:
+
+            @pl.when(z == to)
+            def _():
+                dq_all[:, pl.ds(pl.multiple_of(z * wide, 128), wide)] = dqkv[to * rows : (to + 1) * rows, :]
+
+    send_pieces([to for to in range(nz) if to * rows >= TRUNK])
 
     wave_rows = TRUNK // 4
     wave_mask = causal(wave_rows)
@@ -1106,9 +1393,7 @@
         dqkv[lo:hi, 0:PAIR] = (unstack_turned(turned, wave_rows) * HD ** (-0.5)).astype(BF)
     dqkv[0:TRUNK, PAIR : 2 * PAIR] = dk_trunk[...].astype(BF)
     dqkv[0:TRUNK, 2 * PAIR :] = dv_trunk[...].astype(BF)
-    for to in range(nz):
-        if to * rows < TRUNK:
-            send_piece(to)
+    send_pieces([to for to in range(nz) if to * rows < TRUNK])
 
     def weight(block, carry):
         here = pl.ds(pl.multiple_of(block * 128, 128), 128)
@@ -1116,28 +1401,27 @@
         return carry
 
     lax.fori_loop(0, width // 128, weight, 0)
-    over_peers(lambda d: wg_copy(d).start())
-    wg_recv[me] = wg_send[pl.ds(pl.multiple_of(me * depth, depth), depth), :]
-
-    late[...] = jnp.zeros(late.shape, F32)
-    late[2:3, pl.ds(pl.multiple_of(z * PAIR, 128), PAIR)] = jnp.sum(
+    q_copy(0).start()
+    q_copy(1).start()
+
+    early_mine[...] = early[...]
+    early_mine[6:7, pl.ds(pl.multiple_of(z * PAIR, 128), PAIR)] = jnp.sum(
         dqkv[:, 0:PAIR].astype(F32), axis=0, keepdims=True
     )
-    late[2:3, pl.ds(pl.multiple_of((nz + z) * PAIR, 128), PAIR)] = jnp.sum(
+    early_mine[6:7, pl.ds(pl.multiple_of((nz + z) * PAIR, 128), PAIR)] = jnp.sum(
         dqkv[:, 2 * PAIR :].astype(F32), axis=0, keepdims=True
     )
 
-    for owner in range(nz):
-
-        @pl.when(z != owner)
+    def early_send(d):
+        index, copy = early_copy(d)
+
+        @pl.when(index < owners)
         def _():
-            rcopy(
-                dqkv.at[0:rows, :],
-                dq_all.at[:, owner * wide : (owner + 1) * wide],
-                p_send.at[owner],
-                p_recv.at[owner],
-                {"ctx": owner},
-            ).wait_recv()
+            copy.start()
+
+    over_peers(early_send)
+    early_recv[me] = early_mine[:, owner_cols(lax.rem(me, owners))]
+    load.wait()
 
     def at(i):
         return pl.ds(pl.multiple_of(i * chunk, 32), chunk)
@@ -1145,28 +1429,28 @@
     def n_copy(i):
         return rcopy(n_send.at[at(i), :], n_recv.at[at(i), :], ns_sem.at[i], nr_sem.at[i], other)
 
-    def first(i, carry):
+    def core_join():
+        for index in range(2):
+            q_copy(index).wait_recv()
+            mine = pl.ds(pl.multiple_of(shard_flip((0, 2)[index]) * span, 128), span)
+            (q_near, q_far)[index][...] = (wg_send[mine, :].astype(F32) + q_core[index].astype(F32)).astype(BF)
+        qx_copy().start()
+
+    def first(i):
+        for owner in range(nz):
+
+            @pl.when(z != owner)
+            def _():
+                rcopy(
+                    dqkv.at[0:chunk, :],
+                    dq_all.at[i * chunk : (i + 1) * chunk, owner * wide : (owner + 1) * wide],
+                    p_send.at[owner, i],
+                    p_recv.at[owner, i],
+                    {"ctx": owner},
+                ).wait_recv()
+
         n_send[at(i), :] = nt(dq_all[at(i), :], wqkv[...]).astype(BF)
         n_copy(i).start()
-        return carry
-
-    lax.fori_loop(0, ROWS_WAVE, first, 0)
-
-    down_copy().wait_recv()
-
-    def output(i, carry):
-        here = at(i)
-        result[here, :] = (
-            resid[here, :] + (down_part[here, :].astype(F32) + down_recv[here, :].astype(F32))
-        ).astype(BF)
-        return carry
-
-    lax.fori_loop(0, ROWS_WAVE, output, 0)
-    over_peers(lambda d: early_copy(d).wait_recv())
-    total = early_recv[0]
-    for index in range(1, count):
-        total = total + early_recv[index]
-    early_sum[...] = total
 
     def second(i, carry):
         n_copy(i).wait_recv()
@@ -1178,18 +1462,72 @@
         late[1:2, :] += jnp.sum(grad, axis=0, keepdims=True)
         return carry
 
+    def output(i, carry):
+        here = at(i)
+        result[here, :] = (
+            mid[here, :] + b_down[...] + (down_part[here, :].astype(F32) + down_recv[here, :].astype(F32))
+        ).astype(BF)
+        return carry
+
+    late[...] = jnp.zeros(late.shape, F32)
+    halves[0].step_x()
+    core_join()
+    first(0)
+    halves[1].step_x()
+    first(1)
+    q_spread()
+
+    @pl.when(me < owners)
+    def _():
+        over_peers(lambda d: early_copy(d)[1].wait_recv())
+        total = early_recv[0]
+        for index in range(1, count):
+            total = total + early_recv[index]
+        early_sum[:, owner_cols(lax.rem(me, owners))] = total
+        over_peers(lambda d: spread_copy(d).start())
+
+    halves[2].step_x()
+    first(2)
+    halves[0].step_a()
+    halves[3].step_x()
+    first(3)
+    down_copy().wait_recv()
+    lax.fori_loop(0, ROWS_WAVE, output, 0)
+    halves[1].step_a()
     lax.fori_loop(0, ROWS_WAVE, second, 0)
     over_peers(lambda d: late_copy(d).start())
     late_recv[me] = late[...]
-
-    over_peers(lambda d: wg_copy(d).wait_recv())
+    halves[2].step_a()
+    halves[3].step_a()
+
+    for d in range(1, nz):
+        qz_copy(d).wait_recv()
     for owner in range(nz):
-        block = wg_recv[owner].astype(F32)
-        for source in range(1, ns):
-            block = block + wg_recv[source * nz + owner].astype(F32)
         for part in range(3):
-            gwqkv[part, :, owner * PAIR : (owner + 1) * PAIR] = block[:, part * PAIR : (part + 1) * PAIR]
-
+            gwqkv[part, :, owner * PAIR : (owner + 1) * PAIR] = q_all[
+                owner, :, part * PAIR : (part + 1) * PAIR
+            ].astype(F32)
+    bounds = (0, units, 2 * units, total_cols)
+    for i, half in enumerate(halves):
+        block = half.step_b()
+        lo, hi = i * step_cols, (i + 1) * step_cols
+        for target, start_at, end_at in (
+            (gup, bounds[0], bounds[1]),
+            (gdown, bounds[1], bounds[2]),
+            (gout, bounds[2], bounds[3]),
+        ):
+            a, b = max(lo, start_at), min(hi, end_at)
+            if a < b:
+                target[:, a - start_at : b - start_at] = block[:, a - lo : b - lo]
+
+    def early_wait(d):
+        index, copy = spread_arrival(d)
+
+        @pl.when(index < owners)
+        def _():
+            copy.wait_recv()
+
+    over_peers(early_wait)
     over_peers(lambda d: late_copy(d).wait_recv())
     total = late_recv[0]
     for index in range(1, count):
@@ -1197,9 +1535,28 @@
     late_sum[...] = total
 
     down_copy().wait_send()
-    over_peers(lambda d: early_copy(d).wait_send())
+    for half in halves:
+        half.finish()
+    qx_copy().wait_send()
+    for d in range(1, nz):
+        qz_copy(d).wait_send()
+    q_copy(0).wait_send()
+    q_copy(1).wait_send()
+
+    def early_drain(d):
+        index, copy = early_copy(d)
+
+        @pl.when(index < owners)
+        def _():
+            copy.wait_send()
+
+    over_peers(early_drain)
+
+    @pl.when(me < owners)
+    def _():
+        over_peers(lambda d: spread_copy(d).wait_send())
+
     over_peers(lambda d: late_copy(d).wait_send())
-    over_peers(lambda d: wg_copy(d).wait_send())
 
     def finish(i, carry):
         n_copy(i).wait_send()
@@ -1210,28 +1567,44 @@
 
         @pl.when(z != owner)
         def _():
-            piece_copy(owner).wait_send()
-
-
-def run_back(dims, *inputs):
+            for i in range(ROWS_WAVE):
+                piece_copy(owner, i).wait_send()
+
+
+def run_back(dims, units, *inputs):
     ns, nz, rows = dims
-    width = inputs[12].shape[1]
+    width = inputs[15].shape[1]
+    span, total = inputs[9].shape
     count = ns * nz
     depth = width // count
     wide = 3 * PAIR
+    anywhere = pl.BlockSpec(memory_space=pl.ANY)
     return pl.pallas_call(
         partial(back_kernel, dims),
         name="tree_backward",
         out_shape=(
             shape((rows, width), BF),
             shape((rows, width), F32),
+            shape((depth, units), F32),
+            shape((depth, units), F32),
+            shape((depth, total - 2 * units), F32),
             shape((3, depth, nz * PAIR), F32),
             shape((8, width), F32),
-            shape((8, width), F32),
+            shape((2, width), F32),
         ),
-        in_specs=[vmem()] * 17,
-        out_specs=[vmem()] * 5,
+        in_specs=[vmem()] * 9 + [anywhere] * 2 + [vmem()] * 9,
+        out_specs=[vmem()] * 8,
         scratch_shapes=[
+            pltpu.VMEM((span, total), BF),
+            pltpu.VMEM((span, total), BF),
+            pltpu.VMEM((2, depth, total), BF),
+            pltpu.VMEM((depth, total), BF),
+            pltpu.VMEM((depth, total), BF),
+            pltpu.VMEM((span, wide), BF),
+            pltpu.VMEM((span, wide), BF),
+            pltpu.VMEM((2, span, wide), BF),
+            pltpu.VMEM((span, wide), BF),
+            pltpu.VMEM((nz, depth, wide), BF),
             pltpu.VMEM((TREE, wide), BF),
             pltpu.VMEM((TRUNK, PAIR), F32),
             pltpu.VMEM((TRUNK, PAIR), F32),
@@ -1248,10 +1621,10 @@
             pltpu.VMEM((rows, width), BF),
             pltpu.VMEM((rows, width), BF),
             pltpu.VMEM((width, wide), BF),
-            pltpu.VMEM((count, depth, wide), BF),
-            pltpu.VMEM((count, 8, width), F32),
             pltpu.VMEM((8, width), F32),
-            pltpu.VMEM((count, 8, width), F32),
+            pltpu.VMEM((count, 8, 128), F32),
+            pltpu.VMEM((2, width), F32),
+            pltpu.VMEM((count, 2, width), F32),
             dma(2),
             dma(count - 1),
             dma(count - 1),
@@ -1259,10 +1632,22 @@
             dma(count - 1),
             dma(count - 1),
             dma(count - 1),
-            dma(nz),
-            dma(nz),
+            dma(nz, ROWS_WAVE),
+            dma(nz, ROWS_WAVE),
             dma(ROWS_WAVE),
             dma(ROWS_WAVE),
+            dma(PIECES),
+            dma(PIECES),
+            dma(PIECES, 2),
+            dma(PIECES, 2),
+            dma(PIECES),
+            dma(PIECES),
+            dma(2),
+            dma(2),
+            dma(2),
+            dma(nz - 1),
+            dma(nz - 1),
+            pltpu.SemaphoreType.DMA,
         ],
         compiler_params=pltpu.CompilerParams(
             collective_id=2, has_side_effects=True, vmem_limit_bytes=60 << 20
@@ -1277,7 +1662,6 @@
     rows = tokens.shape[0]
     ns, nz, ntp = lax.axis_size("shard"), lax.axis_size("ctx"), lax.axis_size("tp")
     dims = (ns, nz, rows)
-    both = ("shard", "ctx")
 
     labels = seg_ids.reshape(rows // BRANCH, BRANCH)[:, 0]
     match = labels[:, None] == jnp.arange(parents.shape[0], dtype=jnp.int32)[None, :]
@@ -1297,27 +1681,24 @@
     wfull, wq, act_turned, query, key, value, out_heads, lse, info_all, att = run_tree(
         dims, tokens, w_up, w_out.T, w_down.T, w_qkv, info, b_qv, slopes, ln_gain, ln_bias
     )
-    wqkv, gsum, ga_all, down_part, resid, gmid, sums = run_feed(
-        dims, tokens, cotangent, att, wfull, wq, b_out[None, :], b_up[None, :], b_down[None, :], ln_gain, ln_bias
-    )
-    grads = lax.psum_scatter(gsum, both, scatter_dimension=0, tiled=True)
-    result, grad_tokens, grad_w_qkv, early, late = run_back(
-        dims, query, key, value, out_heads, lse, info_all, ga_all, act_turned, wqkv, down_part, resid, gmid,
-        tokens, slopes, ln_gain, ln_bias, sums,
-    )
     units, inner = b_up.shape[0], w_out.shape[0]
-    grads = grads.astype(F32)
-    width = tokens.shape[1]
+    wqkv, near, far, ga_all, down_part, mid, gmid, sums = run_feed(
+        dims, tokens, cotangent, att, wfull, wq, b_out[None, :], b_up[None, :], ln_gain, ln_bias
+    )
+    result, grad_tokens, gup, gdown, gout, grad_w_qkv, early, late = run_back(
+        dims, units, query, key, value, out_heads, lse, info_all, ga_all, act_turned, wqkv, near, far, down_part,
+        mid, b_down[None, :], gmid, tokens, slopes, ln_gain, ln_bias, sums,
+    )
     return (
         result,
         grad_tokens,
         grad_w_qkv,
-        late[2].reshape(2, nz * PAIR),
-        grads[:, units : units + inner].T,
+        early[6].reshape(2, nz * PAIR),
+        gout.T,
         early[2],
-        grads[:, 0:units],
+        gup,
         early[0:2].reshape(units),
-        grads[:, units + inner :].T,
+        gdown.T,
         early[3],
         jnp.stack([late[0], early[4]]),
         jnp.stack([late[1], early[5]]),

time: 426 us -> 348 us (0.82)
  Pallas kernels: 381 us -> 318 us
  between operations: 14.1 us -> 0.75 us
    pallas_call x1, Pallas kernels: 173 us -> 117 us  [run_back(): pl.pallas_call(partial(back_kernel, dims), name='tree_backward', out_shap...]
    pallas_call x1, Pallas kernels: 90.9 us -> 61.7 us  [run_feed(): pl.pallas_call(partial(feed_kernel, dims), name='feed_both', out_shape=(s...]
    pallas_call x1, Pallas kernels: 117 us -> 139 us  [run_tree(): pl.pallas_call(partial(tree_kernel, dims), name='tree_forward', out_shape...]
    unnamed x47 -> x50, local copies, waits for them, and re-layouts: 18 us -> 20.5 us
  transfers between devices with their start and end apart: 1 -> 0, of which waited for: 0 -> 0; matrix products, arithmetic and copies ran while one was open for 1% -> 0% of each run, Pallas kernels for 41% -> 0%
where the time goes in v3:
time: 348 us; the launch traced here: 345 us
  Pallas kernels  318 us (91%)
  local copies, waits for them, and re-layouts  24.5 us (7%)
    pallas_call x1, Pallas kernels, run_tree(): pl.pallas_call(partial(tree_kernel, dims), name='tree_forward', out_shape...  139 us
    pallas_call x1, Pallas kernels, run_back(): pl.pallas_call(partial(back_kernel, dims), name='tree_backward', out_shap...  117 us
    pallas_call x1, Pallas kernels, run_feed(): pl.pallas_call(partial(feed_kernel, dims), name='feed_both', out_shape=(s...  61.7 us
    unnamed x50, local copies, waits for them, and re-layouts  20.5 us

profile of v3, /device:TPU:12, one launch (start us, length us, event | category | flops | bytes accessed | tf_op | source)
XLA Modules:
  0.0 345.3 jit_solution(1454312788419687722)
XLA Ops:
  0.6 0.8 slice_reduce_fusion.1
  1.5 0.8 select_reduce_fusion
  2.3 0.1 fusion.2
  2.4 0.1 stack.6
  2.5 0.0 copy-start
  2.5 0.1 broadcast_in_dim.31.info
  2.6 0.0 copy-start.1
  2.6 0.9 copy-done.1
  3.5 0.0 copy-start.2
  3.5 0.9 copy-done.2
  4.5 0.0 copy-start.3
  4.5 0.9 copy-done.3
  5.4 0.8 copy-done.4
  6.3 0.7 copy-done.5
  7.0 0.7 copy-done.6
  7.7 0.7 copy-done.7
  8.3 138.7 %tree_forward.1 = (bf16[1024,5120]{1,0:T(8,128)(2,1)}, bf16[64,1536]{1,0:T(8,128)(2,1)S(1)}, bf16[1024,2560]{1,0:T(8,128)(2,1)}, bf16[2560,128]{1,0:T(8,128)(2,1...) custom-call(bf16[640,1024]{1,0:T(8,128)(2,1)} %tok.5, ...), custom_call_target="tpu_custom_call" | custom-call | flops 40000000000 | bytes 20000000 | tf_op jit(solution)/shard_map/tree_forward/pallas_call | solution.py:679
  147.1 0.0 copy-done
  147.1 0.0 copy-start.8
  147.1 1.0 copy-done.8
  148.2 0.8 copy-done.9
  149.0 0.8 copy-done.10
  149.9 0.8 copy-done.11
  150.7 0.8 copy-done.12
  151.5 0.7 copy-done.13
  152.2 0.6 copy-done.14
  152.8 0.6 copy-done.15
  153.4 61.7 %feed_both.1 = (bf16[1024,1536]{1,0:T(8,128)(2,1)}, bf16[256,4608]{1,0:T(8,128)(2,1)}, bf16[256,4608]{1,0:T(8,128)(2,1)}, bf16[2560,128]{1,0:T(8,128)(2,1)}, bf1...) custom-call(bf16[640,1024]{1,0:T(8,128)(2,1)} %tok.5, ...), custom_call_target="tpu_custom_call" | custom-call | flops 40000000000 | bytes 20000000 | tf_op jit(solution)/shard_map/feed_both/pallas_call | solution.py:952
  215.1 117.4 %tree_backward.1 = (bf16[640,1024]{1,0:T(8,128)(2,1)}, f32[640,1024]{1,0:T(8,128)}, f32[64,2048]{1,0:T(8,128)}, f32[64,2048]{1,0:T(8,128)}, f32[64,512]{1,0:T(8,...) custom-call(bf16[2560,128]{1,0:T(8,128)(2,1)} %copy-done.9, bf16[2560,128]{1,0:T(8,128)(2,1)} %copy-done.10, ...), custom_call_target="tpu_custom_call" | custom-call | flops 40000000000 | bytes 20000000 | tf_op jit(solution)/shard_map/tree_backward/pallas_call | solution.py:1582
  332.5 0.0 copy-start.16
  332.6 0.9 slice_bitcast_fusion
  333.5 1.6 fusion.4
  335.1 0.6 copy.28
  335.7 0.6 reshape_squeeze.3
  336.3 0.8 fusion.5
  337.1 0.6 pad_maximum_fusion.1
  337.7 0.6 pad_maximum_fusion
  338.3 2.5 copy.35
  340.8 0.0 copy-done.16
  340.8 1.5 copy.36
  342.3 0.0 copy-done.19
  342.3 0.7 copy.37
  343.0 0.0 copy-done.20
  343.0 0.7 copy.38
  343.7 0.0 copy-done.18
  343.7 0.8 copy.39
  344.5 0.0 copy-done.17
  344.5 0.8 copy.40
  (19 shorter events, 0.1 us)
Async XLA Ops:
  2.5 144.6 %copy-start = (f32[2,128]{1,0:T(2,128)}, f32[2,128]{1,0:T(2,128)S(1)}, u32[]{:S(2)}) copy-start(f32[2,128]{1,0:T(2,128)S(1)} %pad.13.slopes) | copy-start | bytes 3076
  2.6 1.0 copy-start.1
  3.5 0.9 copy-start.2
  4.5 0.9 copy-start.3
  5.4 0.8 copy-start.4
  6.3 0.7 copy-start.5
  7.0 0.7 copy-start.6
  7.7 0.7 copy-start.7
  147.1 1.1 copy-start.8
  148.2 0.8 copy-start.9
  149.0 0.8 copy-start.10
  149.9 0.8 copy-start.11
  150.7 0.8 copy-start.12
  151.5 0.7 copy-start.13
  152.2 0.6 copy-start.14
  152.8 0.6 copy-start.15
  332.5 8.2 %copy-start.16 = (f32[640,1024]{1,0:T(8,128)S(1)}, f32[640,1024]{1,0:T(8,128)}, u32[]{:S(2)}) copy-start(f32[640,1024]{1,0:T(8,128)} %get-tuple-element.86) | copy-start | bytes 7864324
  340.8 1.5 copy-start.19
  340.8 2.3 copy-start.20
  340.8 2.9 copy-start.18
  342.3 2.2 copy-start.17

commit v4 on v3

--- a/solution.py
+++ b/solution.py
@@ -23,7 +23,11 @@
 BF = jnp.bfloat16
 F32 = jnp.float32
 ROWS_WAVE = 4
-SPREAD_AT = ((1, 3), (2,), ())
+FRONT_LIMIT = 62 << 20
+BLOCK = 512
+CURVE = 0.044715
+ROOT = 0.7978845608028654
+SUBS = 2
 
 
 def nt(left, right):
@@ -159,13 +163,13 @@
             high = 1 - high
         return 2 * high + low
 
+    def source(self, d):
+        return lax.rem(self.z + self.nz - d, self.nz)
+
     def z_copy(self, d):
         ref = self.rows(self.s, self.z)
         return rcopy(ref, ref, self.zs.at[d - 1], self.zr.at[d - 1], {"ctx": lax.rem(self.z + d, self.nz)})
 
-    def source(self, d):
-        return lax.rem(self.z + self.nz - d, self.nz)
-
     def x_copy(self, d):
         ref = self.rows(self.s, self.source(d))
         return rcopy(ref, ref, self.xs.at[d], self.xr.at[d], {"shard": self.flip(2)})
@@ -174,8 +178,9 @@
         ref = self.rows(self.flip(2) if far else self.s, self.source(d))
         return rcopy(ref, ref, self.cs.at[far, d], self.cr.at[far, d], {"shard": self.flip(1)})
 
-    def z_start(self, d):
-        self.z_copy(d).start()
+    def z_start(self):
+        for d in (1, 3, 2):
+            self.z_copy(d).start()
 
     def own(self):
         self.x_copy(0).start()
@@ -226,20 +231,21 @@
     return pltpu.SemaphoreType.DMA(dims)
 
 
-def tree_kernel(
+def front_kernel(
     dims,
     tok,
     w_up,
     w_out,
     w_down,
+    cot_in,
     wq3,
     info,
     bias_qv,
     slopes,
     gain,
     shift,
-    wfull,
-    wq,
+    b_out,
+    b_up,
     act_turned,
     query,
     key,
@@ -247,6 +253,15 @@
     out_heads,
     lse,
     info_all,
+    wqkv,
+    core_in,
+    ga_all,
+    down_part,
+    mid,
+    gmid,
+    sums,
+    wfull,
+    wq,
     att,
     tree,
     wcat,
@@ -254,6 +269,14 @@
     values_turned,
     labels,
     parents,
+    cot,
+    far,
+    act,
+    gbranch,
+    g_send,
+    g_recv,
+    ga_send,
+    bup_acc,
     info_send,
     info_recv,
     wz_send,
@@ -271,12 +294,18 @@
     b_recv,
     t_send,
     t_recv,
+    gs_sem,
+    gr_sem,
+    as_sem,
+    ar_sem,
+    cs_sem,
+    cr_sem,
     *spread,
 ):
     ns, nz, rows = dims
     s, z, y = lax.axis_index("shard"), lax.axis_index("ctx"), lax.axis_index("tp")
     half = rows // 2
-    sub = half // 2
+    sub = half // SUBS
     depth = wq.shape[0]
     wide = 3 * PAIR
     my_rows = pl.ds(pl.multiple_of((s * nz + z) * depth, depth), depth)
@@ -288,6 +317,8 @@
         pltpu.make_async_copy(w_down, wfull.at[my_rows, units : 2 * units], local_sem.at[2]),
         pltpu.make_async_copy(w_out, wfull.at[my_rows, pl.ds(own_cols, inner)], local_sem.at[3]),
     ]
+    given_load = pltpu.make_async_copy(cot_in, cot, local_sem.at[4])
+    given_load.start()
     for one in starts:
         one.start()
     for to in range(nz):
@@ -300,8 +331,10 @@
         + [{"shard": lax.rem(s + d, ns)} for d in range(1, ns)]
         + [{"tp": 1 - y}]
     )
-    weights = Spread(wfull, dims, depth, slice(0, 2 * units), spread[:6])
-    outer = Spread(wfull, dims, depth, pl.ds(own_cols, inner), spread[6:])
+    ups = Spread(wfull, dims, depth, slice(0, units), spread[:6])
+    downs = Spread(wfull, dims, depth, slice(units, 2 * units), spread[6:12])
+    weights = Spread(wqkv, dims, depth, slice(None), spread[18:])
+    outer = Spread(wfull, dims, depth, pl.ds(own_cols, inner), spread[12:18])
 
     def info_copy(d):
         return rcopy(
@@ -329,6 +362,7 @@
             {"shard": lax.rem(s + d, ns)},
         )
 
+    wqkv[my_rows, :] = wq[...]
     for d in range(1, nz):
         wz_copy(d).start()
     for d in range(1, nz):
@@ -377,7 +411,7 @@
         return block, here, onward
 
     def forward(k, first):
-        for part in range(2):
+        for part in range(SUBS):
             for direction in range(2):
                 _, here, onward = place(direction, k)
                 if not first:
@@ -397,8 +431,9 @@
                         y_copy(direction, k, part).start()
 
     forward(0, True)
-    weights.own()
     outer.own()
+    ups.own()
+    downs.own()
     for d in range(1, nz):
         wz_copy(d).wait_recv()
     for d in range(1, ns):
@@ -433,7 +468,7 @@
         lax.fori_loop(0, 2, side, 0)
 
     def shared(k):
-        for part in range(2):
+        for part in range(SUBS):
             for direction in range(2):
                 _, here, _ = place(direction, k)
 
@@ -442,10 +477,6 @@
                     y_arrival(direction, k, part).wait_recv()
 
     forward(1, False)
-    for d in range(1, nz):
-        outer.z_start(d)
-    for d in SPREAD_AT[0]:
-        weights.z_start(d)
     for d in range(1, ns):
         ws_copy(d).wait_recv()
     project(0)
@@ -453,29 +484,22 @@
     def wave(k, carry):
         forward(k, False)
 
-        @pl.when(k == 2)
+        @pl.when(k == nz - 2)
         def _():
-            for d in SPREAD_AT[1]:
-                weights.z_start(d)
-
-        @pl.when(k == 3)
-        def _():
-            for d in SPREAD_AT[2]:
-                weights.z_start(d)
+            outer.z_start()
+            ups.z_start()
 
         shared(k - 1)
         project(k - 1)
         return carry
 
     lax.fori_loop(2, nz, wave, 0)
-    for d in range(1, nz):
+    for d in (1, 3, 2):
         outer.z_done(d)
-    for d in SPREAD_AT[0]:
-        weights.z_done(d)
-    for d in range(nz):
-        outer.x_done(d)
     shared(nz - 1)
     project(nz - 1)
+    for d in (0, 1, 3, 2):
+        outer.x_done(d)
 
     for d in range(1, nz):
         info_copy(d).wait_recv()
@@ -539,7 +563,6 @@
             pass_on(z).start()
 
     tile_mask = causal(BRANCH)
-    owners = [((owner + 1) * rows - TRUNK) // BRANCH - 1 for owner in range(nz)]
 
     def segment(slot, carry):
         here = pl.ds(pl.multiple_of(TRUNK + slot * BRANCH, 128), BRANCH)
@@ -572,21 +595,12 @@
         turned = turned / total
         out_heads[here, :] = unstack_turned(turned, BRANCH).astype(BF)
         lse[pl.ds(4 + slot, 1), 0 : 2 * BRANCH] = top + jnp.log2(total)
-        for owner in range(nz):
-            if owners[owner] >= 0 and owner * rows >= TRUNK:
-
-                @pl.when(slot == owners[owner])
-                def _():
-                    send_out(owner)
-
         return carry
-
-    lax.fori_loop(0, SLOTS, segment, 0)
 
     wave_rows = TRUNK // 4
     wave_mask = causal(wave_rows)
-    sent = 0
-    for tile in range(4):
+
+    def trunk_tile(tile):
         lo, hi = tile * wave_rows, (tile + 1) * wave_rows
         asked = jnp.concatenate(
             [stack_heads(query[lo:hi, :]), query_features(slopes, wave_rows)], axis=1
@@ -606,12 +620,24 @@
         turned = turned / total
         out_heads[lo:hi, :] = unstack_turned(turned, wave_rows).astype(BF)
         lse[tile : tile + 1, :] = top + jnp.log2(total)
-        while sent < nz and sent * rows < TRUNK and (sent + 1) * rows <= (hi if hi < TRUNK else TREE):
-            send_out(sent)
-            sent += 1
-
-    for d in SPREAD_AT[1] + SPREAD_AT[2]:
-        weights.z_done(d)
+
+    def segments(lo, hi):
+        lax.fori_loop((lo - TRUNK) // BRANCH, (hi - TRUNK) // BRANCH, segment, 0)
+
+    segments(2 * rows, 3 * rows)
+    send_out(2)
+    for tile in range(3):
+        trunk_tile(tile)
+    send_out(0)
+    ups.z_done(1)
+    ups.z_done(3)
+    segments(3 * rows, 4 * rows)
+    send_out(3)
+    trunk_tile(3)
+    segments(TRUNK, 2 * rows)
+    send_out(1)
+    downs.z_start()
+    ups.z_done(2)
     plane_arrival().wait_recv()
     core_copy().start()
     for owner in range(nz):
@@ -627,166 +653,25 @@
             ).wait_recv()
             pass_on(owner).start()
 
-    for d in (0,) + SPREAD_AT[0] + SPREAD_AT[1] + SPREAD_AT[2]:
-        weights.x_done(d)
+    mid[...] = tree[pl.ds(pl.multiple_of(z * rows, 128), rows), :].astype(F32) + b_out[...]
+    for d in (0, 1, 3, 2):
+        ups.x_done(d)
+    for d in (1, 3):
+        downs.z_done(d)
+    given_load.wait()
     for owner in range(nz):
         ref = att.at[:, att_cols(1 - y, owner)]
         rcopy(ref, ref, b_send.at[owner], b_recv.at[owner], {"tp": 1 - y}).wait_recv()
     core_arrival().wait_recv()
-    weights.all_here()
-    plane_copy().wait_send()
-    core_copy().wait_send()
-    for owner in range(nz):
-        pass_on(owner).wait_send()
-
-    for owner in range(nz):
-
-        @pl.when(z != owner)
-        def _():
-            att_copy(owner).wait_send()
-
-    weights.finish()
-    outer.finish()
-    for d in range(1, nz):
-        info_copy(d).wait_send()
-        wz_copy(d).wait_send()
-    for d in range(1, ns):
-        ws_copy(d).wait_send()
-
-    def drain(k, carry):
-        for part in range(2):
-            for direction in range(2):
-                _, here, onward = place(direction, k)
-
-                @pl.when(onward & (k < nz - 1))
-                def _():
-                    z_copy(direction, k, part).wait_send()
-
-                @pl.when(here & (k > 0))
-                def _():
-                    y_copy(direction, k, part).wait_send()
-
-        return carry
-
-    lax.fori_loop(0, nz, drain, 0)
-
-
-def run_tree(dims, tok, w_up, w_out, w_down, wq3, info, bias_qv, slopes, gain, shift):
-    ns, nz, rows = dims
-    width = tok.shape[1]
-    depth = wq3.shape[1]
-    total = w_up.shape[1] + 2 * w_out.shape[1] + w_down.shape[1]
-    return pl.pallas_call(
-        partial(tree_kernel, dims),
-        name="tree_forward",
-        out_shape=(
-            shape((width, total), BF),
-            shape((depth, nz * 3 * PAIR), BF),
-            shape((width, TREE), BF),
-            shape((TREE, PAIR), BF),
-            shape((TREE, PAIR), BF),
-            shape((TREE, PAIR), BF),
-            shape((TREE, PAIR), BF),
-            shape((16, 512), F32),
-            shape((nz, 16, 128), F32),
-            shape((rows, 2 * nz * PAIR), BF),
-        ),
-        in_specs=[pl.BlockSpec(memory_space=pl.ANY)] * 4 + [vmem()] * 6,
-        out_specs=[vmem()] * 10,
-        scratch_shapes=[
-            pltpu.VMEM((TREE, width), BF),
-            pltpu.VMEM((width, 3 * PAIR), BF),
-            pltpu.VMEM((TRUNK, 2 * PAIR), BF),
-            pltpu.VMEM((PAIR, TRUNK), BF),
-            pltpu.VMEM((16, 128), F32),
-            pltpu.VMEM((16, 128), F32),
-            dma(nz - 1),
-            dma(nz - 1),
-            dma(nz - 1),
-            dma(nz - 1),
-            dma(ns - 1),
-            dma(ns - 1),
-            dma(2, nz, 2),
-            dma(2, nz, 2),
-            dma(2, nz, 2),
-            dma(2, nz, 2),
-            dma(nz),
-            dma(nz),
-            dma(4),
-            dma(nz),
-            dma(nz),
-            dma(2),
-            dma(2),
-            *spread_sems(nz),
-            *spread_sems(nz),
-        ],
-        compiler_params=pltpu.CompilerParams(
-            collective_id=0, has_side_effects=True, vmem_limit_bytes=48 << 20
-        ),
-        cost_estimate=pl.CostEstimate(flops=40_000_000_000, bytes_accessed=20_000_000, transcendentals=0),
-    )(tok, w_up, w_out, w_down, wq3, info, bias_qv, slopes, gain, shift)
-
-
-BLOCK = 512
-CURVE = 0.044715
-ROOT = 0.7978845608028654
-
-
-def feed_kernel(
-    dims,
-    tok,
-    cot,
-    att,
-    wa,
-    wq,
-    b_out,
-    b_up,
-    gain,
-    shift,
-    wqkv,
-    near,
-    far,
-    ga_all,
-    down_part,
-    mid,
-    gmid,
-    sums,
-    gsum,
-    core_in,
-    act,
-    hidden,
-    gup,
-    gbranch,
-    g_send,
-    g_recv,
-    ga_send,
-    bup_acc,
-    gs_sem,
-    gr_sem,
-    as_sem,
-    ar_sem,
-    cs_sem,
-    cr_sem,
-    *spread,
-):
-    ns, nz, rows = dims
-    s, z, y = lax.axis_index("shard"), lax.axis_index("ctx"), lax.axis_index("tp")
+    ups.all_here()
+    other = {"tp": 1 - y}
     chunk = rows // ROWS_WAVE
-    width = tok.shape[1]
-    units = b_up.shape[1]
-    inner = att.shape[1] // 2
-    wd = wa.at[:, units : 2 * units]
-    wo = wa.at[:, 2 * units :]
+    width = act.shape[1]
+    halves = units // width
     own_heads = pl.ds(pl.multiple_of(y * inner, 128), inner)
-    depth = wq.shape[0]
-    weights = Spread(wqkv, dims, depth, slice(None), spread)
-    greet(
-        [{"tp": 1 - y}]
-        + [{"ctx": lax.rem(z + d, nz)} for d in range(1, nz)]
-        + [{"shard": weights.flip(bits)} for bits in (1, 2)]
-    )
-    other = {"tp": 1 - y}
-    wqkv[pl.ds(pl.multiple_of((s * nz + z) * depth, depth), depth), :] = wq[...]
+    own_wide = pl.ds(own_cols, inner)
+    sums[...] = jnp.zeros(sums.shape, F32)
+    bup_acc[...] = jnp.zeros(bup_acc.shape, F32)
 
     def at(i):
         return pl.ds(pl.multiple_of(i * chunk, 32), chunk)
@@ -807,13 +692,10 @@
     span = nz * depth
     parts = ((0, 2 * units), (2 * units, 2 * units + inner))
 
-    def group(bits):
-        return pl.ds(pl.multiple_of(weights.flip(bits) * span, 128), span)
-
     def c_copy(part, index):
         lo, hi = parts[part]
         return rcopy(
-            gsum.at[group((1, 3)[index]), lo:hi],
+            far.at[index, :, lo:hi],
             core_in.at[index, :, lo:hi],
             cs_sem.at[part, index],
             cr_sem.at[part, index],
@@ -822,52 +704,127 @@
 
     sums[...] = jnp.zeros(sums.shape, F32)
     bup_acc[...] = jnp.zeros(bup_acc.shape, F32)
-    weights.own()
-    for d in range(1, nz):
-        weights.z_start(d)
-
-    def stage_b(i, carry):
+    per = width // BLOCK
+
+    def spot(first, i, c):
+        row = (first + lax.div(c, per)) * rows + i * chunk
+        col = lax.rem(c, per) * BLOCK
+        return pl.ds(pl.multiple_of(row, 32), chunk), pl.ds(pl.multiple_of(col, 128), BLOCK)
+
+    def stage_one(i, carry):
         here = at(i)
-        branch = nt(att[here, :], wo[...]) + b_out[...]
-        middle = tok[here, :].astype(F32) + branch
+        middle = mid[here, :] + nt(att[here, :], wfull[:, 2 * units :])
         mid[here, :] = middle
         act[here, :] = norm_rows(middle, gain[1:2, :], shift[1:2, :])[0].astype(BF)
 
         def columns(c, inner_carry):
             cols = pl.ds(pl.multiple_of(c * BLOCK, 128), BLOCK)
-            upper = nn(act[here, :], wa[:, cols]) + b_up[:, cols]
-            slope = nn(cot[here, :], wd[:, cols])
+            upper = nn(act[here, :], wfull[:, cols]) + b_up[:, cols]
             square = upper * upper
             turn = jnp.tanh(ROOT * (upper + CURVE * (square * upper)))
-            hidden[here, cols] = (0.5 * upper * (1.0 + turn)).astype(BF)
+            tree[spot(0, i, c)] = (0.5 * upper * (1.0 + turn)).astype(BF)
             steep = 0.5 * (1.0 + turn) + (0.5 * ROOT) * upper * (1.0 - turn * turn) * (
                 1.0 + (3.0 * CURVE) * square
             )
-            low = (slope * steep).astype(BF)
-            gup[here, cols] = low
+            tree[spot(halves, i, c)] = steep.astype(BF)
+            return inner_carry
+
+        lax.fori_loop(0, units // BLOCK, columns, 0)
+        return carry
+
+    def stage_two(i, carry):
+        here = at(i)
+
+        def columns(c, inner_carry):
+            cols = pl.ds(pl.multiple_of(c * BLOCK, 128), BLOCK)
+            down_cols = pl.ds(pl.multiple_of(units + c * BLOCK, 128), BLOCK)
+            slope = nn(cot[here, :], wfull[:, down_cols])
+            low = (slope * tree[spot(halves, i, c)].astype(F32)).astype(BF)
+            tree[spot(halves, i, c)] = low
             bup_acc[:, cols] += jnp.sum(low.astype(F32), axis=0, keepdims=True)
             return inner_carry
 
         lax.fori_loop(0, units // BLOCK, columns, 0)
-        g_send[here, :] = nt(gup[here, :], wa[:, 0:units]).astype(BF)
+        total = jnp.zeros((chunk, width), F32)
+        for part in range(halves):
+            total = total + nt(
+                tree[spot(halves + part, i, 0)[0], :], wfull[:, part * width : (part + 1) * width]
+            )
+        g_send[here, :] = total.astype(BF)
         g_copy(i).start()
         return carry
 
-    lax.fori_loop(0, ROWS_WAVE, stage_b, 0)
-    for d in range(1, nz):
+    def drain(k, carry):
+        for part in range(SUBS):
+            for direction in range(2):
+                _, here, onward = place(direction, k)
+
+                @pl.when(onward & (k < nz - 1))
+                def _():
+                    z_copy(direction, k, part).wait_send()
+
+                @pl.when(here & (k > 0))
+                def _():
+                    y_copy(direction, k, part).wait_send()
+
+        return carry
+
+    lax.fori_loop(0, nz, drain, 0)
+    lax.fori_loop(0, 2, stage_one, 0)
+    downs.z_done(2)
+    weights.own()
+    weights.z_start()
+    for d in (0, 1, 3, 2):
+        downs.x_done(d)
+    lax.fori_loop(2, ROWS_WAVE, stage_one, 0)
+    downs.all_here()
+    lax.fori_loop(0, ROWS_WAVE, stage_two, 0)
+    for d in (1, 3, 2):
         weights.z_done(d)
 
-    def weight_one(d, carry):
-        cols = pl.ds(pl.multiple_of(d * 128, 128), 128)
-        gsum[cols, 0:units] = nn(act[:, cols].T, gup[...]).astype(BF)
-        gsum[cols, units : 2 * units] = nn(cot[:, cols].T, hidden[...]).astype(BF)
-        return carry
-
-    lax.fori_loop(0, width // 128, weight_one, 0)
-    for index in range(2):
-        c_copy(0, index).start()
-    for d in range(nz):
-        weights.x_done(d)
+    def group_cols(index, block):
+        return pl.ds(pl.multiple_of(weights.flip(index) * span + block * 128, 128), 128)
+
+    def products(cols):
+        turned_act, turned_cot = act[:, cols].T, cot[:, cols].T
+        for part in range(halves):
+            lo = part * width
+            yield lo, nn(turned_act, tree[(halves + part) * rows : (halves + part + 1) * rows, :])
+            yield units + lo, nn(turned_cot, tree[part * rows : (part + 1) * rows, :])
+
+    def each_block(act_on):
+        for index in range(2):
+
+            def one(block, carry):
+                act_on(index, block)
+                return carry
+
+            lax.fori_loop(0, span // 128, one, 0)
+
+    def far_one(index, block):
+        target = pl.ds(pl.multiple_of(block * 128, 128), 128)
+        for lo, value_block in products(group_cols((1, 3)[index], block)):
+            far[index, target, lo : lo + width] = value_block.astype(BF)
+
+    def near_one(index, block):
+        target = pl.ds(pl.multiple_of(block * 128, 128), 128)
+        for lo, value_block in products(group_cols((0, 2)[index], block)):
+            here = slice(lo, lo + width)
+            core_in[index, target, here] = (core_in[index, target, here].astype(F32) + value_block).astype(BF)
+
+    def out_product(cols):
+        return nn(gbranch[:, cols].T, att[:, own_heads])
+
+    def far_two(index, block):
+        target = pl.ds(pl.multiple_of(block * 128, 128), 128)
+        far[index, target, 2 * units :] = out_product(group_cols((1, 3)[index], block)).astype(BF)
+
+    def near_two(index, block):
+        target = pl.ds(pl.multiple_of(block * 128, 128), 128)
+        here = slice(2 * units, 2 * units + inner)
+        core_in[index, target, here] = (
+            core_in[index, target, here].astype(F32) + out_product(group_cols((0, 2)[index], block))
+        ).astype(BF)
 
     def stage_c(i, carry):
         g_copy(i).wait_recv()
@@ -883,7 +840,7 @@
         sums[3:4, :] += jnp.sum(given, axis=0, keepdims=True)
         sums[4:5, :] += jnp.sum(grad * normed, axis=0, keepdims=True)
         sums[5:6, :] += jnp.sum(grad, axis=0, keepdims=True)
-        ga_send[here, :] = nn(low, wo[:, own_heads]).astype(BF)
+        ga_send[here, :] = nn(low, wfull[:, own_wide]).astype(BF)
         for d in range(1, nz):
             a_copy(i, d).start()
         ga_all[pl.ds(pl.multiple_of(z * rows + i * chunk, 32), chunk), :] = ga_send[
@@ -891,43 +848,35 @@
         ]
         return carry
 
-    lax.fori_loop(0, ROWS_WAVE, stage_c, 0)
-
-    def weight_two(d, carry):
-        cols = pl.ds(pl.multiple_of(d * 128, 128), 128)
-        gsum[cols, 2 * units : 2 * units + inner] = nn(gbranch[:, cols].T, att[:, own_heads]).astype(BF)
-        return carry
-
-    lax.fori_loop(0, width // 128, weight_two, 0)
+    lax.fori_loop(0, 2, stage_c, 0)
+    each_block(far_one)
+    for index in range(2):
+        c_copy(0, index).start()
+    for d in (0, 1, 3, 2):
+        weights.x_done(d)
+    lax.fori_loop(2, ROWS_WAVE, stage_c, 0)
+    each_block(far_two)
     for index in range(2):
         c_copy(1, index).start()
 
     def down(i, carry):
-        down_part[at(i), :] = nt(hidden[at(i), :], wd[...]).astype(BF)
+        total = jnp.zeros((chunk, width), F32)
+        for part in range(halves):
+            total = total + nt(
+                tree[spot(part, i, 0)[0], :], wfull[:, units + part * width : units + (part + 1) * width]
+            )
+        down_part[at(i), :] = total.astype(BF)
         return carry
 
     lax.fori_loop(0, ROWS_WAVE, down, 0)
-    for part in range(units // width):
+    for index in range(2):
+        c_copy(0, index).wait_recv()
+    each_block(near_one)
+    for index in range(2):
+        c_copy(1, index).wait_recv()
+    each_block(near_two)
+    for part in range(halves):
         sums[part : part + 1, :] = bup_acc[:, part * width : (part + 1) * width]
-
-    def join(part):
-        lo, hi = parts[part]
-        for index in range(2):
-            c_copy(part, index).wait_recv()
-
-        def one(r, carry):
-            here = pl.ds(pl.multiple_of(r * 32, 32), 32)
-            for index, target in ((0, near), (1, far)):
-                mine = pl.ds(pl.multiple_of(weights.flip((0, 2)[index]) * span + r * 32, 32), 32)
-                target[here, lo:hi] = (
-                    gsum[mine, lo:hi].astype(F32) + core_in[index, here, lo:hi].astype(F32)
-                ).astype(BF)
-            return carry
-
-        lax.fori_loop(0, span // 32, one, 0)
-
-    join(0)
-    join(1)
     weights.all_here()
     weights.finish()
     for part in range(2):
@@ -942,39 +891,89 @@
         return carry
 
     lax.fori_loop(0, ROWS_WAVE, finish, 0)
-
-
-def run_feed(dims, tok, cot, att, wa, wq, b_out, b_up, gain, shift):
+    plane_copy().wait_send()
+    core_copy().wait_send()
+    for owner in range(nz):
+        pass_on(owner).wait_send()
+
+    for owner in range(nz):
+
+        @pl.when(z != owner)
+        def _():
+            att_copy(owner).wait_send()
+
+    ups.finish()
+    downs.finish()
+    outer.finish()
+    for d in range(1, nz):
+        info_copy(d).wait_send()
+        wz_copy(d).wait_send()
+    for d in range(1, ns):
+        ws_copy(d).wait_send()
+
+
+def run_front(
+    dims, tok, w_up, w_out, w_down, cot, wq3, info, bias_qv, slopes, gain, shift, b_out, b_up
+):
     ns, nz, rows = dims
-    width, units, inner = tok.shape[1], b_up.shape[1], att.shape[1] // 2
-    span = nz * wq.shape[0]
-    total = 2 * units + inner
+    width, units, inner, depth = tok.shape[1], w_up.shape[1], w_out.shape[1], wq3.shape[1]
+    span, total, wide = nz * depth, 2 * units + inner, 3 * PAIR
     return pl.pallas_call(
-        partial(feed_kernel, dims),
-        name="feed_both",
+        partial(front_kernel, dims),
+        name="front",
         out_shape=(
-            shape((width, wq.shape[1]), BF),
-            shape((span, total), BF),
-            shape((span, total), BF),
+            shape((width, TREE), BF),
+            shape((TREE, PAIR), BF),
+            shape((TREE, PAIR), BF),
+            shape((TREE, PAIR), BF),
+            shape((TREE, PAIR), BF),
+            shape((16, 512), F32),
+            shape((nz, 16, 128), F32),
+            shape((width, nz * wide), BF),
+            shape((2, span, total), BF),
             shape((TREE, PAIR), BF),
             shape((rows, width), BF),
             shape((rows, width), F32),
             shape((rows, width), F32),
             shape((8, width), F32),
         ),
-        in_specs=[vmem()] * 9,
-        out_specs=[vmem()] * 8,
+        in_specs=[pl.BlockSpec(memory_space=pl.ANY)] * 5 + [vmem()] * 8,
+        out_specs=[vmem()] * 14,
         scratch_shapes=[
-            pltpu.VMEM((width, total), BF),
+            pltpu.VMEM((width, 2 * units + 2 * inner), BF),
+            pltpu.VMEM((depth, nz * wide), BF),
+            pltpu.VMEM((rows, 2 * inner), BF),
+            pltpu.VMEM((TREE, width), BF),
+            pltpu.VMEM((width, wide), BF),
+            pltpu.VMEM((TRUNK, 2 * PAIR), BF),
+            pltpu.VMEM((PAIR, TRUNK), BF),
+            pltpu.VMEM((16, 128), F32),
+            pltpu.VMEM((16, 128), F32),
+            pltpu.VMEM((rows, width), BF),
             pltpu.VMEM((2, span, total), BF),
             pltpu.VMEM((rows, width), BF),
-            pltpu.VMEM((rows, units), BF),
-            pltpu.VMEM((rows, units), BF),
             pltpu.VMEM((rows, width), BF),
             pltpu.VMEM((rows, width), BF),
             pltpu.VMEM((rows, width), BF),
             pltpu.VMEM((rows, inner), BF),
             pltpu.VMEM((1, units), F32),
+            dma(nz - 1),
+            dma(nz - 1),
+            dma(nz - 1),
+            dma(nz - 1),
+            dma(ns - 1),
+            dma(ns - 1),
+            dma(2, nz, SUBS),
+            dma(2, nz, SUBS),
+            dma(2, nz, SUBS),
+            dma(2, nz, SUBS),
+            dma(nz),
+            dma(nz),
+            dma(5),
+            dma(nz),
+            dma(nz),
+            dma(2),
+            dma(2),
             dma(ROWS_WAVE),
             dma(ROWS_WAVE),
             dma(nz - 1, ROWS_WAVE),
@@ -982,12 +981,15 @@
             dma(2, 2),
             dma(2, 2),
             *spread_sems(nz),
+            *spread_sems(nz),
+            *spread_sems(nz),
+            *spread_sems(nz),
         ],
         compiler_params=pltpu.CompilerParams(
-            collective_id=1, has_side_effects=True, vmem_limit_bytes=62 << 20
+            collective_id=0, has_side_effects=True, vmem_limit_bytes=FRONT_LIMIT
         ),
         cost_estimate=pl.CostEstimate(flops=40_000_000_000, bytes_accessed=20_000_000, transcendentals=0),
-    )(tok, cot, att, wa, wq, b_out, b_up, gain, shift)
+    )(tok, w_up, w_out, w_down, cot, wq3, info, bias_qv, slopes, gain, shift, b_out, b_up)
 
 
 class Halve:
@@ -1082,8 +1084,7 @@
     ga_all,
     act_turned,
     wqkv,
-    near_in,
-    far,
+    partial_in,
     down_part,
     mid,
     b_down,
@@ -1140,6 +1141,8 @@
     l_recv,
     p_send,
     p_recv,
+    r_send,
+    r_recv,
     ns_sem,
     nr_sem,
     xs_sem,
@@ -1169,7 +1172,8 @@
     step_cols = total_cols // PIECES
     units = gup.shape[1]
 
-    load = pltpu.make_async_copy(near_in, near, n_local)
+    far = partial_in.at[1]
+    load = pltpu.make_async_copy(partial_in.at[0], near, n_local)
     load.start()
 
     def peer(d):
@@ -1325,7 +1329,63 @@
         dqkv[here, 0:PAIR] = (unstack_turned(turned, BRANCH) * HD ** (-0.5)).astype(BF)
         return carry
 
-    lax.fori_loop(0, SLOTS, segment, 0)
+    def dq_copy(to):
+        return rcopy(
+            dqkv.at[to * rows : (to + 1) * rows, 0:PAIR],
+            dq_all.at[:, pl.ds(pl.multiple_of(z * wide, 128), PAIR)],
+            r_send.at[to],
+            r_recv.at[z],
+            {"ctx": to},
+        )
+
+    def send_dq(to):
+        @pl.when(z != to)
+        def _():
+            dq_copy(to).start()
+
+    def piece_copy(to, i):
+        return rcopy(
+            dqkv.at[to * rows + i * chunk : to * rows + (i + 1) * chunk, PAIR:],
+            dq_all.at[i * chunk : (i + 1) * chunk, pl.ds(pl.multiple_of(z * wide + PAIR, 128), 2 * PAIR)],
+            p_send.at[to, i],
+            p_recv.at[z, i],
+            {"ctx": to},
+        )
+
+    wave_rows = TRUNK // 4
+    wave_mask = causal(wave_rows)
+    for tile in range(4):
+        lo, hi = tile * wave_rows, (tile + 1) * wave_rows
+        stacked = stack_heads(query[lo:hi, :])
+        asked = jnp.concatenate([stacked, query_features(slopes, wave_rows)], axis=1)
+        given = stack_heads(ga_all[lo:hi, :])
+        level = lse[tile : tile + 1, :]
+        drow = row_products(pl.ds(lo, wave_rows), wave_rows)
+        probs, grads = part_back(
+            keys_aug[lo:hi, :], value[lo:hi, :], asked, given, level, drow, wave_mask
+        )
+        dv_trunk[lo:hi, :] += nn(probs, given)
+        dk_trunk[lo:hi, :] += nn(grads, stacked)
+        turned = nn(keys_turned[:, lo:hi], grads)
+        if tile:
+            probs, grads = part_back(
+                keys_aug[0:lo, :], value[0:lo, :], asked, given, level, drow, None
+            )
+            dv_trunk[0:lo, :] += nn(probs, given)
+            dk_trunk[0:lo, :] += nn(grads, stacked)
+            turned = turned + nn(keys_turned[:, 0:lo], grads)
+        dqkv[lo:hi, 0:PAIR] = (unstack_turned(turned, wave_rows) * HD ** (-0.5)).astype(BF)
+    send_dq(0)
+
+    def segments(lo, hi):
+        lax.fori_loop((lo - TRUNK) // BRANCH, (hi - TRUNK) // BRANCH, segment, 0)
+
+    segments(2 * rows, 3 * rows)
+    send_dq(2)
+    segments(TRUNK, 2 * rows)
+    send_dq(1)
+    segments(3 * rows, 4 * rows)
+    send_dq(3)
 
     def gather_up(slot, carry):
         here = pl.ds(pl.multiple_of(TRUNK + slot * BRANCH, 128), BRANCH)
@@ -1342,58 +1402,20 @@
         return carry
 
     lax.fori_loop(0, SLOTS, gather_up, 0)
-
-    def piece_copy(to, i):
-        return rcopy(
-            dqkv.at[to * rows + i * chunk : to * rows + (i + 1) * chunk, :],
-            dq_all.at[i * chunk : (i + 1) * chunk, pl.ds(pl.multiple_of(z * wide, 128), wide)],
-            p_send.at[to, i],
-            p_recv.at[z, i],
-            {"ctx": to},
-        )
-
-    def send_pieces(targets):
-        for i in range(ROWS_WAVE):
-            for to in targets:
-
-                @pl.when(z != to)
-                def _():
-                    piece_copy(to, i).start()
-
-        for to in targets:
-
-            @pl.when(z == to)
-            def _():
-                dq_all[:, pl.ds(pl.multiple_of(z * wide, 128), wide)] = dqkv[to * rows : (to + 1) * rows, :]
-
-    send_pieces([to for to in range(nz) if to * rows >= TRUNK])
-
-    wave_rows = TRUNK // 4
-    wave_mask = causal(wave_rows)
-    for tile in range(4):
-        lo, hi = tile * wave_rows, (tile + 1) * wave_rows
-        stacked = stack_heads(query[lo:hi, :])
-        asked = jnp.concatenate([stacked, query_features(slopes, wave_rows)], axis=1)
-        given = stack_heads(ga_all[lo:hi, :])
-        level = lse[tile : tile + 1, :]
-        drow = row_products(pl.ds(lo, wave_rows), wave_rows)
-        probs, grads = part_back(
-            keys_aug[lo:hi, :], value[lo:hi, :], asked, given, level, drow, wave_mask
-        )
-        dv_trunk[lo:hi, :] += nn(probs, given)
-        dk_trunk[lo:hi, :] += nn(grads, stacked)
-        turned = nn(keys_turned[:, lo:hi], grads)
-        if tile:
-            probs, grads = part_back(
-                keys_aug[0:lo, :], value[0:lo, :], asked, given, level, drow, None
-            )
-            dv_trunk[0:lo, :] += nn(probs, given)
-            dk_trunk[0:lo, :] += nn(grads, stacked)
-            turned = turned + nn(keys_turned[:, 0:lo], grads)
-        dqkv[lo:hi, 0:PAIR] = (unstack_turned(turned, wave_rows) * HD ** (-0.5)).astype(BF)
     dqkv[0:TRUNK, PAIR : 2 * PAIR] = dk_trunk[...].astype(BF)
     dqkv[0:TRUNK, 2 * PAIR :] = dv_trunk[...].astype(BF)
-    send_pieces([to for to in range(nz) if to * rows < TRUNK])
+    for i in range(ROWS_WAVE):
+        for to in range(nz):
+
+            @pl.when(z != to)
+            def _():
+                piece_copy(to, i).start()
+
+    for to in range(nz):
+
+        @pl.when(z == to)
+        def _():
+            dq_all[:, pl.ds(pl.multiple_of(z * wide, 128), wide)] = dqkv[to * rows : (to + 1) * rows, :]
 
     def weight(block, carry):
         here = pl.ds(pl.multiple_of(block * 128, 128), 128)
@@ -1441,9 +1463,17 @@
 
             @pl.when(z != owner)
             def _():
+                if i == 0:
+                    rcopy(
+                        dqkv.at[0:rows, 0:PAIR],
+                        dq_all.at[:, owner * wide : owner * wide + PAIR],
+                        r_send.at[owner],
+                        r_recv.at[owner],
+                        {"ctx": owner},
+                    ).wait_recv()
                 rcopy(
-                    dqkv.at[0:chunk, :],
-                    dq_all.at[i * chunk : (i + 1) * chunk, owner * wide : (owner + 1) * wide],
+                    dqkv.at[0:chunk, PAIR:],
+                    dq_all.at[i * chunk : (i + 1) * chunk, owner * wide + PAIR : (owner + 1) * wide],
                     p_send.at[owner, i],
                     p_recv.at[owner, i],
                     {"ctx": owner},
@@ -1470,12 +1500,17 @@
         return carry
 
     late[...] = jnp.zeros(late.shape, F32)
+    core_join()
     halves[0].step_x()
-    core_join()
+    halves[1].step_x()
     first(0)
-    halves[1].step_x()
     first(1)
-    q_spread()
+    halves[2].step_x()
+    first(2)
+    halves[3].step_x()
+    first(3)
+    down_copy().wait_recv()
+    lax.fori_loop(0, ROWS_WAVE, output, 0)
 
     @pl.when(me < owners)
     def _():
@@ -1486,15 +1521,11 @@
         early_sum[:, owner_cols(lax.rem(me, owners))] = total
         over_peers(lambda d: spread_copy(d).start())
 
-    halves[2].step_x()
-    first(2)
+    q_spread()
     halves[0].step_a()
-    halves[3].step_x()
-    first(3)
-    down_copy().wait_recv()
-    lax.fori_loop(0, ROWS_WAVE, output, 0)
+    lax.fori_loop(0, 2, second, 0)
     halves[1].step_a()
-    lax.fori_loop(0, ROWS_WAVE, second, 0)
+    lax.fori_loop(2, ROWS_WAVE, second, 0)
     over_peers(lambda d: late_copy(d).start())
     late_recv[me] = late[...]
     halves[2].step_a()
@@ -1567,14 +1598,15 @@
 
         @pl.when(z != owner)
         def _():
+            dq_copy(owner).wait_send()
             for i in range(ROWS_WAVE):
                 piece_copy(owner, i).wait_send()
 
 
 def run_back(dims, units, *inputs):
     ns, nz, rows = dims
-    width = inputs[15].shape[1]
-    span, total = inputs[9].shape
+    width = inputs[14].shape[1]
+    _, span, total = inputs[9].shape
     count = ns * nz
     depth = width // count
     wide = 3 * PAIR
@@ -1592,7 +1624,7 @@
             shape((8, width), F32),
             shape((2, width), F32),
         ),
-        in_specs=[vmem()] * 9 + [anywhere] * 2 + [vmem()] * 9,
+        in_specs=[vmem()] * 9 + [anywhere] + [vmem()] * 9,
         out_specs=[vmem()] * 8,
         scratch_shapes=[
             pltpu.VMEM((span, total), BF),
@@ -1634,6 +1666,8 @@
             dma(count - 1),
             dma(nz, ROWS_WAVE),
             dma(nz, ROWS_WAVE),
+            dma(nz),
+            dma(nz),
             dma(ROWS_WAVE),
             dma(ROWS_WAVE),
             dma(PIECES),
@@ -1678,15 +1712,15 @@
     table = jnp.stack([one, two, three, one, two, three, jnp.ones_like(one)], axis=1)
     slopes = jnp.pad(table, ((0, 0), (0, 121)))
 
-    wfull, wq, act_turned, query, key, value, out_heads, lse, info_all, att = run_tree(
-        dims, tokens, w_up, w_out.T, w_down.T, w_qkv, info, b_qv, slopes, ln_gain, ln_bias
-    )
-    units, inner = b_up.shape[0], w_out.shape[0]
-    wqkv, near, far, ga_all, down_part, mid, gmid, sums = run_feed(
-        dims, tokens, cotangent, att, wfull, wq, b_out[None, :], b_up[None, :], ln_gain, ln_bias
+    units = b_up.shape[0]
+    (
+        act_turned, query, key, value, out_heads, lse, info_all, wqkv, partial_sums, ga_all, down_part, mid, gmid, sums
+    ) = run_front(
+        dims, tokens, w_up, w_out.T, w_down.T, cotangent, w_qkv, info, b_qv, slopes, ln_gain, ln_bias,
+        b_out[None, :], b_up[None, :],
     )
     result, grad_tokens, gup, gdown, gout, grad_w_qkv, early, late = run_back(
-        dims, units, query, key, value, out_heads, lse, info_all, ga_all, act_turned, wqkv, near, far, down_part,
+        dims, units, query, key, value, out_heads, lse, info_all, ga_all, act_turned, wqkv, partial_sums, down_part,
         mid, b_down[None, :], gmid, tokens, slopes, ln_gain, ln_bias, sums,
     )
     return (

time: 348 us -> 321 us (0.922)
  Pallas kernels: 318 us -> 304 us
  local copies, waits for them, and re-layouts: 24.5 us -> 13.6 us
    pallas_call x2 -> x1, Pallas kernels: 200 us -> 188 us  [run_front(): pl.pallas_call(partial(front_kernel, dims), name='front', out_shape=(shap...]
    unnamed x50 -> x18, local copies, waits for them, and re-layouts: 20.5 us -> 8.48 us
where the time goes in v4:
time: 321 us; the launch traced here: 320 us
  Pallas kernels  304 us (95%)
  local copies, waits for them, and re-layouts  13.6 us (4%)
    pallas_call x1, Pallas kernels, run_front(): pl.pallas_call(partial(front_kernel, dims), name='front', out_shape=(shap...  188 us
    pallas_call x1, Pallas kernels, run_back(): pl.pallas_call(partial(back_kernel, dims), name='tree_backward', out_shap...  116 us
    unnamed x18, local copies, waits for them, and re-layouts  8.48 us

profile of v4, /device:TPU:12, one launch (start us, length us, event | category | flops | bytes accessed | tf_op | source)
XLA Modules:
  0.0 320.3 jit_solution(7557058382762042816)
XLA Ops:
  0.6 0.8 slice_reduce_fusion.1
  1.5 0.8 select_reduce_fusion
  2.3 0.1 fusion.2
  2.4 0.1 stack.6
  2.5 0.6 pad.13.slopes
  3.1 0.7 broadcast_in_dim.31.info
  3.7 187.9 %front.1 = (bf16[1024,2560]{1,0:T(8,128)(2,1)}, bf16[2560,128]{1,0:T(8,128)(2,1)}, bf16[2560,128]{1,0:T(8,128)(2,1)}, bf16[2560,128]{1,0:T(8,128)(2,1)}, bf16[25...) custom-call(bf16[640,1024]{1,0:T(8,128)(2,1)} %tok.3, ...), custom_call_target="tpu_custom_call" | custom-call | flops 40000000000 | bytes 20000000 | tf_op jit(solution)/shard_map/front/pallas_call | solution.py:921
  191.7 115.9 %tree_backward.1 = (bf16[640,1024]{1,0:T(8,128)(2,1)}, f32[640,1024]{1,0:T(8,128)}, f32[64,2048]{1,0:T(8,128)}, f32[64,2048]{1,0:T(8,128)}, f32[64,512]{1,0:T(8,...) custom-call(bf16[2560,128]{1,0:T(8,128)(2,1)} %get-tuple-element.34.query, ...), custom_call_target="tpu_custom_call" | custom-call | flops 40000000000 | bytes 20000000 | tf_op jit(solution)/shard_map/tree_backward/pallas_call | solution.py:1614
  307.6 0.0 copy-start
  307.6 0.9 slice_bitcast_fusion
  308.5 1.6 fusion.4
  310.1 0.6 copy.28
  310.7 0.6 reshape_squeeze.3
  311.3 0.8 fusion.5
  312.1 0.6 pad_maximum_fusion.1
  312.7 0.6 pad_maximum_fusion
  313.3 2.5 copy.35
  315.8 0.0 copy-done
  315.8 0.0 copy-start.3
  315.8 0.0 copy-start.4
  315.8 0.0 copy-start.2
  315.8 0.0 copy-start.1
  315.8 1.5 copy.36
  317.3 0.0 copy-done.3
  317.3 0.7 copy.37
  318.0 0.0 copy-done.4
  318.0 0.7 copy.38
  318.7 0.0 copy-done.2
  318.7 0.8 copy.39
  319.5 0.0 copy-done.1
  319.5 0.8 copy.40
  (3 shorter events, 0.0 us)
Async XLA Ops:
  307.6 8.1 %copy-start = (f32[640,1024]{1,0:T(8,128)S(1)}, f32[640,1024]{1,0:T(8,128)}, u32[]{:S(2)}) copy-start(f32[640,1024]{1,0:T(8,128)} %get-tuple-element.78) | copy-start | bytes 7864324
  315.8 1.5 copy-start.3
  315.8 2.3 copy-start.4
  315.8 2.9 copy-start.2
  315.8 3.7 %copy-start.1 = (f32[64,2048]{1,0:T(8,128)S(1)}, f32[64,2048]{1,0:T(8,128)}, u32[]{:S(2)}) copy-start(f32[64,2048]{1,0:T(8,128)} %get-tuple-element.54) | copy-start | bytes 1572868

commit v5 on v4

--- a/solution.py
+++ b/solution.py
@@ -144,7 +144,8 @@
 
 
 class Spread:
-    def __init__(self, full, dims, depth, cols, sems):
+    def __init__(self, full, dims, depth, cols, sems, doubling=True):
+        self.doubling = doubling
         self.full, self.depth, self.cols = full, depth, cols
         self.ns, self.nz, _ = dims
         self.s, self.z = lax.axis_index("shard"), lax.axis_index("ctx")
@@ -164,11 +165,15 @@
         return 2 * high + low
 
     def source(self, d):
-        return lax.rem(self.z + self.nz - d, self.nz)
+        low, high = lax.rem(self.z, 2), lax.div(self.z, 2)
+        low = 1 - low if d & 1 else low
+        high = 1 - high if d & 2 else high
+        return 2 * high + low
 
     def z_copy(self, d):
-        ref = self.rows(self.s, self.z)
-        return rcopy(ref, ref, self.zs.at[d - 1], self.zr.at[d - 1], {"ctx": lax.rem(self.z + d, self.nz)})
+        ref = self.rows(self.s, self.source(2 if self.doubling and d == 3 else 0))
+        to = self.source(1 if self.doubling and d == 3 else d)
+        return rcopy(ref, ref, self.zs.at[d - 1], self.zr.at[d - 1], {"ctx": to})
 
     def x_copy(self, d):
         ref = self.rows(self.s, self.source(d))
@@ -179,8 +184,10 @@
         return rcopy(ref, ref, self.cs.at[far, d], self.cr.at[far, d], {"shard": self.flip(1)})
 
     def z_start(self):
-        for d in (1, 3, 2):
-            self.z_copy(d).start()
+        self.z_copy(2).start()
+        self.z_copy(1).start()
+        if not self.doubling:
+            self.z_copy(3).start()
 
     def own(self):
         self.x_copy(0).start()
@@ -188,7 +195,9 @@
 
     def z_done(self, d):
         ref = self.rows(self.s, self.source(d))
-        rcopy(ref, ref, self.zs.at[d - 1], self.zr.at[d - 1], {"ctx": self.z}).wait_recv()
+        rcopy(ref, ref, self.zs.at[d - 1], self.zr.at[d - 1], {"ctx": self.source(1)}).wait_recv()
+        if self.doubling and d == 2:
+            self.z_copy(3).start()
         self.x_copy(d).start()
         self.c_copy(0, d).start()
 
@@ -334,7 +343,7 @@
     ups = Spread(wfull, dims, depth, slice(0, units), spread[:6])
     downs = Spread(wfull, dims, depth, slice(units, 2 * units), spread[6:12])
     weights = Spread(wqkv, dims, depth, slice(None), spread[18:])
-    outer = Spread(wfull, dims, depth, pl.ds(own_cols, inner), spread[12:18])
+    outer = Spread(wfull, dims, depth, pl.ds(own_cols, inner), spread[12:18], False)
 
     def info_copy(d):
         return rcopy(
@@ -488,6 +497,7 @@
         def _():
             outer.z_start()
             ups.z_start()
+            downs.z_start()
 
         shared(k - 1)
         project(k - 1)
@@ -500,6 +510,8 @@
     project(nz - 1)
     for d in (0, 1, 3, 2):
         outer.x_done(d)
+    ups.z_done(2)
+    ups.z_done(1)
 
     for d in range(1, nz):
         info_copy(d).wait_recv()
@@ -629,17 +641,17 @@
     for tile in range(3):
         trunk_tile(tile)
     send_out(0)
-    ups.z_done(1)
-    ups.z_done(3)
+    downs.z_done(2)
     segments(3 * rows, 4 * rows)
     send_out(3)
     trunk_tile(3)
     segments(TRUNK, 2 * rows)
     send_out(1)
-    downs.z_start()
-    ups.z_done(2)
+    downs.z_done(1)
+    ups.z_done(3)
     plane_arrival().wait_recv()
     core_copy().start()
+    downs.z_done(3)
     for owner in range(nz):
 
         @pl.when(z != owner)
@@ -654,10 +666,8 @@
             pass_on(owner).start()
 
     mid[...] = tree[pl.ds(pl.multiple_of(z * rows, 128), rows), :].astype(F32) + b_out[...]
-    for d in (0, 1, 3, 2):
+    for d in (0, 2, 1, 3):
         ups.x_done(d)
-    for d in (1, 3):
-        downs.z_done(d)
     given_load.wait()
     for owner in range(nz):
         ref = att.at[:, att_cols(1 - y, owner)]
@@ -771,15 +781,14 @@
 
     lax.fori_loop(0, nz, drain, 0)
     lax.fori_loop(0, 2, stage_one, 0)
-    downs.z_done(2)
     weights.own()
     weights.z_start()
-    for d in (0, 1, 3, 2):
+    for d in (0, 2, 1, 3):
         downs.x_done(d)
     lax.fori_loop(2, ROWS_WAVE, stage_one, 0)
     downs.all_here()
     lax.fori_loop(0, ROWS_WAVE, stage_two, 0)
-    for d in (1, 3, 2):
+    for d in (2, 1, 3):
         weights.z_done(d)
 
     def group_cols(index, block):
@@ -848,17 +857,13 @@
         ]
         return carry
 
-    lax.fori_loop(0, 2, stage_c, 0)
+    lax.fori_loop(0, 1, stage_c, 0)
     each_block(far_one)
     for index in range(2):
         c_copy(0, index).start()
-    for d in (0, 1, 3, 2):
+    lax.fori_loop(1, 2, stage_c, 0)
+    for d in (0, 2, 1, 3):
         weights.x_done(d)
-    lax.fori_loop(2, ROWS_WAVE, stage_c, 0)
-    each_block(far_two)
-    for index in range(2):
-        c_copy(1, index).start()
-
     def down(i, carry):
         total = jnp.zeros((chunk, width), F32)
         for part in range(halves):
@@ -869,9 +874,14 @@
         return carry
 
     lax.fori_loop(0, ROWS_WAVE, down, 0)
+    lax.fori_loop(2, 3, stage_c, 0)
     for index in range(2):
         c_copy(0, index).wait_recv()
     each_block(near_one)
+    lax.fori_loop(3, ROWS_WAVE, stage_c, 0)
+    each_block(far_two)
+    for index in range(2):
+        c_copy(1, index).start()
     for index in range(2):
         c_copy(1, index).wait_recv()
     each_block(near_two)
@@ -1070,7 +1080,7 @@
         self.b_copy().wait_send()
 
 
-PIECES = 4
+PIECES = 6
 
 
 def back_kernel(
@@ -1384,7 +1394,10 @@
     send_dq(2)
     segments(TRUNK, 2 * rows)
     send_dq(1)
+    load.wait()
+    halves[0].step_x()
     segments(3 * rows, 4 * rows)
+    halves[1].step_x()
     send_dq(3)
 
     def gather_up(slot, carry):
@@ -1443,7 +1456,6 @@
 
     over_peers(early_send)
     early_recv[me] = early_mine[:, owner_cols(lax.rem(me, owners))]
-    load.wait()
 
     def at(i):
         return pl.ds(pl.multiple_of(i * chunk, 32), chunk)
@@ -1501,14 +1513,14 @@
 
     late[...] = jnp.zeros(late.shape, F32)
     core_join()
-    halves[0].step_x()
-    halves[1].step_x()
+    halves[2].step_x()
     first(0)
     first(1)
-    halves[2].step_x()
+    halves[3].step_x()
     first(2)
-    halves[3].step_x()
+    halves[4].step_x()
     first(3)
+    halves[5].step_x()
     down_copy().wait_recv()
     lax.fori_loop(0, ROWS_WAVE, output, 0)
 
@@ -1523,13 +1535,15 @@
 
     q_spread()
     halves[0].step_a()
+    halves[1].step_a()
     lax.fori_loop(0, 2, second, 0)
-    halves[1].step_a()
+    halves[2].step_a()
     lax.fori_loop(2, ROWS_WAVE, second, 0)
     over_peers(lambda d: late_copy(d).start())
     late_recv[me] = late[...]
-    halves[2].step_a()
     halves[3].step_a()
+    halves[4].step_a()
+    halves[5].step_a()
 
     for d in range(1, nz):
         qz_copy(d).wait_recv()
@@ -1690,6 +1704,50 @@
     )(*inputs)
 
 
+def place_kernel(early, late, *refs):
+    count = (len(refs) - 7) // 2
+    sources, targets = refs[:count], refs[count : 2 * count]
+    b_qv, b_out, b_up, b_down, gains, shifts, sems = refs[2 * count :]
+    copies = [pltpu.make_async_copy(a, b, sems.at[k]) for k, (a, b) in enumerate(zip(sources, targets))]
+    for copy in copies:
+        copy.start()
+    wide, width = b_qv.shape[1], b_out.shape[1]
+    for row in range(2):
+        b_qv[row : row + 1, :] = early[6:7, row * wide : (row + 1) * wide]
+    b_out[...] = early[2:3, :]
+    for row in range(b_up.shape[1] // width):
+        b_up[:, row * width : (row + 1) * width] = early[row : row + 1, :]
+    b_down[...] = early[3:4, :]
+    gains[0:1, :] = late[0:1, :]
+    gains[1:2, :] = early[4:5, :]
+    shifts[0:1, :] = late[1:2, :]
+    shifts[1:2, :] = early[5:6, :]
+    for copy in copies:
+        copy.wait()
+
+
+def run_place(early, late, wide, units, *arrays):
+    width = early.shape[1]
+    anywhere = pl.BlockSpec(memory_space=pl.ANY)
+    return pl.pallas_call(
+        place_kernel,
+        name="place",
+        out_shape=(
+            *[shape(a.shape, a.dtype) for a in arrays],
+            shape((2, wide), F32),
+            shape((1, width), F32),
+            shape((1, units), F32),
+            shape((1, width), F32),
+            shape((2, width), F32),
+            shape((2, width), F32),
+        ),
+        in_specs=[vmem()] * 2 + [anywhere] * len(arrays),
+        out_specs=[anywhere] * len(arrays) + [vmem()] * 6,
+        scratch_shapes=[dma(len(arrays))],
+        compiler_params=pltpu.CompilerParams(vmem_limit_bytes=60 << 20),
+    )(early, late, *arrays)
+
+
 def fast_device(
     tokens, cotangent, seg_ids, positions, parents, w_qkv, b_qv, w_out, b_out, w_up, b_up, w_down, b_down, ln_gain, ln_bias
 ):
@@ -1723,19 +1781,22 @@
         dims, units, query, key, value, out_heads, lse, info_all, ga_all, act_turned, wqkv, partial_sums, down_part,
         mid, b_down[None, :], gmid, tokens, slopes, ln_gain, ln_bias, sums,
     )
+    result, grad_tokens, grad_w_qkv, gup, gdown, gout, b_qv_sum, b_out_sum, b_up_sum, b_down_sum, gains, shifts = run_place(
+        early, late, nz * PAIR, units, result, grad_tokens, grad_w_qkv, gup, gdown, gout
+    )
     return (
         result,
         grad_tokens,
         grad_w_qkv,
-        early[6].reshape(2, nz * PAIR),
+        b_qv_sum,
         gout.T,
-        early[2],
+        b_out_sum.reshape(-1),
         gup,
-        early[0:2].reshape(units),
+        b_up_sum.reshape(-1),
         gdown.T,
-        early[3],
-        jnp.stack([late[0], early[4]]),
-        jnp.stack([late[1], early[5]]),
+        b_down_sum.reshape(-1),
+        gains,
+        shifts,
     )
 
 

time: 321 us -> 461 us (1.44)
  Pallas kernels: 304 us -> 452 us
  local copies, waits for them, and re-layouts: 13.6 us -> 2.14 us
    pallas_call x0 -> x1, Pallas kernels: none -> 169 us  [run_place(): pl.pallas_call(place_kernel, name='place', out_shape=(*[shape(a.shape, a....]
    pallas_call x1, Pallas kernels: 188 us -> 175 us  [run_front(): pl.pallas_call(partial(front_kernel, dims), name='front', out_shape=(shap...]
    unnamed x18 -> x0, local copies, waits for them, and re-layouts: 8.48 us -> none
    pallas_call x1, Pallas kernels: 116 us -> 108 us  [run_back(): pl.pallas_call(partial(back_kernel, dims), name='tree_backward', out_shap...]
where the time goes in v5:
time: 461 us; the launch traced here: 456 us
  Pallas kernels  452 us (98%)
    pallas_call x1, Pallas kernels, run_front(): pl.pallas_call(partial(front_kernel, dims), name='front', out_shape=(shap...  175 us
    pallas_call x1, Pallas kernels, run_place(): pl.pallas_call(place_kernel, name='place', out_shape=(*[shape(a.shape, a....  169 us
    pallas_call x1, Pallas kernels, run_back(): pl.pallas_call(partial(back_kernel, dims), name='tree_backward', out_shap...  108 us

profile of v5, /device:TPU:12, one launch (start us, length us, event | category | flops | bytes accessed | tf_op | source)
XLA Modules:
  0.0 456.1 jit_solution(5572577655149550608)
XLA Ops:
  0.6 0.8 slice_reduce_fusion
  1.5 0.8 select_reduce_fusion
  2.3 0.1 fusion.2
  2.4 0.1 stack.2
  2.5 0.6 pad.13.slopes
  3.1 0.7 broadcast_in_dim.31.info
  3.7 175.3 %front.1 = (bf16[1024,2560]{1,0:T(8,128)(2,1)}, bf16[2560,128]{1,0:T(8,128)(2,1)}, bf16[2560,128]{1,0:T(8,128)(2,1)}, bf16[2560,128]{1,0:T(8,128)(2,1)}, bf16[25...) custom-call(bf16[640,1024]{1,0:T(8,128)(2,1)} %tok.3, ...), custom_call_target="tpu_custom_call" | custom-call | flops 40000000000 | bytes 20000000 | tf_op jit(solution)/shard_map/front/pallas_call | solution.py:931
  179.0 107.5 %tree_backward.1 = (bf16[640,1024]{1,0:T(8,128)(2,1)}, f32[640,1024]{1,0:T(8,128)}, f32[64,2048]{1,0:T(8,128)}, f32[64,2048]{1,0:T(8,128)}, f32[64,512]{1,0:T(8,...) custom-call(bf16[2560,128]{1,0:T(8,128)(2,1)} %get-tuple-element.46.query, ...), custom_call_target="tpu_custom_call" | custom-call | flops 40000000000 | bytes 20000000 | tf_op jit(solution)/shard_map/tree_backward/pallas_call | solution.py:1628
  286.6 169.3 %place.1 = (bf16[640,1024]{1,0:T(8,128)(2,1)}, f32[640,1024]{1,0:T(8,128)}, f32[3,64,512]{2,1,0:T(8,128)}, f32[64,2048]{1,0:T(8,128)}, f32[64,2048]{1,0:T(8,128)...) custom-call(f32[8,1024]{1,0:T(8,128)} %get-tuple-element.60.early, ...), custom_call_target="tpu_custom_call" | custom-call | tf_op jit(solution)/shard_map/place/pallas_call | solution.py:1732
  (3 shorter events, 0.0 us)

commit v6 on v5

--- a/solution.py
+++ b/solution.py
@@ -255,20 +255,31 @@
     shift,
     b_out,
     b_up,
+    act_turned_o,
+    query_o,
+    key_o,
+    value_o,
+    out_heads_o,
+    lse,
+    info_all,
+    wqkv_o,
+    core_o,
+    ga_o,
+    down_o,
+    mid_o,
+    gmid_o,
+    sums,
     act_turned,
     query,
     key,
     value,
     out_heads,
-    lse,
-    info_all,
     wqkv,
     core_in,
     ga_all,
     down_part,
     mid,
     gmid,
-    sums,
     wfull,
     wq,
     att,
@@ -309,6 +320,7 @@
     ar_sem,
     cs_sem,
     cr_sem,
+    store_sem,
     *spread,
 ):
     ns, nz, rows = dims
@@ -328,6 +340,25 @@
     ]
     given_load = pltpu.make_async_copy(cot_in, cot, local_sem.at[4])
     given_load.start()
+    stores = [
+        pltpu.make_async_copy(a, b, store_sem.at[k])
+        for k, (a, b) in enumerate(
+            (
+                (act_turned, act_turned_o),
+                (query, query_o),
+                (key, key_o),
+                (value, value_o),
+                (out_heads, out_heads_o),
+                (mid, mid_o),
+                (gmid, gmid_o),
+                (down_part, down_o),
+                (core_in.at[:, :, 0 : 2 * units], core_o.at[:, :, 0 : 2 * units]),
+                (core_in.at[:, :, 2 * units :], core_o.at[:, :, 2 * units :]),
+                (wqkv, wqkv_o),
+                (ga_all, ga_o),
+            )
+        )
+    ]
     for one in starts:
         one.start()
     for to in range(nz):
@@ -508,6 +539,8 @@
         outer.z_done(d)
     shared(nz - 1)
     project(nz - 1)
+    for k in range(4):
+        stores[k].start()
     for d in (0, 1, 3, 2):
         outer.x_done(d)
     ups.z_done(2)
@@ -649,6 +682,7 @@
     send_out(1)
     downs.z_done(1)
     ups.z_done(3)
+    stores[4].start()
     plane_arrival().wait_recv()
     core_copy().start()
     downs.z_done(3)
@@ -786,6 +820,7 @@
     for d in (0, 2, 1, 3):
         downs.x_done(d)
     lax.fori_loop(2, ROWS_WAVE, stage_one, 0)
+    stores[5].start()
     downs.all_here()
     lax.fori_loop(0, ROWS_WAVE, stage_two, 0)
     for d in (2, 1, 3):
@@ -874,20 +909,25 @@
         return carry
 
     lax.fori_loop(0, ROWS_WAVE, down, 0)
+    stores[7].start()
     lax.fori_loop(2, 3, stage_c, 0)
     for index in range(2):
         c_copy(0, index).wait_recv()
     each_block(near_one)
+    stores[8].start()
     lax.fori_loop(3, ROWS_WAVE, stage_c, 0)
+    stores[6].start()
     each_block(far_two)
     for index in range(2):
         c_copy(1, index).start()
     for index in range(2):
         c_copy(1, index).wait_recv()
     each_block(near_two)
+    stores[9].start()
     for part in range(halves):
         sums[part : part + 1, :] = bup_acc[:, part * width : (part + 1) * width]
     weights.all_here()
+    stores[10].start()
     weights.finish()
     for part in range(2):
         for index in range(2):
@@ -901,6 +941,7 @@
         return carry
 
     lax.fori_loop(0, ROWS_WAVE, finish, 0)
+    stores[11].start()
     plane_copy().wait_send()
     core_copy().wait_send()
     for owner in range(nz):
@@ -920,6 +961,8 @@
         wz_copy(d).wait_send()
     for d in range(1, ns):
         ws_copy(d).wait_send()
+    for store in stores:
+        store.wait()
 
 
 def run_front(
@@ -928,6 +971,7 @@
     ns, nz, rows = dims
     width, units, inner, depth = tok.shape[1], w_up.shape[1], w_out.shape[1], wq3.shape[1]
     span, total, wide = nz * depth, 2 * units + inner, 3 * PAIR
+    anywhere = pl.BlockSpec(memory_space=pl.ANY)
     return pl.pallas_call(
         partial(front_kernel, dims),
         name="front",
@@ -948,8 +992,19 @@
             shape((8, width), F32),
         ),
         in_specs=[pl.BlockSpec(memory_space=pl.ANY)] * 5 + [vmem()] * 8,
-        out_specs=[vmem()] * 14,
+        out_specs=[anywhere] * 5 + [vmem()] * 2 + [anywhere] * 6 + [vmem()],
         scratch_shapes=[
+            pltpu.VMEM((width, TREE), BF),
+            pltpu.VMEM((TREE, PAIR), BF),
+            pltpu.VMEM((TREE, PAIR), BF),
+            pltpu.VMEM((TREE, PAIR), BF),
+            pltpu.VMEM((TREE, PAIR), BF),
+            pltpu.VMEM((width, nz * wide), BF),
+            pltpu.VMEM((2, span, total), BF),
+            pltpu.VMEM((TREE, PAIR), BF),
+            pltpu.VMEM((rows, width), BF),
+            pltpu.VMEM((rows, width), F32),
+            pltpu.VMEM((rows, width), F32),
             pltpu.VMEM((width, 2 * units + 2 * inner), BF),
             pltpu.VMEM((depth, nz * wide), BF),
             pltpu.VMEM((rows, 2 * inner), BF),
@@ -990,6 +1045,7 @@
             dma(nz - 1, ROWS_WAVE),
             dma(2, 2),
             dma(2, 2),
+            dma(12),
             *spread_sems(nz),
             *spread_sems(nz),
             *spread_sems(nz),
@@ -1092,14 +1148,14 @@
     lse,
     info_all,
     ga_all,
-    act_turned,
-    wqkv,
+    act_turned_in,
+    wqkv_in,
     partial_in,
-    down_part,
-    mid,
+    down_in,
+    mid_in,
     b_down,
-    gmid,
-    tok,
+    gmid_in,
+    tok_in,
     slopes,
     gain,
     shift,
@@ -1112,6 +1168,12 @@
     gwqkv,
     early_sum,
     late_sum,
+    act_turned,
+    wqkv,
+    down_part,
+    mid,
+    gmid,
+    tok,
     near,
     x_in,
     a_in,
@@ -1167,6 +1229,7 @@
     qz_send,
     qz_recv,
     n_local,
+    load_sem,
 ):
     ns, nz, rows = dims
     s, z, y = lax.axis_index("shard"), lax.axis_index("ctx"), lax.axis_index("tp")
@@ -1184,7 +1247,23 @@
 
     far = partial_in.at[1]
     load = pltpu.make_async_copy(partial_in.at[0], near, n_local)
+    loads = [
+        pltpu.make_async_copy(a, c, load_sem.at[k])
+        for k, (a, c) in enumerate(
+            (
+                (down_in, down_part),
+                (act_turned_in, act_turned),
+                (wqkv_in, wqkv),
+                (mid_in, mid),
+                (gmid_in, gmid),
+                (tok_in, tok),
+            )
+        )
+    ]
+    loads[0].start()
     load.start()
+    for one in loads[1:]:
+        one.start()
 
     def peer(d):
         index = lax.rem(me + d, count)
@@ -1282,6 +1361,7 @@
 
     for half in halves:
         half.x_copy().start()
+    loads[0].wait()
     down_copy().start()
 
     fill_labels(info_all, rows // BRANCH, labels, parents)
@@ -1435,6 +1515,7 @@
         wg_send[here, :] = nn(act_turned[here, :], dqkv[...]).astype(BF)
         return carry
 
+    loads[1].wait()
     lax.fori_loop(0, width // 128, weight, 0)
     q_copy(0).start()
     q_copy(1).start()
@@ -1512,6 +1593,8 @@
         return carry
 
     late[...] = jnp.zeros(late.shape, F32)
+    for one in loads[2:]:
+        one.wait()
     core_join()
     halves[2].step_x()
     first(0)
@@ -1638,9 +1721,10 @@
             shape((8, width), F32),
             shape((2, width), F32),
         ),
-        in_specs=[vmem()] * 9 + [anywhere] + [vmem()] * 9,
+        in_specs=[vmem()] * 7 + [anywhere] * 5 + [vmem()] + [anywhere] * 2 + [vmem()] * 4,
         out_specs=[vmem()] * 8,
         scratch_shapes=[
+            *[pltpu.VMEM(inputs[k].shape, inputs[k].dtype) for k in (7, 8, 10, 11, 13, 14)],
             pltpu.VMEM((span, total), BF),
             pltpu.VMEM((span, total), BF),
             pltpu.VMEM((2, depth, total), BF),
@@ -1696,6 +1780,7 @@
             dma(nz - 1),
             dma(nz - 1),
             pltpu.SemaphoreType.DMA,
+            dma(6),
         ],
         compiler_params=pltpu.CompilerParams(
             collective_id=2, has_side_effects=True, vmem_limit_bytes=60 << 20
@@ -1705,11 +1790,16 @@
 
 
 def place_kernel(early, late, *refs):
-    count = (len(refs) - 7) // 2
-    sources, targets = refs[:count], refs[count : 2 * count]
-    b_qv, b_out, b_up, b_down, gains, shifts, sems = refs[2 * count :]
-    copies = [pltpu.make_async_copy(a, b, sems.at[k]) for k, (a, b) in enumerate(zip(sources, targets))]
-    for copy in copies:
+    count = (len(refs) - 7) // 3
+    sources, targets, middle = refs[:count], refs[count : 2 * count], refs[2 * count + 6 : -1]
+    b_qv, b_out, b_up, b_down, gains, shifts = refs[2 * count : 2 * count + 6]
+    sems = refs[-1]
+    loads = [pltpu.make_async_copy(a, b, sems.at[0, k]) for k, (a, b) in enumerate(zip(sources, middle))]
+    copies = [pltpu.make_async_copy(a, b, sems.at[1, k]) for k, (a, b) in enumerate(zip(middle, targets))]
+    for load in loads:
+        load.start()
+    for load, copy in zip(loads, copies):
+        load.wait()
         copy.start()
     wide, width = b_qv.shape[1], b_out.shape[1]
     for row in range(2):
@@ -1743,7 +1833,7 @@
         ),
         in_specs=[vmem()] * 2 + [anywhere] * len(arrays),
         out_specs=[anywhere] * len(arrays) + [vmem()] * 6,
-        scratch_shapes=[dma(len(arrays))],
+        scratch_shapes=[*[pltpu.VMEM(a.shape, a.dtype) for a in arrays], dma(2, len(arrays))],
         compiler_params=pltpu.CompilerParams(vmem_limit_bytes=60 << 20),
     )(early, late, *arrays)
 

time: 461 us -> 287 us (0.62)
  Pallas kernels: 452 us -> 278 us
    pallas_call x1, Pallas kernels: 169 us -> 5.6 us  [run_place(): pl.pallas_call(place_kernel, name='place', out_shape=(*[shape(a.shape, a....]
    pallas_call x1, Pallas kernels: 175 us -> 169 us  [run_front(): pl.pallas_call(partial(front_kernel, dims), name='front', out_shape=(shap...]
where the time goes in v6:
time: 287 us; the launch traced here: 282 us
  Pallas kernels  278 us (97%)
    pallas_call x1, Pallas kernels, run_front(): pl.pallas_call(partial(front_kernel, dims), name='front', out_shape=(shap...  169 us
    pallas_call x1, Pallas kernels, run_back(): pl.pallas_call(partial(back_kernel, dims), name='tree_backward', out_shap...  104 us

profile of v6, /device:TPU:12, one launch (start us, length us, event | category | flops | bytes accessed | tf_op | source)
XLA Modules:
  0.0 282.1 jit_solution(8252546353199344721)
XLA Ops:
  0.6 0.8 slice_reduce_fusion
  1.5 0.8 select_reduce_fusion
  2.3 0.1 fusion.2
  2.4 0.1 stack.2
  2.5 0.6 pad.13.slopes
  3.1 0.7 broadcast_in_dim.31.info
  3.7 168.7 %front.1 = (bf16[1024,2560]{1,0:T(8,128)(2,1)}, bf16[2560,128]{1,0:T(8,128)(2,1)}, bf16[2560,128]{1,0:T(8,128)(2,1)}, bf16[2560,128]{1,0:T(8,128)(2,1)}, bf16[25...) custom-call(bf16[640,1024]{1,0:T(8,128)(2,1)} %tok_in.1, ...), custom_call_target="tpu_custom_call" | custom-call | flops 40000000000 | bytes 20000000 | tf_op jit(solution)/shard_map/front/pallas_call | solution.py:975
  172.4 103.8 %tree_backward.1 = (bf16[640,1024]{1,0:T(8,128)(2,1)}, f32[640,1024]{1,0:T(8,128)}, f32[64,2048]{1,0:T(8,128)}, f32[64,2048]{1,0:T(8,128)}, f32[64,512]{1,0:T(8,...) custom-call(bf16[2560,128]{1,0:T(8,128)(2,1)} %get-tuple-element.46.query, ...), custom_call_target="tpu_custom_call" | custom-call | flops 40000000000 | bytes 20000000 | tf_op jit(solution)/shard_map/tree_backward/pallas_call | solution.py:1711
  276.3 5.6 %place.1 = (bf16[640,1024]{1,0:T(8,128)(2,1)}, f32[640,1024]{1,0:T(8,128)}, f32[3,64,512]{2,1,0:T(8,128)}, f32[64,2048]{1,0:T(8,128)}, f32[64,2048]{1,0:T(8,128)...) custom-call(f32[8,1024]{1,0:T(8,128)} %get-tuple-element.60.early, ...), custom_call_target="tpu_custom_call" | custom-call | tf_op jit(solution)/shard_map/place/pallas_call | solution.py:1822
  (3 shorter events, 0.0 us)

commit v7 on v6

--- a/solution.py
+++ b/solution.py
@@ -2,6 +2,7 @@
 
 import jax
 import jax.numpy as jnp
+import numpy as np
 from jax import lax
 from jax.experimental import pallas as pl
 from jax.experimental.pallas import tpu as pltpu
@@ -248,9 +249,10 @@
     w_down,
     cot_in,
     wq3,
-    info,
+    seg,
+    above,
     bias_qv,
-    slopes,
+    slope_table,
     gain,
     shift,
     b_out,
@@ -280,6 +282,7 @@
     down_part,
     mid,
     gmid,
+    info,
     wfull,
     wq,
     att,
@@ -325,6 +328,7 @@
 ):
     ns, nz, rows = dims
     s, z, y = lax.axis_index("shard"), lax.axis_index("ctx"), lax.axis_index("tp")
+    slopes = slope_table.at[y * nz + z]
     half = rows // 2
     sub = half // SUBS
     depth = wq.shape[0]
@@ -366,6 +370,13 @@
             wq[:, to * wide + part * PAIR : to * wide + (part + 1) * PAIR] = wq3[
                 part, :, to * PAIR : (to + 1) * PAIR
             ]
+    lane = lax.broadcasted_iota(jnp.int32, above.shape, 1)
+    info[...] = jnp.zeros(info.shape, F32)
+    for block in range(rows // BRANCH):
+        label = seg[block : block + 1, 0:1]
+        upper_label = jnp.sum(jnp.where(lane == label, above[...], 0), axis=1, keepdims=True)
+        info[block : block + 1, :] = jnp.broadcast_to(label, (1, 128)).astype(F32)
+        info[8 + block : 9 + block, :] = jnp.broadcast_to(upper_label, (1, 128)).astype(F32)
     greet(
         [{"ctx": lax.rem(z + d, nz)} for d in range(1, nz)]
         + [{"shard": lax.rem(s + d, ns)} for d in range(1, ns)]
@@ -666,19 +677,23 @@
         out_heads[lo:hi, :] = unstack_turned(turned, wave_rows).astype(BF)
         lse[tile : tile + 1, :] = top + jnp.log2(total)
 
-    def segments(lo, hi):
-        lax.fori_loop((lo - TRUNK) // BRANCH, (hi - TRUNK) // BRANCH, segment, 0)
-
-    segments(2 * rows, 3 * rows)
-    send_out(2)
-    for tile in range(3):
-        trunk_tile(tile)
-    send_out(0)
-    downs.z_done(2)
-    segments(3 * rows, 4 * rows)
-    send_out(3)
-    trunk_tile(3)
-    segments(TRUNK, 2 * rows)
+    def turn(n, carry):
+        @pl.when(n == 5)
+        def _():
+            send_out(2)
+            for tile in range(3):
+                trunk_tile(tile)
+            send_out(0)
+            downs.z_done(2)
+
+        @pl.when(n == 10)
+        def _():
+            send_out(3)
+            trunk_tile(3)
+
+        return segment(lax.rem(n + 2, SLOTS), carry)
+
+    lax.fori_loop(0, SLOTS, turn, 0)
     send_out(1)
     downs.z_done(1)
     ups.z_done(3)
@@ -750,13 +765,18 @@
     bup_acc[...] = jnp.zeros(bup_acc.shape, F32)
     per = width // BLOCK
 
-    def spot(first, i, c):
-        row = (first + lax.div(c, per)) * rows + i * chunk
+    def spot(first, i, c, size):
+        row = (first + lax.div(c, per)) * rows + i * size
         col = lax.rem(c, per) * BLOCK
-        return pl.ds(pl.multiple_of(row, 32), chunk), pl.ds(pl.multiple_of(col, 128), BLOCK)
+        return pl.ds(pl.multiple_of(row, 32), size), pl.ds(pl.multiple_of(col, 128), BLOCK)
+
+    large = 2 * chunk
+
+    def large_at(i):
+        return pl.ds(pl.multiple_of(i * large, 64), large)
 
     def stage_one(i, carry):
-        here = at(i)
+        here = large_at(i)
         middle = mid[here, :] + nt(att[here, :], wfull[:, 2 * units :])
         mid[here, :] = middle
         act[here, :] = norm_rows(middle, gain[1:2, :], shift[1:2, :])[0].astype(BF)
@@ -766,36 +786,37 @@
             upper = nn(act[here, :], wfull[:, cols]) + b_up[:, cols]
             square = upper * upper
             turn = jnp.tanh(ROOT * (upper + CURVE * (square * upper)))
-            tree[spot(0, i, c)] = (0.5 * upper * (1.0 + turn)).astype(BF)
+            tree[spot(0, i, c, large)] = (0.5 * upper * (1.0 + turn)).astype(BF)
             steep = 0.5 * (1.0 + turn) + (0.5 * ROOT) * upper * (1.0 - turn * turn) * (
                 1.0 + (3.0 * CURVE) * square
             )
-            tree[spot(halves, i, c)] = steep.astype(BF)
+            tree[spot(halves, i, c, large)] = steep.astype(BF)
             return inner_carry
 
         lax.fori_loop(0, units // BLOCK, columns, 0)
         return carry
 
     def stage_two(i, carry):
-        here = at(i)
+        here = large_at(i)
 
         def columns(c, inner_carry):
             cols = pl.ds(pl.multiple_of(c * BLOCK, 128), BLOCK)
             down_cols = pl.ds(pl.multiple_of(units + c * BLOCK, 128), BLOCK)
             slope = nn(cot[here, :], wfull[:, down_cols])
-            low = (slope * tree[spot(halves, i, c)].astype(F32)).astype(BF)
-            tree[spot(halves, i, c)] = low
+            low = (slope * tree[spot(halves, i, c, large)].astype(F32)).astype(BF)
+            tree[spot(halves, i, c, large)] = low
             bup_acc[:, cols] += jnp.sum(low.astype(F32), axis=0, keepdims=True)
             return inner_carry
 
         lax.fori_loop(0, units // BLOCK, columns, 0)
-        total = jnp.zeros((chunk, width), F32)
+        total = jnp.zeros((large, width), F32)
         for part in range(halves):
             total = total + nt(
-                tree[spot(halves + part, i, 0)[0], :], wfull[:, part * width : (part + 1) * width]
+                tree[spot(halves + part, i, 0, large)[0], :], wfull[:, part * width : (part + 1) * width]
             )
         g_send[here, :] = total.astype(BF)
-        g_copy(i).start()
+        g_copy(2 * i).start()
+        g_copy(2 * i + 1).start()
         return carry
 
     def drain(k, carry):
@@ -814,15 +835,15 @@
         return carry
 
     lax.fori_loop(0, nz, drain, 0)
-    lax.fori_loop(0, 2, stage_one, 0)
+    lax.fori_loop(0, 1, stage_one, 0)
     weights.own()
     weights.z_start()
     for d in (0, 2, 1, 3):
         downs.x_done(d)
-    lax.fori_loop(2, ROWS_WAVE, stage_one, 0)
+    lax.fori_loop(1, ROWS_WAVE // 2, stage_one, 0)
     stores[5].start()
     downs.all_here()
-    lax.fori_loop(0, ROWS_WAVE, stage_two, 0)
+    lax.fori_loop(0, ROWS_WAVE // 2, stage_two, 0)
     for d in (2, 1, 3):
         weights.z_done(d)
 
@@ -900,15 +921,15 @@
     for d in (0, 2, 1, 3):
         weights.x_done(d)
     def down(i, carry):
-        total = jnp.zeros((chunk, width), F32)
+        total = jnp.zeros((large, width), F32)
         for part in range(halves):
             total = total + nt(
-                tree[spot(part, i, 0)[0], :], wfull[:, units + part * width : units + (part + 1) * width]
+                tree[spot(part, i, 0, large)[0], :], wfull[:, units + part * width : units + (part + 1) * width]
             )
-        down_part[at(i), :] = total.astype(BF)
+        down_part[large_at(i), :] = total.astype(BF)
         return carry
 
-    lax.fori_loop(0, ROWS_WAVE, down, 0)
+    lax.fori_loop(0, ROWS_WAVE // 2, down, 0)
     stores[7].start()
     lax.fori_loop(2, 3, stage_c, 0)
     for index in range(2):
@@ -966,7 +987,7 @@
 
 
 def run_front(
-    dims, tok, w_up, w_out, w_down, cot, wq3, info, bias_qv, slopes, gain, shift, b_out, b_up
+    dims, tok, w_up, w_out, w_down, cot, wq3, seg, above, bias_qv, slopes, gain, shift, b_out, b_up
 ):
     ns, nz, rows = dims
     width, units, inner, depth = tok.shape[1], w_up.shape[1], w_out.shape[1], wq3.shape[1]
@@ -991,7 +1012,7 @@
             shape((rows, width), F32),
             shape((8, width), F32),
         ),
-        in_specs=[pl.BlockSpec(memory_space=pl.ANY)] * 5 + [vmem()] * 8,
+        in_specs=[anywhere] * 5 + [vmem()] * 9,
         out_specs=[anywhere] * 5 + [vmem()] * 2 + [anywhere] * 6 + [vmem()],
         scratch_shapes=[
             pltpu.VMEM((width, TREE), BF),
@@ -1005,6 +1026,7 @@
             pltpu.VMEM((rows, width), BF),
             pltpu.VMEM((rows, width), F32),
             pltpu.VMEM((rows, width), F32),
+            pltpu.VMEM((16, 128), F32),
             pltpu.VMEM((width, 2 * units + 2 * inner), BF),
             pltpu.VMEM((depth, nz * wide), BF),
             pltpu.VMEM((rows, 2 * inner), BF),
@@ -1055,7 +1077,7 @@
             collective_id=0, has_side_effects=True, vmem_limit_bytes=FRONT_LIMIT
         ),
         cost_estimate=pl.CostEstimate(flops=40_000_000_000, bytes_accessed=20_000_000, transcendentals=0),
-    )(tok, w_up, w_out, w_down, cot, wq3, info, bias_qv, slopes, gain, shift, b_out, b_up)
+    )(tok, w_up, w_out, w_down, cot, wq3, seg, above, bias_qv, slopes, gain, shift, b_out, b_up)
 
 
 class Halve:
@@ -1156,7 +1178,7 @@
     b_down,
     gmid_in,
     tok_in,
-    slopes,
+    slope_table,
     gain,
     shift,
     early,
@@ -1241,6 +1263,7 @@
     span = nz * depth
     wide = 3 * PAIR
     other = {"tp": 1 - y}
+    slopes = slope_table.at[y * nz + z]
     total_cols = near.shape[1]
     step_cols = total_cols // PIECES
     units = gup.shape[1]
@@ -1467,16 +1490,20 @@
         dqkv[lo:hi, 0:PAIR] = (unstack_turned(turned, wave_rows) * HD ** (-0.5)).astype(BF)
     send_dq(0)
 
-    def segments(lo, hi):
-        lax.fori_loop((lo - TRUNK) // BRANCH, (hi - TRUNK) // BRANCH, segment, 0)
-
-    segments(2 * rows, 3 * rows)
-    send_dq(2)
-    segments(TRUNK, 2 * rows)
-    send_dq(1)
-    load.wait()
-    halves[0].step_x()
-    segments(3 * rows, 4 * rows)
+    def turn(n, carry):
+        @pl.when(n == 5)
+        def _():
+            send_dq(2)
+
+        @pl.when(n == 7)
+        def _():
+            send_dq(1)
+            load.wait()
+            halves[0].step_x()
+
+        return segment(jnp.where(n < 5, n + 2, jnp.where(n < 7, n - 5, n)), carry)
+
+    lax.fori_loop(0, SLOTS, turn, 0)
     halves[1].step_x()
     send_dq(3)
 
@@ -1838,6 +1865,20 @@
     )(early, late, *arrays)
 
 
+def position_slopes(ntp, nz):
+    index = np.arange(HEADS, dtype=np.float32).reshape(ntp * nz, 2)
+    slope = np.exp2(-8.0 * (index + 1.0) / HEADS).astype(np.float32)
+    table = np.zeros((ntp * nz, 2, 128), np.float32)
+    left = slope
+    for part in range(3):
+        piece = left.astype(BF).astype(np.float32)
+        table[:, :, part] = piece
+        table[:, :, part + 3] = piece
+        left = left - piece
+    table[:, :, 6] = 1.0
+    return table
+
+
 def fast_device(
     tokens, cotangent, seg_ids, positions, parents, w_qkv, b_qv, w_out, b_out, w_up, b_up, w_down, b_down, ln_gain, ln_bias
 ):
@@ -1845,26 +1886,13 @@
     ns, nz, ntp = lax.axis_size("shard"), lax.axis_size("ctx"), lax.axis_size("tp")
     dims = (ns, nz, rows)
 
-    labels = seg_ids.reshape(rows // BRANCH, BRANCH)[:, 0]
-    match = labels[:, None] == jnp.arange(parents.shape[0], dtype=jnp.int32)[None, :]
-    above = jnp.sum(jnp.where(match, parents[None, :], 0), axis=1)
-    fill = 8 - rows // BRANCH
-    lines = jnp.concatenate([jnp.pad(labels, (0, fill)), jnp.pad(above, (0, fill))]).astype(F32)
-    info = jnp.broadcast_to(lines[:, None], (16, 128))
-    per = HEADS // ntp
-    index = lax.axis_index("tp") * per + lax.axis_index("ctx") * 2 + jnp.arange(2)
-    slope = 2.0 ** (-8.0 * (index.astype(F32) + 1.0) / HEADS)
-    one = lax.reduce_precision(slope, 8, 7)
-    two = lax.reduce_precision(slope - one, 8, 7)
-    three = lax.reduce_precision(slope - one - two, 8, 7)
-    table = jnp.stack([one, two, three, one, two, three, jnp.ones_like(one)], axis=1)
-    slopes = jnp.pad(table, ((0, 0), (0, 121)))
-
+    slopes = jnp.asarray(position_slopes(ntp, nz))
     units = b_up.shape[0]
     (
         act_turned, query, key, value, out_heads, lse, info_all, wqkv, partial_sums, ga_all, down_part, mid, gmid, sums
     ) = run_front(
-        dims, tokens, w_up, w_out.T, w_down.T, cotangent, w_qkv, info, b_qv, slopes, ln_gain, ln_bias,
+        dims, tokens, w_up, w_out.T, w_down.T, cotangent, w_qkv, seg_ids.reshape(rows // BRANCH, BRANCH),
+        parents[None, :], b_qv, slopes, ln_gain, ln_bias,
         b_out[None, :], b_up[None, :],
     )
     result, grad_tokens, gup, gdown, gout, grad_w_qkv, early, late = run_back(

time: 287 us -> 274 us (0.955); the launches traced: 282 us -> 274 us
  Pallas kernels: 278 us -> 273 us
    pallas_call x1, Pallas kernels: 169 us -> 162 us  [run_front(): pl.pallas_call(partial(front_kernel, dims), name='front', out_shape=(shap...]
where the time goes in v7:
time: 274 us
  Pallas kernels  273 us (100%)
    pallas_call x1, Pallas kernels, run_front(): pl.pallas_call(partial(front_kernel, dims), name='front', out_shape=(shap...  162 us
    pallas_call x1, Pallas kernels, run_back(): pl.pallas_call(partial(back_kernel, dims), name='tree_backward', out_shap...  106 us
    pallas_call x1, Pallas kernels, run_place(): pl.pallas_call(place_kernel, name='place', out_shape=(*[shape(a.shape, a....  5.6 us

profile of v7, /device:TPU:12, one launch (start us, length us, event | category | flops | bytes accessed | tf_op | source)
XLA Modules:
  0.0 273.6 jit_solution(5600041594163528680)
XLA Ops:
  0.6 161.6 %front.1 = (bf16[1024,2560]{1,0:T(8,128)(2,1)}, bf16[2560,128]{1,0:T(8,128)(2,1)}, bf16[2560,128]{1,0:T(8,128)(2,1)}, bf16[2560,128]{1,0:T(8,128)(2,1)}, bf16[25...) custom-call(bf16[640,1024]{1,0:T(8,128)(2,1)} %tok_in.1, ...), custom_call_target="tpu_custom_call" | custom-call | flops 40000000000 | bytes 20000000 | tf_op jit(solution)/shard_map/front/pallas_call | solution.py:996
  162.3 105.6 %tree_backward.1 = (bf16[640,1024]{1,0:T(8,128)(2,1)}, f32[640,1024]{1,0:T(8,128)}, f32[64,2048]{1,0:T(8,128)}, f32[64,2048]{1,0:T(8,128)}, f32[64,512]{1,0:T(8,...) custom-call(bf16[2560,128]{1,0:T(8,128)(2,1)} %get-tuple-element.46.query, ...), custom_call_target="tpu_custom_call" | custom-call | flops 40000000000 | bytes 20000000 | tf_op jit(solution)/shard_map/tree_backward/pallas_call | solution.py:1738
  267.8 5.6 %place.1 = (bf16[640,1024]{1,0:T(8,128)(2,1)}, f32[640,1024]{1,0:T(8,128)}, f32[3,64,512]{2,1,0:T(8,128)}, f32[64,2048]{1,0:T(8,128)}, f32[64,2048]{1,0:T(8,128)...) custom-call(f32[8,1024]{1,0:T(8,128)} %get-tuple-element.60.early, ...), custom_call_target="tpu_custom_call" | custom-call | tf_op jit(solution)/shard_map/place/pallas_call | solution.py:1849

commit v8 on v7

--- a/solution.py
+++ b/solution.py
@@ -1182,14 +1182,16 @@
     gain,
     shift,
     early,
-    result,
-    gtok,
+    result_o,
+    gtok_o,
     gup,
     gdown,
     gout,
     gwqkv,
     early_sum,
     late_sum,
+    result,
+    gtok,
     act_turned,
     wqkv,
     down_part,
@@ -1252,6 +1254,7 @@
     qz_recv,
     n_local,
     load_sem,
+    out_sem,
 ):
     ns, nz, rows = dims
     s, z, y = lax.axis_index("shard"), lax.axis_index("ctx"), lax.axis_index("tp")
@@ -1602,6 +1605,11 @@
         n_send[at(i), :] = nt(dq_all[at(i), :], wqkv[...]).astype(BF)
         n_copy(i).start()
 
+    def gtok_store(i):
+        return pltpu.make_async_copy(gtok.at[at(i), :], gtok_o.at[at(i), :], out_sem.at[i])
+
+    result_store = pltpu.make_async_copy(result, result_o, out_sem.at[ROWS_WAVE])
+
     def second(i, carry):
         n_copy(i).wait_recv()
         here = at(i)
@@ -1610,6 +1618,7 @@
         gtok[here, :] = gmid[here, :] + norm_rows_back(grad, normed, inverse, gain[0:1, :])
         late[0:1, :] += jnp.sum(grad * normed, axis=0, keepdims=True)
         late[1:2, :] += jnp.sum(grad, axis=0, keepdims=True)
+        gtok_store(i).start()
         return carry
 
     def output(i, carry):
@@ -1633,6 +1642,7 @@
     halves[5].step_x()
     down_copy().wait_recv()
     lax.fori_loop(0, ROWS_WAVE, output, 0)
+    result_store.start()
 
     @pl.when(me < owners)
     def _():
@@ -1688,6 +1698,7 @@
     for index in range(1, count):
         total = total + late_recv[index]
     late_sum[...] = total
+    result_store.wait()
 
     down_copy().wait_send()
     for half in halves:
@@ -1715,6 +1726,7 @@
 
     def finish(i, carry):
         n_copy(i).wait_send()
+        gtok_store(i).wait()
         return carry
 
     lax.fori_loop(0, ROWS_WAVE, finish, 0)
@@ -1749,8 +1761,10 @@
             shape((2, width), F32),
         ),
         in_specs=[vmem()] * 7 + [anywhere] * 5 + [vmem()] + [anywhere] * 2 + [vmem()] * 4,
-        out_specs=[vmem()] * 8,
+        out_specs=[anywhere] * 2 + [vmem()] * 6,
         scratch_shapes=[
+            pltpu.VMEM((rows, width), BF),
+            pltpu.VMEM((rows, width), F32),
             *[pltpu.VMEM(inputs[k].shape, inputs[k].dtype) for k in (7, 8, 10, 11, 13, 14)],
             pltpu.VMEM((span, total), BF),
             pltpu.VMEM((span, total), BF),
@@ -1808,6 +1822,7 @@
             dma(nz - 1),
             pltpu.SemaphoreType.DMA,
             dma(6),
+            dma(ROWS_WAVE + 1),
         ],
         compiler_params=pltpu.CompilerParams(
             collective_id=2, has_side_effects=True, vmem_limit_bytes=60 << 20

time: 274 us -> 273 us (level)
  no operation moved by 1% of the time
where the time goes in v8:
time: 273 us; the launch traced here: 272 us
  Pallas kernels  271 us (99%)
    pallas_call x1, Pallas kernels, run_front(): pl.pallas_call(partial(front_kernel, dims), name='front', out_shape=(shap...  162 us
    pallas_call x1, Pallas kernels, run_back(): pl.pallas_call(partial(back_kernel, dims), name='tree_backward', out_shap...  104 us
    pallas_call x1, Pallas kernels, run_place(): pl.pallas_call(place_kernel, name='place', out_shape=(*[shape(a.shape, a....  5.6 us

profile of v8, /device:TPU:12, one launch (start us, length us, event | category | flops | bytes accessed | tf_op | source)
XLA Modules:
  0.0 272.3 jit_solution(5662054317789854018)
XLA Ops:
  0.6 161.6 %front.1 = (bf16[1024,2560]{1,0:T(8,128)(2,1)}, bf16[2560,128]{1,0:T(8,128)(2,1)}, bf16[2560,128]{1,0:T(8,128)(2,1)}, bf16[2560,128]{1,0:T(8,128)(2,1)}, bf16[25...) custom-call(bf16[640,1024]{1,0:T(8,128)(2,1)} %tok_in.1, ...), custom_call_target="tpu_custom_call" | custom-call | flops 40000000000 | bytes 20000000 | tf_op jit(solution)/shard_map/front/pallas_call | solution.py:996
  162.3 104.3 %tree_backward.1 = (bf16[640,1024]{1,0:T(8,128)(2,1)}, f32[640,1024]{1,0:T(8,128)}, f32[64,2048]{1,0:T(8,128)}, f32[64,2048]{1,0:T(8,128)}, f32[64,512]{1,0:T(8,...) custom-call(bf16[2560,128]{1,0:T(8,128)(2,1)} %get-tuple-element.46.query, ...), custom_call_target="tpu_custom_call" | custom-call | flops 40000000000 | bytes 20000000 | tf_op jit(solution)/shard_map/tree_backward/pallas_call | solution.py:1750
  266.6 5.6 %place.1 = (bf16[640,1024]{1,0:T(8,128)(2,1)}, f32[640,1024]{1,0:T(8,128)}, f32[3,64,512]{2,1,0:T(8,128)}, f32[64,2048]{1,0:T(8,128)}, f32[64,2048]{1,0:T(8,128)...) custom-call(f32[8,1024]{1,0:T(8,128)} %get-tuple-element.60.early, ...), custom_call_target="tpu_custom_call" | custom-call | tf_op jit(solution)/shard_map/place/pallas_call | solution.py:1864

commit v9 on v8

--- a/solution.py
+++ b/solution.py
@@ -11,6 +11,7 @@
 HEADS = 16
 HD = 64
 KEY_BLOCK = 512
+TALL = 256
 TRUNK = 1024
 BRANCH = 128
 SLOTS = 12
@@ -848,7 +849,7 @@
         weights.z_done(d)
 
     def group_cols(index, block):
-        return pl.ds(pl.multiple_of(weights.flip(index) * span + block * 128, 128), 128)
+        return pl.ds(pl.multiple_of(weights.flip(index) * span + block * TALL, 128), TALL)
 
     def products(cols):
         turned_act, turned_cot = act[:, cols].T, cot[:, cols].T
@@ -864,15 +865,15 @@
                 act_on(index, block)
                 return carry
 
-            lax.fori_loop(0, span // 128, one, 0)
+            lax.fori_loop(0, span // TALL, one, 0)
 
     def far_one(index, block):
-        target = pl.ds(pl.multiple_of(block * 128, 128), 128)
+        target = pl.ds(pl.multiple_of(block * TALL, 128), TALL)
         for lo, value_block in products(group_cols((1, 3)[index], block)):
             far[index, target, lo : lo + width] = value_block.astype(BF)
 
     def near_one(index, block):
-        target = pl.ds(pl.multiple_of(block * 128, 128), 128)
+        target = pl.ds(pl.multiple_of(block * TALL, 128), TALL)
         for lo, value_block in products(group_cols((0, 2)[index], block)):
             here = slice(lo, lo + width)
             core_in[index, target, here] = (core_in[index, target, here].astype(F32) + value_block).astype(BF)
@@ -881,11 +882,11 @@
         return nn(gbranch[:, cols].T, att[:, own_heads])
 
     def far_two(index, block):
-        target = pl.ds(pl.multiple_of(block * 128, 128), 128)
+        target = pl.ds(pl.multiple_of(block * TALL, 128), TALL)
         far[index, target, 2 * units :] = out_product(group_cols((1, 3)[index], block)).astype(BF)
 
     def near_two(index, block):
-        target = pl.ds(pl.multiple_of(block * 128, 128), 128)
+        target = pl.ds(pl.multiple_of(block * TALL, 128), TALL)
         here = slice(2 * units, 2 * units + inner)
         core_in[index, target, here] = (
             core_in[index, target, here].astype(F32) + out_product(group_cols((0, 2)[index], block))

time: 273 us -> 272 us (level)
  no operation moved by 1% of the time
where the time goes in v9:
time: 272 us
  Pallas kernels  271 us (100%)
    pallas_call x1, Pallas kernels, run_front(): pl.pallas_call(partial(front_kernel, dims), name='front', out_shape=(shap...  161 us
    pallas_call x1, Pallas kernels, run_back(): pl.pallas_call(partial(back_kernel, dims), name='tree_backward', out_shap...  104 us
    pallas_call x1, Pallas kernels, run_place(): pl.pallas_call(place_kernel, name='place', out_shape=(*[shape(a.shape, a....  5.6 us

profile of v9, /device:TPU:12, one launch (start us, length us, event | category | flops | bytes accessed | tf_op | source)
XLA Modules:
  0.0 271.9 jit_solution(16145530408851201478)
XLA Ops:
  0.6 161.3 %front.1 = (bf16[1024,2560]{1,0:T(8,128)(2,1)}, bf16[2560,128]{1,0:T(8,128)(2,1)}, bf16[2560,128]{1,0:T(8,128)(2,1)}, bf16[2560,128]{1,0:T(8,128)(2,1)}, bf16[25...) custom-call(bf16[640,1024]{1,0:T(8,128)(2,1)} %tok_in.1, ...), custom_call_target="tpu_custom_call" | custom-call | flops 40000000000 | bytes 20000000 | tf_op jit(solution)/shard_map/front/pallas_call | solution.py:997
  162.0 104.1 %tree_backward.1 = (bf16[640,1024]{1,0:T(8,128)(2,1)}, f32[640,1024]{1,0:T(8,128)}, f32[64,2048]{1,0:T(8,128)}, f32[64,2048]{1,0:T(8,128)}, f32[64,512]{1,0:T(8,...) custom-call(bf16[2560,128]{1,0:T(8,128)(2,1)} %get-tuple-element.46.query, ...), custom_call_target="tpu_custom_call" | custom-call | flops 40000000000 | bytes 20000000 | tf_op jit(solution)/shard_map/tree_backward/pallas_call | solution.py:1751
  266.1 5.6 %place.1 = (bf16[640,1024]{1,0:T(8,128)(2,1)}, f32[640,1024]{1,0:T(8,128)}, f32[3,64,512]{2,1,0:T(8,128)}, f32[64,2048]{1,0:T(8,128)}, f32[64,2048]{1,0:T(8,128)...) custom-call(f32[8,1024]{1,0:T(8,128)} %get-tuple-element.60.early, ...), custom_call_target="tpu_custom_call" | custom-call | tf_op jit(solution)/shard_map/place/pallas_call | solution.py:1865
